TPU v7x, 32 devices: a whole 2x2x4 slice. The times are simulated.
32 devices in a mesh: wide: 16 (over z, y, core), narrow: 2 (over x).
Axes of the slice: x: 2, y: 2, z: 4, core: 2. Of those that a mesh axis runs over, the one named last changes fastest.
Arguments:
- inputs: bfloat16 [32, 1024, 512], P('narrow', 'wide'), may hold values from -6 to 6
- segment_ids: int32 [1024], replicated, may hold values from 0 to 31, never falling along the last dimension, each value on 1 to 64 neighbouring positions
- norm1_gain: float32 [512], replicated, may hold values from 0.5 to 1.5
- norm1_shift: float32 [512], replicated, may hold values from -1.2 to 1.2
- w_qkv: bfloat16 [512, 3, 512], P(None, None, 'narrow'), may hold values from -0.375 to 0.375
- w_out: bfloat16 [512, 512], P('narrow'), may hold values from -1.5 to 1.5
- norm2_gain: float32 [512], replicated, may hold values from 0.5 to 1.5
- norm2_shift: float32 [512], replicated, may hold values from -1.2 to 1.2
- w_up: bfloat16 [512, 2048], P(None, 'narrow'), may hold values from -0.25 to 0.25
- w_down: bfloat16 [2048, 512], P('narrow'), may hold values from -0.125 to 0.125
- cotangent: bfloat16 [32, 1024, 512], P('narrow', 'wide'), may hold values from -6 to 6
Outputs:
- block_out: bfloat16 [32, 1024, 512], P('narrow', 'wide')
- input_grad: float32 [32, 1024, 512], P('narrow', 'wide')
- norm1_gain_grad: float32 [512], replicated
- norm1_shift_grad: float32 [512], replicated
- w_qkv_grad: float32 [512, 3, 512], P(None, None, 'narrow')
- w_out_grad: float32 [512, 512], P('narrow')
- norm2_gain_grad: float32 [512], replicated
- norm2_shift_grad: float32 [512], replicated
- w_up_grad: float32 [512, 2048], P(None, 'narrow')
- w_down_grad: float32 [2048, 512], P('narrow')
Inputs may be any that keep to these rules, and one draw needn't show every extreme that they name: `segment_ids`: segment ids never fall along the samples; each task spans 1 to 64 samples, and some task spans exactly 64.
All inputs are finite; a program needn't handle non-finite values.
Results may differ from a plain program's by a relative error of at most 0.017.
The roundings to bfloat16 on the way count: a program that leaves them out, or rounds other values in their place, can miss the bound.
Values may be sent and summed in bfloat16 or wider, within the bound.
No kernel may reach another device: no remote copies, remote signals or barrier semaphores. Data moves between devices by JAX's collectives and lax.ppermute only.
A program may use at most 128 MiB of HBM per device.

v0:
```python
import jax
import jax.numpy as jnp
from jax import lax
from jax.sharding import PartitionSpec as P

HEAD_DIM = 64


epsilon = 1e-05


def extended(cells, sides, width):
    for axis, dim in sides:
        count = lax.axis_size(axis)
        ends = count - 1
        head = lax.slice_in_dim(cells, 0, width, axis=dim)
        tail = lax.slice_in_dim(cells, cells.shape[dim] - width, cells.shape[dim], axis=dim)
        cells = jnp.concatenate(
            [
                lax.ppermute(tail, axis, [(i, (i + 1) % count) for i in range(ends)]),
                cells,
                lax.ppermute(head, axis, [((i + 1) % count, i) for i in range(ends)]),
            ],
            axis=dim,
        )
    return cells


def layer_norm(features, norm_gain, norm_shift):
    row_mean = jnp.mean(features, axis=-1, keepdims=True)
    centred = features - row_mean
    row_var = jnp.mean(centred * centred, axis=-1, keepdims=True)
    return centred * lax.rsqrt(row_var + epsilon) * norm_gain + norm_shift


def exact_gelu(pre_act):
    return jax.nn.gelu(pre_act, approximate=False)


def split_heads(query_group, pair_group, heads_here):
    group_size, rows_here, head_cols = query_group.shape
    head_size = head_cols // heads_here
    query_split = query_group.reshape(group_size, rows_here, heads_here, head_size)
    key_split = pair_group[:, :, :head_cols].reshape(group_size, -1, heads_here, head_size)
    value_split = pair_group[:, :, head_cols:].reshape(group_size, -1, heads_here, head_size)
    return (query_split, key_split, value_split)


def masked_scores(query_split, key_split, allowed, score_scale):
    scores = (
        jnp.einsum("fqhd,fkhd->fhqk", query_split, key_split, preferred_element_type=jnp.float32)
        * score_scale
    )
    return jnp.where(allowed, scores, -1e30)


def attend_group(query_group, pair_group, allowed, score_scale, heads_here):
    group_size, rows_here, head_cols = query_group.shape
    query_split, key_split, value_split = split_heads(query_group, pair_group, heads_here)
    scores = masked_scores(query_split, key_split, allowed, score_scale)
    row_top = jnp.max(scores, axis=-1, keepdims=True)
    expo_terms = jnp.exp(scores - row_top)
    row_total = jnp.sum(expo_terms, axis=-1, keepdims=True)
    attn_probs = (expo_terms / row_total).astype(jnp.bfloat16)
    attended = jnp.einsum(
        "fhqk,fkhd->fqhd", attn_probs, value_split, preferred_element_type=jnp.float32
    )
    log_total = row_top[..., 0] + jnp.log(row_total[..., 0])
    return (attended.reshape(group_size, rows_here, head_cols).astype(jnp.bfloat16), log_total)


def attend_group_back(
    query_group, pair_group, grad_group, log_total, allowed, score_scale, heads_here
):
    group_size, rows_here, head_cols = query_group.shape
    query_split, key_split, value_split = split_heads(query_group, pair_group, heads_here)
    out_split = grad_group.reshape(query_split.shape)
    scores = masked_scores(query_split, key_split, allowed, score_scale)
    attn_probs = jnp.exp(scores - log_total[..., None])
    prob_grad = jnp.einsum(
        "fqhd,fkhd->fhqk", out_split, value_split, preferred_element_type=jnp.float32
    )
    score_grad = (
        attn_probs * (prob_grad - jnp.sum(attn_probs * prob_grad, axis=-1, keepdims=True))
    ).astype(jnp.bfloat16)
    query_grad = (
        jnp.einsum("fhqk,fkhd->fqhd", score_grad, key_split, preferred_element_type=jnp.float32)
        * score_scale
    )
    key_grad = (
        jnp.einsum("fhqk,fqhd->fkhd", score_grad, query_split, preferred_element_type=jnp.float32)
        * score_scale
    )
    value_grad = jnp.einsum(
        "fhqk,fqhd->fkhd",
        attn_probs.astype(jnp.bfloat16),
        out_split,
        preferred_element_type=jnp.float32,
    )
    key_rows = key_grad.reshape(group_size, -1, head_cols)
    value_rows = value_grad.reshape(group_size, -1, head_cols)
    return (
        query_grad.reshape(group_size, rows_here, head_cols),
        jnp.concatenate([key_rows, value_rows], axis=-1),
    )


def local(
    inputs,
    segment_ids,
    norm1_gain,
    norm1_shift,
    w_qkv,
    w_out,
    norm2_gain,
    norm2_shift,
    w_up,
    w_down,
    cotangent,
):
    feat_local, samp_local, model_width = inputs.shape
    full_qkv, full_out, full_up, full_down = (w_qkv, w_out, w_up, w_down)
    head_cols = full_qkv.shape[2]
    heads_here = head_cols // HEAD_DIM
    score_scale = HEAD_DIM ** (-0.5)
    qkv_flat = full_qkv.reshape(model_width, 3 * head_cols)
    id_rim = jnp.full((samp_local,), -1, jnp.int32)
    padded_ids = jnp.concatenate([id_rim, segment_ids, id_rim])
    window_ids = lax.dynamic_slice_in_dim(
        padded_ids, lax.axis_index("wide") * samp_local, 3 * samp_local, 0
    )
    allowed = (window_ids[samp_local : 2 * samp_local, None] == window_ids[None, :])[None, None]
    features = inputs.astype(jnp.float32)
    normed_one, norm1_back = jax.vjp(layer_norm, features, norm1_gain, norm1_shift)
    normed_one = normed_one.astype(jnp.bfloat16)
    gathered_one = lax.all_gather(normed_one, "narrow", axis=0, tiled=True)
    work_feats = gathered_one.shape[0]
    group_feats = min(work_feats, max(1, 512 // samp_local))
    group_count = work_feats // group_feats
    projected = jnp.einsum(
        "fsd,dc->fsc", gathered_one, qkv_flat, preferred_element_type=jnp.float32
    ).astype(jnp.bfloat16)
    query_rows = projected[:, :, :head_cols]
    key_value = projected[:, :, head_cols:]
    key_value_wide = extended(key_value, (("wide", 1),), samp_local)
    query_grouped = query_rows.reshape(group_count, group_feats, samp_local, head_cols)
    pair_grouped = key_value_wide.reshape(group_count, group_feats, 3 * samp_local, 2 * head_cols)

    def forward_group(group_pair):
        return attend_group(group_pair[0], group_pair[1], allowed, score_scale, heads_here)

    attended, log_total = lax.map(forward_group, (query_grouped, pair_grouped))
    attended = attended.reshape(work_feats, samp_local, head_cols)
    attn_branch = lax.psum_scatter(
        jnp.einsum("fsc,cd->fsd", attended, full_out, preferred_element_type=jnp.float32),
        "narrow",
        scatter_dimension=0,
        tiled=True,
    )
    hidden_state = features + attn_branch
    normed_two, norm2_back = jax.vjp(layer_norm, hidden_state, norm2_gain, norm2_shift)
    normed_two = normed_two.astype(jnp.bfloat16)
    gathered_two = lax.all_gather(normed_two, "narrow", axis=0, tiled=True)
    pre_act = jnp.einsum("fsd,dc->fsc", gathered_two, full_up, preferred_element_type=jnp.float32)
    activated, gelu_back = jax.vjp(exact_gelu, pre_act)
    activated = activated.astype(jnp.bfloat16)
    mlp_branch = lax.psum_scatter(
        jnp.einsum("fsc,cd->fsd", activated, full_down, preferred_element_type=jnp.float32).astype(
            jnp.bfloat16
        ),
        "narrow",
        scatter_dimension=0,
        tiled=True,
    ).astype(jnp.float32)
    block_out = (hidden_state + mlp_branch).astype(jnp.bfloat16)
    cot_full = lax.all_gather(cotangent, "narrow", axis=0, tiled=True)
    down_grad = jnp.einsum("fsc,fsd->cd", activated, cot_full, preferred_element_type=jnp.float32)
    act_grad = jnp.einsum("fsd,cd->fsc", cot_full, full_down, preferred_element_type=jnp.float32)
    pre_grad = gelu_back(act_grad)[0].astype(jnp.bfloat16)
    up_grad = jnp.einsum("fsd,fsc->dc", gathered_two, pre_grad, preferred_element_type=jnp.float32)
    grad_rows = pre_grad
    normed_two_grad = lax.psum_scatter(
        jnp.einsum("fsc,dc->fsd", grad_rows, full_up, preferred_element_type=jnp.float32),
        "narrow",
        scatter_dimension=0,
        tiled=True,
    )
    hidden_grad, gain2_grad, shift2_grad = norm2_back(normed_two_grad)
    hidden_grad = hidden_grad + cotangent.astype(jnp.float32)
    residual_low = hidden_grad.astype(jnp.bfloat16)
    residual_full = lax.all_gather(residual_low, "narrow", axis=0, tiled=True)
    out_grad = jnp.einsum(
        "fsc,fsd->cd", attended, residual_full, preferred_element_type=jnp.float32
    )
    attended_grad = jnp.einsum(
        "fsd,cd->fsc", residual_full, full_out, preferred_element_type=jnp.float32
    ).astype(jnp.bfloat16)
    grad_grouped = attended_grad.reshape(group_count, group_feats, samp_local, head_cols)

    def backward_group(group_items):
        return attend_group_back(
            group_items[0],
            group_items[1],
            group_items[2],
            group_items[3],
            allowed,
            score_scale,
            heads_here,
        )

    query_grad, pair_grad = lax.map(
        backward_group, (query_grouped, pair_grouped, grad_grouped, log_total)
    )
    pair_grad = pair_grad.reshape(work_feats, 3 * samp_local, 2 * head_cols)
    returned = extended(pair_grad.astype(jnp.bfloat16), (("wide", 1),), samp_local).astype(
        pair_grad.dtype
    )
    pair_sum = (
        returned[:, :samp_local]
        + returned[:, 2 * samp_local : 3 * samp_local]
        + returned[:, 4 * samp_local :]
    )
    projected_grad = jnp.concatenate(
        [query_grad.reshape(work_feats, samp_local, head_cols), pair_sum], axis=-1
    ).astype(jnp.bfloat16)
    qkv_grad = jnp.einsum(
        "fsd,fsc->dc", gathered_one, projected_grad, preferred_element_type=jnp.float32
    ).reshape(model_width, 3, head_cols)
    grad_rows = projected_grad
    normed_one_grad = lax.psum_scatter(
        jnp.einsum("fsc,dc->fsd", grad_rows, qkv_flat, preferred_element_type=jnp.float32).astype(
            jnp.bfloat16
        ),
        "narrow",
        scatter_dimension=0,
        tiled=True,
    ).astype(jnp.float32)
    input_part, gain1_grad, shift1_grad = norm1_back(normed_one_grad)
    input_grad = input_part + hidden_grad
    norm_sums = lax.psum((gain1_grad, shift1_grad, gain2_grad, shift2_grad), ("wide", "narrow"))
    grad_parts = (qkv_grad, out_grad, up_grad, down_grad)
    weight_sums = (
        lax.psum(grad_parts[0].astype(jnp.bfloat16), "wide").astype(jnp.float32),
        lax.psum(grad_parts[1].astype(jnp.bfloat16), "wide").astype(jnp.float32),
        lax.psum(grad_parts[2].astype(jnp.bfloat16), "wide").astype(jnp.float32),
        lax.psum(grad_parts[3].astype(jnp.bfloat16), "wide").astype(jnp.float32),
    )
    return (
        block_out,
        input_grad,
        norm_sums[0],
        norm_sums[1],
        weight_sums[0],
        weight_sums[1],
        norm_sums[2],
        norm_sums[3],
        weight_sums[2],
        weight_sums[3],
    )


def solution(mesh):
    placed = (
        P("narrow", "wide", None),
        P(),
        P(),
        P(),
        P(None, None, "narrow"),
        P("narrow", None),
        P(),
        P(),
        P(None, "narrow"),
        P("narrow", None),
        P("narrow", "wide", None),
    )
    return jax.shard_map(
        local,
        mesh=mesh,
        in_specs=placed,
        out_specs=(
            P("narrow", "wide", None),
            P("narrow", "wide", None),
            P(),
            P(),
            P(None, None, "narrow"),
            P("narrow", None),
            P(),
            P(),
            P(None, "narrow"),
            P("narrow", None),
        ),
        check_vma=False,
    )
```

profile of v0, /device:TPU:0, one launch (start us, length us, event | category | flops | bytes accessed | tf_op | source)
XLA Modules:
  0.0 755.5 jit_solution(4085179811300507098)
XLA Ops:
  13.7 35.6 %all-gather.5.cloned.1.call-done = bf16[32,64,512]{2,1,0:T(8,128)(2,1)} async-done(((bf16[16,64,512]{2,1,0:T(8,128)(2,1)}), bf16[32,64,512]{2,1,0:T(8,128)(2,1)}) %all-gather.5.cloned.1.call-update) | async-done | bytes 2097168 | tf_op jit(solution)/shard_map/all_gather | solution.py:136
  55.7 4.4 collective-permute-start
  62.6 5.4 pad_maximum_fusion
  68.0 10.9 %copy.53 = bf16[4,8,192,512]{2,3,1,0:T(8,128)(2,1)} copy(bf16[4,8,192,512]{3,2,1,0:T(8,128)(2,1)} %bitcast.171) | data formatting | bytes 12582912
  78.9 30.9 %while.26 = (s32[]{:T(128)}, bf16[4,8,64,256]{2,3,1,0:T(8,128)(2,1)}, f32[4,8,4,64]{3,2,1,0:T(4,128)S(1)}, bf16[4,8,192,512]{2,3,1,0:T(8,128)(2,1)}, bf16[4,8,64...) while((s32[]{:T(128)}, bf16[4,8,64,256]{2,3,1,0:T(8,128)(2,1)}, ...), condition=%wide.region_5.6_spmd.clone, body=%wide.region_2.5_spmd.clone.sunk | while | flops 105523200 | bytes 18228360 | solution.py:152
  109.8 4.3 fusion.46
  114.2 96.0 %reduce-scatter.5.cloned.1.call-done = f32[16,64,512]{2,1,0:T(8,128)} async-done(((f32[32,64,512]{2,1,0:T(8,128)}), f32[16,64,512]{2,1,0:T(8,128)}) %reduce-scatter.5.cloned.1.call-update) | async-done | bytes 2097168 | tf_op jit(solution)/shard_map/reduce_scatter | solution.py:154
  215.2 32.4 %all-gather.7.cloned.1.call-done = bf16[32,64,512]{2,1,0:T(8,128)(2,1)} async-done(((bf16[16,64,512]{2,1,0:T(8,128)(2,1)}), bf16[32,64,512]{2,1,0:T(8,128)(2,1)}) %all-gather.7.cloned.1.call-update) | async-done | bytes 2097168 | tf_op jit(solution)/shard_map/all_gather | solution.py:163
  247.6 5.3 convert_reduce_fusion.1
  256.4 19.7 %multiply_convert_fusion.1 = (bf16[32,64,1024]{2,1,0:T(8,128)(2,1)}, f32[32,64,1024]{2,1,0:T(8,128)}) fusion(f32[32,64,1024]{2,1,0:T(8,128)S(1)} %get-tuple-element.266, u32[64,1024]{1,0:T(8,128)S(1)} %get-tuple-element.199, u32[64,1024]{1,0:T(8,128)S(1)} %get-tuple-element.198), kind=kLoop, calls=%fused_computation.41 | loop fusion | flops 142606336 | bytes 21495808 | tf_op jit(solution)/shard_map/convert_element_type | solution.py:166
  276.1 6.1 all-gather.9.cloned.1.call-done
  282.1 9.0 %add_convert_fusion = bf16[32,64,1024]{2,1,0:T(8,128)(2,1)S(1)} fusion(f32[32,64,1024]{2,1,0:T(8,128)} %get-tuple-element.250, f32[32,64,1024]{2,1,0:T(8,128)} %copy-done.10, bf16[32,64,512]{2,1,0:T(8,128)(2,1)} %all-gather.9.cloned.1.call-done, bf16[1024,512]{1,0:T(8,128)(2,1)} %param.24), kind=kOutput, calls=%fused_computation.40 | convolution fusion | flops 2176843776 | bytes 24117248 | tf_op jit(solution)/shard_map/fsd,cd->fsc/dot_general | solution.py:178
  293.1 4.4 fusion.41
  298.7 5.9 convolution_convert_fusion.2
  304.9 47.2 %reduce-scatter.9.cloned.1.call-done = f32[16,64,512]{2,1,0:T(8,128)} async-done(((f32[32,64,512]{2,1,0:T(8,128)}), f32[16,64,512]{2,1,0:T(8,128)}) %reduce-scatter.9.cloned.1.call-update) | async-done | bytes 2097168 | tf_op jit(solution)/shard_map/reduce_scatter | solution.py:182
  354.4 32.2 %reduce-scatter.7.cloned.1.call-done = bf16[16,64,512]{2,1,0:T(8,128)(2,1)} async-done(((bf16[32,64,512]{2,1,0:T(8,128)(2,1)}), bf16[16,64,512]{2,1,0:T(8,128)(2,1)}) %reduce-scatter.7.cloned.1.call-update) | async-done | bytes 1048592 | tf_op jit(solution)/shard_map/reduce_scatter | solution.py:167
  392.6 33.2 %all-gather.11.cloned.1.call-done = bf16[32,64,512]{2,1,0:T(8,128)(2,1)} async-done(((bf16[16,64,512]{2,1,0:T(8,128)(2,1)}), bf16[32,64,512]{2,1,0:T(8,128)(2,1)}) %all-gather.11.cloned.1.call-update) | async-done | bytes 2097168 | tf_op jit(solution)/shard_map/all_gather | solution.py:191
  428.1 61.1 %while.27 = (s32[]{:T(128)}, bf16[4,8,64,256]{2,3,1,0:T(8,128)(2,1)}, bf16[4,8,192,512]{2,3,1,0:T(8,128)(2,1)}, bf16[4,8,192,512]{2,3,1,0:T(8,128)(2,1)}, bf16[4...) while((s32[]{:T(128)}, ...), condition=%wide.region_15.16_spmd.clone, body=%wide.region_13.15_spmd.clone.sunk | while | flops 259401728 | bytes 40436976 | solution.py:211
  489.2 11.0 %copy.57 = bf16[4,8,192,512]{3,2,1,0:T(8,128)(2,1)} copy(bf16[4,8,192,512]{2,3,1,0:T(8,128)(2,1)} %get-tuple-element.89) | data formatting | bytes 12582912 | tf_op jit(solution)/shard_map/convert_element_type | solution.py:215
  500.2 4.9 fusion.57
  506.4 4.9 collective-permute-start.2
  536.3 131.8 %all-reduce.4.cloned.1.call-done = (bf16[512,3,256]{0,2,1:T(8,128)(2,1)}, bf16[256,512]{1,0:T(8,128)(2,1)}, bf16[512,1024]{1,0:T(8,128)(2,1)}, bf16[1024,512]{1,0:T(8,128)(2,1)}) async-done(((bf16[512,3,256]{0,2,1:T(8,128)(2,1)}, bf16[256,512]{1,0:T(8,128)(2,1)}, bf16[512,1024]{1,0:T(8,128)(2,1)}, bf16[1024,512]{1,0:T(8,128)(2,1)}), (bf16[512,3,256]{0,2,1:T(8,128)(2,1)}, bf16[256,512]{1,0:T(8,128)(2,1)}, ...) | async-done | bytes 3145744 | tf_op jit(solution)/shard_map/psum | solution.py:243
  674.8 27.1 %reduce-scatter.11.cloned.1.call-done = bf16[16,64,512]{2,1,0:T(8,128)(2,1)} async-done(((bf16[32,64,512]{2,1,0:T(8,128)(2,1)}), bf16[16,64,512]{2,1,0:T(8,128)(2,1)}) %reduce-scatter.11.cloned.1.call-update) | async-done | bytes 1048592 | tf_op jit(solution)/shard_map/reduce_scatter | solution.py:230
  705.7 39.4 %all-reduce = (f32[512]{0:T(512)}, f32[512]{0:T(512)}, f32[512]{0:T(512)}, f32[512]{0:T(512)}) all-reduce(f32[512]{0:T(512)S(1)} %get-tuple-element.202, f32[512]{0:T(512)S(1)} %get-tuple-element.205, f32[512]{0:T(512)S(1)} %get-tuple-element.200, f32[512]{0:T(512)S(1)} %get-tuple-element.204), channel_id=1, replica_groups=mesh['wide'=16,'narrow'=2] {'wide','narrow'}, use_global_device_ids=true, to_apply=%region_20.21 | all-reduce | flops 2048 | bytes 16384 | tf_op jit(solution)/shard_map/psum | solution.py:240
  (279 shorter events, 169.1 us)
Async XLA Ops:
  7.2 240.5 %copy-start = (bf16[512,1024]{1,0:T(8,128)(2,1)S(1)}, bf16[512,1024]{1,0:T(8,128)(2,1)}, u32[]{:S(2)}) copy-start(bf16[512,1024]{1,0:T(8,128)(2,1)} %param.23) | copy-start | bytes 3145732
  7.2 42.1 %all-gather.5.cloned.1.call-start = ((), (), s32[]{:S(2)}) async-start(), calls=%async_computation.4 | async-start | bytes 3145728 | tf_op jit(solution)/shard_map/all_gather | solution.py:136
  13.3 196.9 %reduce-scatter.5.cloned.1.call-start = ((), (), s32[]{:S(2)}) async-start(), calls=%async_computation.5 | async-start | bytes 6291456 | tf_op jit(solution)/shard_map/reduce_scatter | solution.py:154
  13.7 35.6 %copy-start.20 = (bf16[512,3,256]{0,2,1:T(8,128)(2,1)}, bf16[512,3,256]{0,2,1:T(8,128)(2,1)S(1)}, u32[]{:S(2)}) copy-start(bf16[512,3,256]{0,2,1:T(8,128)(2,1)S(1)} %copy.51) | copy-start | bytes 2359300
  54.4 8.2 %collective-permute-start.1 = (bf16[32,64,512]{2,1,0:T(8,128)(2,1)S(1)}, bf16[32,64,512]{2,1,0:T(8,128)(2,1)}, u32[]{:S(2)}, u32[]{:S(2)}) collective-permute-start(bf16[32,64,512]{2,1,0:T(8,128)(2,1)S(1)} %slice.52), channel_id=1, source_target_pairs={{2,0},{4,2},{6,4},{8,6},{10,8},{12,10},{14,12},{16,14},{18,16},{20... | collective-permute-start | bytes 6291464 | tf_op jit(solution)/shard_map/ppermute | solution.py:22
  55.7 6.9 collective-permute-start
  78.9 30.9 %copy-start.18 = (bf16[256,512]{1,0:T(8,128)(2,1)S(1)}, bf16[256,512]{1,0:T(8,128)(2,1)}, u32[]{:S(2)}) copy-start(bf16[256,512]{1,0:T(8,128)(2,1)} %param.20) | copy-start | bytes 786436
  114.1 133.5 %all-gather.7.cloned.1.call-start = ((), (), s32[]{:S(2)}) async-start(), calls=%async_computation.6 | async-start | bytes 3145728 | tf_op jit(solution)/shard_map/all_gather | solution.py:163
  214.4 67.7 %all-gather.9.cloned.1.call-start = ((), (), s32[]{:S(2)}) async-start(), calls=%async_computation.8 | async-start | bytes 3145728 | tf_op jit(solution)/shard_map/all_gather | solution.py:176
  215.0 137.1 %reduce-scatter.9.cloned.1.call-start = ((), (), s32[]{:S(2)}) async-start(), calls=%async_computation.9 | async-start | bytes 6291456 | tf_op jit(solution)/shard_map/reduce_scatter | solution.py:182
  297.5 89.1 %reduce-scatter.7.cloned.1.call-start = ((), (), s32[]{:S(2)}) async-start(), calls=%async_computation.7 | async-start | bytes 3145728 | tf_op jit(solution)/shard_map/reduce_scatter | solution.py:167
  304.6 121.2 %all-gather.11.cloned.1.call-start = ((), (), s32[]{:S(2)}) async-start(), calls=%async_computation.10 | async-start | bytes 3145728 | tf_op jit(solution)/shard_map/all_gather | solution.py:191
  354.4 36.7 %copy-start.9 = (bf16[16,64,512]{2,1,0:T(8,128)(2,1)S(1)}, bf16[16,64,512]{2,1,0:T(8,128)(2,1)}, u32[]{:S(2)}) copy-start(bf16[16,64,512]{2,1,0:T(8,128)(2,1)} %param.25) | copy-start | bytes 3145732
  392.5 275.6 %all-reduce.4.cloned.1.call-start = ((), (), s32[]{:S(2)}) async-start(), calls=%async_computation.12 | async-start | bytes 6291456 | tf_op jit(solution)/shard_map/psum | solution.py:243
  500.2 11.2 %copy-start.39 = (bf16[32,64,1024]{2,1,0:T(8,128)(2,1)S(1)}, bf16[32,64,1024]{2,1,0:T(8,128)(2,1)}, u32[]{:S(2)}) copy-start(bf16[32,64,1024]{2,1,0:T(8,128)(2,1)} %copy-done.38) | copy-start | bytes 12582916
  505.1 18.3 %collective-permute-start.3 = (bf16[32,64,512]{2,1,0:T(8,128)(2,1)}, bf16[32,64,512]{2,1,0:T(8,128)(2,1)}, u32[]{:S(2)}, u32[]{:S(2)}) collective-permute-start(bf16[32,64,512]{2,1,0:T(8,128)(2,1)} %get-tuple-element.264), channel_id=1, source_target_pairs={{2,0},{4,2},{6,4},{8,6},{10,8},{12,10},{14,12},{16,14},{18,16},{20... | collective-permute-start | bytes 6291464 | tf_op jit(solution)/shard_map/ppermute | solution.py:22
  506.4 17.0 %collective-permute-start.2 = (bf16[32,64,512]{2,1,0:T(8,128)(2,1)}, bf16[32,64,512]{2,1,0:T(8,128)(2,1)}, u32[]{:S(2)}, u32[]{:S(2)}) collective-permute-start(bf16[32,64,512]{2,1,0:T(8,128)(2,1)} %get-tuple-element.263), channel_id=1, source_target_pairs={{0,2},{2,4},{4,6},{6,8},{8,10},{10,12},{12,14},{14,16},{16,18},{18... | collective-permute-start | bytes 6291464 | tf_op jit(solution)/shard_map/ppermute | solution.py:20
  532.0 169.9 %reduce-scatter.11.cloned.1.call-start = ((), (), s32[]{:S(2)}) async-start(), calls=%async_computation.11 | async-start | bytes 3145728 | tf_op jit(solution)/shard_map/reduce_scatter | solution.py:230
  673.2 28.7 %copy-start.5 = (bf16[16,64,512]{2,1,0:T(8,128)(2,1)S(1)}, bf16[16,64,512]{2,1,0:T(8,128)(2,1)}, u32[]{:S(2)}) copy-start(bf16[16,64,512]{2,1,0:T(8,128)(2,1)} %param.15) | copy-start | bytes 3145732
  673.2 28.7 %copy-start.22 = (f32[16,64]{1,0:T(8,128)S(1)}, f32[16,64]{1,0:T(8,128)}, u32[]{:S(2)}) copy-start(f32[16,64]{1,0:T(8,128)} %copy-done.21) | copy-start | bytes 12292
  673.2 28.7 %copy-start.29 = (f32[512]{0:T(512)S(1)}, f32[512]{0:T(512)}, u32[]{:S(2)}) copy-start(f32[512]{0:T(512)} %param.17) | copy-start | bytes 6148
  673.2 31.1 %copy-start.27 = (f32[16,64]{1,0:T(8,128)S(1)}, f32[16,64]{1,0:T(8,128)}, u32[]{:S(2)}) copy-start(f32[16,64]{1,0:T(8,128)} %copy-done.26) | copy-start | bytes 12292
  673.2 31.1 %copy-start.25 = (f32[16,64]{1,0:T(8,128)S(1)}, f32[16,64]{1,0:T(8,128)}, u32[]{:S(2)}) copy-start(f32[16,64]{1,0:T(8,128)} %copy-done.24) | copy-start | bytes 12292
  705.7 42.8 %copy-start.1 = (bf16[512,1024]{1,0:T(8,128)(2,1)S(1)}, bf16[512,1024]{1,0:T(8,128)(2,1)}, u32[]{:S(2)}) copy-start(bf16[512,1024]{1,0:T(8,128)(2,1)} %param.23) | copy-start | bytes 3145732
  (44 other events, 120.0 us)
Sparse Core Ops, SparseCore 0:
  13.4 35.8 all-gather.4
  114.2 95.8 reduce-scatter.4
  214.5 33.0 all-gather.6
  249.0 33.0 all-gather.8
  297.6 54.3 reduce-scatter.8
  354.7 31.8 reduce-scatter.6
  392.6 33.0 all-gather.10
  532.1 135.9 all-reduce.3
  670.9 30.9 reduce-scatter.10
where the time goes:
time: 764 us; the launch traced here: 755 us
  waiting for transfers between devices  442 us (58%)
  local copies, waits for them, and re-layouts  98.2 us (13%)
  matrix products  79.6 us (10%)
  other arithmetic  68.1 us (9%)
  blocking collectives  39.4 us (5%)
  between operations  14.8 us (2%)
  starting transfers between devices  12.6 us (2%)
    psum x1, waiting for transfers between devices, local(): lax.psum(grad_parts[0].astype(jnp.bfloat16), 'wide').astype(jnp.float32)  132 us
    reduce_scatter x1, waiting for transfers between devices, local(): lax.psum_scatter(jnp.einsum('fsc,cd->fsd', attended, full_out, preferred_...  96 us
    reduce_scatter x1, waiting for transfers between devices, local(): lax.psum_scatter(jnp.einsum('fsc,dc->fsd', grad_rows, full_up, preferred_...  47.2 us
    psum x1, blocking collectives, local(): lax.psum((gain1_grad, shift1_grad, gain2_grad, shift2_grad), ('wide', 'na...  39.4 us
    all_gather x1, waiting for transfers between devices, local(): gathered_one = lax.all_gather(normed_one, 'narrow', axis=0, tiled=True)  35.6 us
    all_gather x1, waiting for transfers between devices, local(): residual_full = lax.all_gather(residual_low, 'narrow', axis=0, tiled=True)  33.2 us
    all_gather x1, waiting for transfers between devices, local(): gathered_two = lax.all_gather(normed_two, 'narrow', axis=0, tiled=True)  32.4 us
    reduce_scatter x1, waiting for transfers between devices, local(): lax.psum_scatter(jnp.einsum('fsc,cd->fsd', activated, full_down, preferre...  32.2 us
  transfers between devices with their start and end apart: 13, of which 9 were waited for; matrix products, arithmetic and copies ran while one was open for 8% of the time, Pallas kernels for 0%

commit v1 on v0

v1 whole, which is shorter than its diff:
```python
import jax
import jax.numpy as jnp
from jax import lax
from jax.experimental import pallas as pl
from jax.experimental.pallas import tpu as pltpu
from jax.sharding import PartitionSpec as P

HEAD_DIM = 64
HEADS_PER_GROUP = 4
GROUP_COLS = HEAD_DIM * HEADS_PER_GROUP
EPS = 1e-05
SCALE = HEAD_DIM ** (-0.5)
F32 = jnp.float32
BF16 = jnp.bfloat16
NEG = -1e30


def dot_nn(a, b):
    return lax.dot_general(a, b, (((1,), (0,)), ((), ())), preferred_element_type=F32)


def dot_nt(a, b):
    return lax.dot_general(a, b, (((1,), (1,)), ((), ())), preferred_element_type=F32)


def dot_tn(a, b):
    return lax.dot_general(a, b, (((0,), (0,)), ((), ())), preferred_element_type=F32)


def norm_parts(z):
    mean = jnp.mean(z, axis=-1, keepdims=True)
    centred = z - mean
    var = jnp.mean(centred * centred, axis=-1, keepdims=True)
    rstd = lax.rsqrt(var + EPS)
    return centred * rstd, rstd


def norm_back(grad, xhat, rstd, gain):
    gg = grad * gain
    m1 = jnp.mean(gg, axis=-1, keepdims=True)
    m2 = jnp.mean(gg * xhat, axis=-1, keepdims=True)
    return rstd * (gg - m1 - xhat * m2)


def lane_head(rows, dtype):
    lane = lax.broadcasted_iota(jnp.int32, (rows, GROUP_COLS), 1)
    return [
        ((lane >= h * HEAD_DIM) & (lane < (h + 1) * HEAD_DIM)).astype(F32).astype(dtype)
        for h in range(HEADS_PER_GROUP)
    ]


def block_diag(rows, masks):
    return jnp.concatenate([rows * m for m in masks], axis=0)


def pick_heads(full, masks, rows):
    out = full[0:rows] * masks[0]
    for h in range(1, HEADS_PER_GROUP):
        out = out + full[h * rows : (h + 1) * rows] * masks[h]
    return out


def attn_fwd_kernel(idc, idr, xp, xo, xn, w0, w1, gain, shift, qkv_ref, att_ref):
    feats, samp, width = xo.shape
    rows = feats * samp
    x = jnp.concatenate(
        [xp[...].reshape(rows, width), xo[...].reshape(rows, width), xn[...].reshape(rows, width)],
        axis=0,
    ).astype(F32)
    xhat, _ = norm_parts(x)
    normed = (xhat * gain[...] + shift[...]).astype(BF16)
    for hg, w in enumerate((w0, w1)):
        qkv = dot_nn(normed, w[...]).astype(BF16)
        qkv_ref[hg] = qkv.reshape(3, rows, 3 * GROUP_COLS)
    allowed = idc[...] == idr[1:2, :]
    m16 = lane_head(1, BF16)
    m32 = lane_head(1, F32)
    for f in range(feats):
        sl = slice(f * samp, (f + 1) * samp)
        for hg in range(2):
            q = qkv_ref[hg, 1, sl, 0:GROUP_COLS]
            k = jnp.concatenate(
                [qkv_ref[hg, w, sl, GROUP_COLS : 2 * GROUP_COLS] for w in range(3)], axis=0
            )
            v = jnp.concatenate(
                [qkv_ref[hg, w, sl, 2 * GROUP_COLS : 3 * GROUP_COLS] for w in range(3)], axis=0
            )
            s = dot_nt(k, block_diag(q, m16)) * SCALE
            s = jnp.where(allowed, s, NEG)
            top = jnp.max(s, axis=0, keepdims=True)
            e = jnp.exp(s - top)
            total = jnp.sum(e, axis=0, keepdims=True)
            p = (e * (1.0 / total)).astype(BF16)
            o = pick_heads(dot_tn(p, v), m32, samp)
            att_ref[f, :, hg * GROUP_COLS : (hg + 1) * GROUP_COLS] = o.astype(BF16)


def phi_parts(u):
    e = jnp.exp(-0.5 * (u * u))
    t = 1.0 / (1.0 + (0.3275911 * 0.7071067811865476) * jnp.abs(u))
    poly = t * (
        0.127414796
        + t * (-0.142248368 + t * (0.7107068705 + t * (-0.7265760135 + t * 0.5307027145)))
    )
    tail = poly * e
    cdf = jnp.where(u < 0, tail, 1.0 - tail)
    return cdf, u * (e * 0.3989422804014327)


def chain_kernel(
    x, att, cot, wo0, wo1, wu0, wu1, wd0, wd1, gain, shift,
    out_ref, n2_ref, act_ref, pre_ref, hgrad_ref, res_ref, dat_ref, g2_ref, s2_ref,
):
    half = wo0.shape[0]
    hidden = (
        x[...].astype(F32) + dot_nn(att[:, :half], wo0[...]) + dot_nn(att[:, half:], wo1[...])
    )
    xhat, rstd = norm_parts(hidden)
    normed = (xhat * gain[...] + shift[...]).astype(BF16)
    n2_ref[...] = normed
    c = cot[...]
    ff = wu0.shape[1]
    step = min(512, ff)
    mlp = jnp.zeros_like(hidden)
    dn2 = jnp.zeros_like(hidden)
    for part, (wu, wd) in enumerate(((wu0, wd0), (wu1, wd1))):
        for j in range(0, ff, step):
            up = wu[:, j : j + step]
            down = wd[j : j + step, :]
            u = dot_nn(normed, up)
            cdf, upd = phi_parts(u)
            act = (u * cdf).astype(BF16)
            act_ref[part, :, j : j + step] = act
            mlp = mlp + dot_nn(act, down)
            pre = (dot_nt(c, down) * (cdf + upd)).astype(BF16)
            pre_ref[part, :, j : j + step] = pre
            dn2 = dn2 + dot_nt(pre, up)
    out_ref[...] = (hidden + mlp).astype(BF16)

    @pl.when(pl.program_id(0) == 0)
    def _():
        g2_ref[...] = jnp.zeros_like(g2_ref)
        s2_ref[...] = jnp.zeros_like(s2_ref)

    g2_ref[...] += jnp.sum(dn2 * xhat, axis=0, keepdims=True)
    s2_ref[...] += jnp.sum(dn2, axis=0, keepdims=True)
    hgrad = c.astype(F32) + norm_back(dn2, xhat, rstd, gain[...])
    hgrad_ref[...] = hgrad
    res = hgrad.astype(BF16)
    res_ref[...] = res
    dat_ref[:, :half] = dot_nt(res, wo0[...]).astype(BF16)
    dat_ref[:, half:] = dot_nt(res, wo1[...]).astype(BF16)


def attn_bwd_kernel(
    idc, idr, x, qkv_ref, dp_ref, do_ref, dn_ref, hgrad, w0, w1, gain, shift,
    igrad_ref, dw_ref, g1_ref, s1_ref, acc, dqkv,
):
    feats, samp, width = x.shape
    rows = feats * samp
    m16 = lane_head(1, BF16)
    m32 = lane_head(1, F32)
    spans = ((0, 2), (0, 3), (1, 3))
    masks = [idc[a * samp : b * samp, :] == idr[g : g + 1, :] for g, (a, b) in enumerate(spans)]
    grads = (dp_ref, do_ref, dn_ref)
    for f in range(feats):
        sl = slice(f * samp, (f + 1) * samp)
        for hg in range(2):
            cols = slice(hg * GROUP_COLS, (hg + 1) * GROUP_COLS)
            k = jnp.concatenate(
                [qkv_ref[hg, w, sl, GROUP_COLS : 2 * GROUP_COLS] for w in range(3)], axis=0
            )
            v = jnp.concatenate(
                [qkv_ref[hg, w, sl, 2 * GROUP_COLS : 3 * GROUP_COLS] for w in range(3)], axis=0
            )
            dk = jnp.zeros((samp, GROUP_COLS), F32)
            dv = jnp.zeros((samp, GROUP_COLS), F32)
            for g, (a, b) in enumerate(spans):
                ks = k[a * samp : b * samp]
                vs = v[a * samp : b * samp]
                qbd = block_diag(qkv_ref[hg, g, sl, 0:GROUP_COLS], m16)
                dbd = block_diag(grads[g][f, :, cols], m16)
                s = dot_nt(ks, qbd) * SCALE
                s = jnp.where(masks[g], s, NEG)
                top = jnp.max(s, axis=0, keepdims=True)
                e = jnp.exp(s - top)
                total = jnp.sum(e, axis=0, keepdims=True)
                p = e * (1.0 / total)
                dp = dot_nt(vs, dbd)
                pd = p * dp
                delta = jnp.sum(pd, axis=0, keepdims=True)
                ds = (pd - p * delta).astype(BF16)
                own = slice((1 - a) * samp, (2 - a) * samp)
                dk = dk + dot_nn(ds[own], qbd)
                dv = dv + dot_nn(p[own].astype(BF16), dbd)
                if g == 1:
                    dq = pick_heads(dot_tn(ds, ks), m32, samp)
            dqkv[hg, sl, 0:GROUP_COLS] = (dq * SCALE).astype(BF16)
            dqkv[hg, sl, GROUP_COLS : 2 * GROUP_COLS] = (dk * SCALE).astype(BF16)
            dqkv[hg, sl, 2 * GROUP_COLS : 3 * GROUP_COLS] = dv.astype(BF16)
    xhat, rstd = norm_parts(x[...].reshape(rows, width).astype(F32))
    normed = (xhat * gain[...] + shift[...]).astype(BF16)
    dn1 = dot_nt(dqkv[0], w0[...]) + dot_nt(dqkv[1], w1[...])

    @pl.when(pl.program_id(0) == 0)
    def _():
        g1_ref[...] = jnp.zeros_like(g1_ref)
        s1_ref[...] = jnp.zeros_like(s1_ref)
        acc[...] = jnp.zeros_like(acc)

    g1_ref[...] += jnp.sum(dn1 * xhat, axis=0, keepdims=True)
    s1_ref[...] += jnp.sum(dn1, axis=0, keepdims=True)
    for hg in range(2):
        acc[hg] += dot_tn(normed, dqkv[hg])
    igrad_ref[...] = hgrad[...] + norm_back(dn1, xhat, rstd, gain[...])

    @pl.when(pl.program_id(0) == pl.num_programs(0) - 1)
    def _():
        dw_ref[...] = acc[...].astype(BF16)


def swap(x, axis, bit):
    count = lax.axis_size(axis)
    return lax.ppermute(x, axis, [(i, i ^ bit) for i in range(count)])


def halo(x, axis):
    count = lax.axis_size(axis)
    prev = lax.ppermute(x, axis, [(i, i + 1) for i in range(count - 1)])
    nxt = lax.ppermute(x, axis, [(i + 1, i) for i in range(count - 1)])
    return prev, nxt


def gather_pieces(x, axis):
    pieces = [x]
    bit = 1
    while bit < lax.axis_size(axis):
        pieces = pieces + [swap(p, axis, bit) for p in pieces]
        bit *= 2
    return pieces


def two_halves(pieces, dim):
    if len(pieces) == 2:
        return pieces
    cut = len(pieces) // 2
    return [jnp.concatenate(pieces[:cut], axis=dim), jnp.concatenate(pieces[cut:], axis=dim)]


def bit_of(axis, bit):
    return (lax.axis_index(axis) // bit) % 2 == 1


def scatter_step(pieces, axis, bit):
    mine = bit_of(axis, bit)
    out = []
    for p in pieces:
        cut = p.shape[0] // 2
        lo, hi = p[:cut], p[cut:]
        got = swap(jnp.where(mine, lo, hi), axis, bit)
        out.append((jnp.where(mine, hi, lo).astype(F32) + got.astype(F32)).astype(BF16))
    return out


def gather_step(p, axis, bit):
    mine = bit_of(axis, bit)
    got = swap(p, axis, bit)
    return jnp.concatenate([jnp.where(mine, got, p), jnp.where(mine, p, got)], axis=0)


def reduce_pieces(pieces, wide, narrow):
    count = lax.axis_size(wide)
    if count > 1:
        pieces = scatter_step(pieces, wide, 1)
    bit = lax.axis_size(narrow) // 2
    while bit >= 1:
        got = [swap(p, narrow, bit) for p in pieces[bit:]]
        pieces = [(a.astype(F32) + b.astype(F32)).astype(BF16) for a, b in zip(pieces[:bit], got)]
        bit //= 2
    bits = []
    bit = 2
    while bit < count:
        bits.append(bit)
        bit *= 2
    for bit in bits:
        pieces = scatter_step(pieces, wide, bit)
    total = pieces[0]
    for bit in reversed(bits):
        total = gather_step(total, wide, bit)
    if count > 1:
        total = gather_step(total, wide, 1)
    return total


def rows512(a):
    cols = a.shape[1]
    if cols < 512:
        return a.reshape(-1, 512)
    return jnp.concatenate([a[:, j : j + 512] for j in range(0, cols, 512)], axis=0)


def unrows512(a, rows, cols):
    if cols < 512:
        return a.reshape(rows, cols)
    return jnp.concatenate([a[j * rows : (j + 1) * rows] for j in range(cols // 512)], axis=1)


def local(
    inputs, segment_ids, norm1_gain, norm1_shift, w_qkv, w_out,
    norm2_gain, norm2_shift, w_up, w_down, cotangent,
):
    feats, samp, width = inputs.shape
    tokens = feats * samp
    blocks = lax.axis_size("narrow")
    group = max(g for g in (1, 2, 4) if feats % g == 0)
    steps = feats // group
    rows = group * samp
    head_cols = w_qkv.shape[2]

    x_prev, x_next = halo(inputs, "wide")
    qkv_halves = [
        h.reshape(width, 3 * h.shape[2]) for h in two_halves(gather_pieces(w_qkv, "narrow"), 2)
    ]
    out_halves = two_halves(gather_pieces(w_out, "narrow"), 0)
    up_halves = two_halves(gather_pieces(w_up, "narrow"), 1)
    down_halves = two_halves(gather_pieces(w_down, "narrow"), 0)

    id_rim = jnp.full((samp,), -1, jnp.int32)
    padded_ids = jnp.concatenate([id_rim, segment_ids, id_rim])
    window_ids = lax.dynamic_slice_in_dim(
        padded_ids, lax.axis_index("wide") * samp, 3 * samp, 0
    )
    id_col = window_ids[:, None]
    id_row = jnp.tile(window_ids.reshape(3, samp), (1, HEADS_PER_GROUP))
    gain1, shift1 = norm1_gain[None, :], norm1_shift[None, :]
    gain2, shift2 = norm2_gain[None, :], norm2_shift[None, :]

    def whole(a):
        return pl.BlockSpec(a.shape, lambda i: (0,) * a.ndim, pipeline_mode=pl.Buffered(1))

    cube = pl.BlockSpec((group, samp, width), lambda i: (i, 0, 0))
    flat = pl.BlockSpec((rows, width), lambda i: (i, 0))
    line = pl.BlockSpec((1, width), lambda i: (0, 0))
    qkv_block = pl.BlockSpec((2, 3, rows, 3 * GROUP_COLS), lambda i: (0, 0, i, 0))

    qkv, attended = pl.pallas_call(
        attn_fwd_kernel,
        grid=(steps,),
        in_specs=[whole(id_col), whole(id_row), cube, cube, cube]
        + [whole(a) for a in (*qkv_halves, gain1, shift1)],
        out_specs=[qkv_block, cube],
        out_shape=[
            jax.ShapeDtypeStruct((2, 3, tokens, 3 * GROUP_COLS), BF16),
            jax.ShapeDtypeStruct((feats, samp, width), BF16),
        ],
        name="attn_fwd",
    )(id_col, id_row, x_prev, inputs, x_next, *qkv_halves, gain1, shift1)

    att_flat = attended.reshape(tokens, width)
    x_flat = inputs.reshape(tokens, width)
    cot_flat = cotangent.reshape(tokens, width)
    half_ff = up_halves[0].shape[1]
    wide_block = pl.BlockSpec((2, rows, half_ff), lambda i: (0, i, 0))
    chain_args = (*out_halves, up_halves[0], up_halves[1], down_halves[0], down_halves[1], gain2, shift2)
    tok = lambda dtype: jax.ShapeDtypeStruct((tokens, width), dtype)
    vec = jax.ShapeDtypeStruct((1, width), F32)
    block_out, normed_two, activated, pre_grad, hidden_grad, residual, dattended, gain2_grad, shift2_grad = pl.pallas_call(
        chain_kernel,
        grid=(steps,),
        in_specs=[flat, flat, flat] + [whole(a) for a in chain_args],
        out_specs=[flat, flat, wide_block, wide_block, flat, flat, flat, line, line],
        out_shape=[
            tok(BF16), tok(BF16),
            jax.ShapeDtypeStruct((2, tokens, half_ff), BF16),
            jax.ShapeDtypeStruct((2, tokens, half_ff), BF16),
            tok(F32), tok(BF16), tok(BF16), vec, vec,
        ],
        name="chain",
    )(x_flat, att_flat, cot_flat, *chain_args)

    datt = dattended.reshape(feats, samp, width)
    d_prev, d_next = halo(datt, "wide")

    def pieces_of(a, dim):
        per = blocks // 2
        size = a[0].shape[dim] // per
        return [lax.slice_in_dim(h, j * size, (j + 1) * size, axis=dim) for h in a for j in range(per)]

    up_grads = pieces_of([dot_tn(normed_two, pre_grad[h]).astype(BF16) for h in range(2)], 1)
    down_grads = pieces_of([dot_tn(activated[h], cot_flat).astype(BF16) for h in range(2)], 0)
    half = width // 2
    out_grads = pieces_of(
        [dot_tn(att_flat[:, h * half : (h + 1) * half], residual).astype(BF16) for h in range(2)], 0
    )
    packs = [
        jnp.concatenate([rows512(u), d, o], axis=0)
        for u, d, o in zip(up_grads, down_grads, out_grads)
    ]
    pack = reduce_pieces(packs, "wide", "narrow")
    up_rows = rows512(jnp.zeros(w_up.shape, BF16)).shape[0]
    down_rows = w_down.shape[0]
    up_grad = unrows512(pack[:up_rows], *w_up.shape).astype(F32)
    down_grad = pack[up_rows : up_rows + down_rows].astype(F32)
    out_grad = pack[up_rows + down_rows :].astype(F32)

    input_grad, qkv_grads, gain1_grad, shift1_grad = pl.pallas_call(
        attn_bwd_kernel,
        grid=(steps,),
        in_specs=[whole(id_col), whole(id_row), cube, qkv_block, cube, cube, cube, flat]
        + [whole(a) for a in (*qkv_halves, gain1, shift1)],
        out_specs=[
            flat,
            pl.BlockSpec((2, width, 3 * GROUP_COLS), lambda i: (0, 0, 0)),
            line,
            line,
        ],
        out_shape=[
            tok(F32),
            jax.ShapeDtypeStruct((2, width, 3 * GROUP_COLS), BF16),
            vec,
            vec,
        ],
        scratch_shapes=[
            pltpu.VMEM((2, width, 3 * GROUP_COLS), F32),
            pltpu.VMEM((2, rows, 3 * GROUP_COLS), BF16),
        ],
        name="attn_bwd",
    )(id_col, id_row, inputs, qkv, d_prev, datt, d_next, hidden_grad, *qkv_halves, gain1, shift1)

    if blocks == 2:
        qkv_pieces = [qkv_grads[0], qkv_grads[1]]
    else:
        qkv_pieces = [
            p.reshape(width, 3 * head_cols)
            for p in pieces_of([qkv_grads[h].reshape(width, 3, GROUP_COLS) for h in range(2)], 2)
        ]
    qkv_grad = reduce_pieces(qkv_pieces, "wide", "narrow").reshape(width, 3, head_cols).astype(F32)
    norm_sums = lax.psum(
        jnp.concatenate([gain1_grad, shift1_grad, gain2_grad, shift2_grad], axis=0),
        ("wide", "narrow"),
    )
    return (
        block_out.reshape(feats, samp, width),
        input_grad.reshape(feats, samp, width),
        norm_sums[0],
        norm_sums[1],
        qkv_grad,
        out_grad,
        norm_sums[2],
        norm_sums[3],
        up_grad,
        down_grad,
    )


def solution(mesh):
    rows = P("narrow", "wide", None)
    placed = (
        rows, P(), P(), P(), P(None, None, "narrow"), P("narrow", None),
        P(), P(), P(None, "narrow"), P("narrow", None), rows,
    )
    outs = (
        rows, rows, P(), P(), P(None, None, "narrow"), P("narrow", None),
        P(), P(), P(None, "narrow"), P("narrow", None),
    )
    return jax.shard_map(local, mesh=mesh, in_specs=placed, out_specs=outs, check_vma=False)
```

time: 764 us -> 300 us (0.39); the launches traced: 755 us -> 299 us
  waiting for transfers between devices: 442 us -> 80.2 us
  local copies, waits for them, and re-layouts: 98.2 us -> 13.5 us
  matrix products: 79.6 us -> 8.12 us
  Pallas kernels: 0 us -> 71.4 us
  starting transfers between devices: 12.6 us -> 64 us
  other arithmetic: 68.1 us -> 20.8 us
  between operations: 14.8 us -> 1.2 us
    reduce_scatter x4 -> x0, waiting for transfers between devices: 202 us -> none  [the longest x1 96 us: local(): lax.psum_scatter(jnp.einsum('fsc,cd->fsd', attended, full_out, preferred_...]
    psum x1 -> x0, waiting for transfers between devices: 132 us -> none  [local(): lax.psum(grad_parts[0].astype(jnp.bfloat16), 'wide').astype(jnp.float32)]
    all_gather x4 -> x0, waiting for transfers between devices: 107 us -> none  [the longest x1 35.6 us: local(): gathered_one = lax.all_gather(normed_one, 'narrow', axis=0, tiled=True)]
    ppermute x4 -> x28, waiting for transfers between devices: 0.02 us -> 80.2 us  [the longest x24 80.2 us: swap(): return lax.ppermute(x, axis, [(i, i ^ bit) for i in range(count)])]
    dot_general x40 -> x6, matrix products: 79.6 us -> 8.12 us  [dot_tn(): lax.dot_general(a, b, (((0,), (0,)), ((), ())), preferred_element_type=F32)]
    pallas_call x0 -> x3, Pallas kernels: none -> 71.4 us  [the longest x1 33.2 us: local(): pl.pallas_call(attn_bwd_kernel, grid=(steps,), in_specs=[whole(id_col), w...]
    ppermute x4 -> x28, starting transfers between devices: 11.9 us -> 64 us  [the longest x24 53.7 us: swap(): return lax.ppermute(x, axis, [(i, i ^ bit) for i in range(count)])]
    reduce_sum x12 -> x0, other arithmetic: 18.7 us -> none  [the longest x3 6.07 us: layer_norm(): return centred * lax.rsqrt(row_var + epsilon) * norm_gain + norm_shift]
  transfers between devices with their start and end apart: 13 -> 28, of which waited for: 9 -> 13; matrix products, arithmetic and copies ran while one was open for 8% -> 9% of each run, Pallas kernels for 0% -> 16%
where the time goes in v1:
time: 300 us; the launch traced here: 299 us
  waiting for transfers between devices  80.2 us (27%)
  Pallas kernels  71.4 us (24%)
  starting transfers between devices  64 us (21%)
  blocking collectives  40 us (13%)
  other arithmetic  20.8 us (7%)
  local copies, waits for them, and re-layouts  13.5 us (4%)
  matrix products  8.12 us (3%)
    ppermute x24, waiting for transfers between devices, swap(): return lax.ppermute(x, axis, [(i, i ^ bit) for i in range(count)])  80.2 us
    ppermute x24, starting transfers between devices, swap(): return lax.ppermute(x, axis, [(i, i ^ bit) for i in range(count)])  53.7 us
    psum x1, blocking collectives, local(): lax.psum(jnp.concatenate([gain1_grad, shift1_grad, gain2_grad, shift2_gra...  40 us
    pallas_call x1, Pallas kernels, local(): pl.pallas_call(attn_bwd_kernel, grid=(steps,), in_specs=[whole(id_col), w...  33.2 us
    pallas_call x1, Pallas kernels, local(): pl.pallas_call(chain_kernel, grid=(steps,), in_specs=[flat, flat, flat] +...  23.9 us
    pallas_call x1, Pallas kernels, local(): pl.pallas_call(attn_fwd_kernel, grid=(steps,), in_specs=[whole(id_col), w...  14.4 us
    dot_general x6, matrix products, dot_tn(): lax.dot_general(a, b, (((0,), (0,)), ((), ())), preferred_element_type=F32)  8.12 us
    ppermute x2, starting transfers between devices, halo(): prev = lax.ppermute(x, axis, [(i, i + 1) for i in range(count - 1)])  7.31 us
  transfers between devices with their start and end apart: 28, of which 13 were waited for; matrix products, arithmetic and copies ran while one was open for 9% of the time, Pallas kernels for 16%

profile of v1, /device:TPU:0, one launch (start us, length us, event | category | flops | bytes accessed | tf_op | source)
XLA Modules:
  0.0 299.2 jit_solution(8565306257474494267)
XLA Ops:
  2.1 4.0 %collective-permute-start = (bf16[16,64,512]{2,1,0:T(8,128)(2,1)}, bf16[16,64,512]{2,1,0:T(8,128)(2,1)}, u32[]{:S(2)}, u32[]{:S(2)}) collective-permute-start(bf16[16,64,512]{2,1,0:T(8,128)(2,1)} %x.1), channel_id=1, source_target_pairs={{0,2},{2,4},{4,6},{6,8},{8,10},{10,12},{12,14},{14,16},{16,18},{18... | collective-permute-start | bytes 3145736 | tf_op jit(solution)/shard_map/ppermute | solution.py:230
  7.5 3.0 %collective-permute-start.2 = (bf16[512,3,256]{0,2,1:T(8,128)(2,1)S(1)}, bf16[512,3,256]{0,2,1:T(8,128)(2,1)S(1)}, u32[]{:S(2)}, u32[]{:S(2)}) collective-permute-start(bf16[512,3,256]{0,2,1:T(8,128)(2,1)S(1)} %copy.24), channel_id=1, source_target_pairs={{0,1},{1,0},{2,3},{3,2},{4,5},{5,4},{6,7},{7,6},{8,9},{9,8},{10,11... | collective-permute-start | bytes 2359304 | tf_op jit(solution)/shard_map/ppermute | solution.py:225
  12.6 16.4 %collective-permute-done.2 = bf16[512,3,256]{0,2,1:T(8,128)(2,1)S(1)} collective-permute-done((bf16[512,3,256]{0,2,1:T(8,128)(2,1)S(1)}, bf16[512,3,256]{0,2,1:T(8,128)(2,1)S(1)}, u32[]{:S(2)}, u32[]{:S(2)}) %collective-permute-start.2) | collective-permute-done | bytes 786464 | tf_op jit(solution)/shard_map/ppermute | solution.py:225
  37.1 14.4 %attn_fwd.1 = (bf16[2,3,1024,768]{3,2,1,0:T(8,128)(2,1)}, bf16[16,64,512]{2,1,0:T(8,128)(2,1)}) custom-call(s32[192,1]{1,0:T(8,128)} %copy.26.idc, s32[3,256]{1,0:T(4,128)} %tile.12.idr, bf16[16,64,512]{2,1,0:T(8,128)(2,1)} %collective-permute-done.xp, bf16[16,64,512]{2,1,0:T(8,128)(2,1)} %x.1, bf16[16,64,512]{2,1,0:T(8,128)(2,1)} %collective-permute-done.1.xn, ...), custom_call_target="tpu_custom_call" | custom-call | tf_op jit(solution)/shard_map/attn_fwd/pallas_call | solution.py:347
  51.5 27.8 %collective-permute-done.3.wo1 = bf16[256,512]{1,0:T(8,128)(2,1)S(1)} collective-permute-done((bf16[256,512]{1,0:T(8,128)(2,1)S(1)}, bf16[256,512]{1,0:T(8,128)(2,1)S(1)}, u32[]{:S(2)}, u32[]{:S(2)}) %collective-permute-start.3) | collective-permute-done | bytes 262176 | tf_op jit(solution)/shard_map/ppermute | solution.py:225
  80.3 23.9 %chain.1 = (bf16[1024,512]{1,0:T(8,128)(2,1)}, bf16[1024,512]{1,0:T(8,128)(2,1)}, bf16[2,1024,1024]{2,1,0:T(8,128)(2,1)}, bf16[2,1024,1024]{2,1,0:T(8,128)(2,1)}...) custom-call(bf16[1024,512]{1,0:T(8,128)(2,1)} %bitcast.54, ...), custom_call_target="tpu_custom_call" | custom-call | tf_op jit(solution)/shard_map/chain/pallas_call | solution.py:368
  104.2 3.3 %fusion.21 = bf16[512,1024]{1,0:T(8,128)(2,1)S(1)} fusion(bf16[1024,512]{1,0:T(8,128)(2,1)} %get-tuple-element.38, bf16[2,1024,1024]{2,1,0:T(8,128)(2,1)} %get-tuple-element.39), kind=kOutput, calls=%fused_computation.18 | convolution fusion | flops 1074266112 | bytes 4194304 | tf_op jit(solution)/shard_map/dot_general | solution.py:27
  110.5 3.3 %collective-permute-start.6 = (bf16[16,64,512]{2,1,0:T(8,128)(2,1)S(1)}, bf16[16,64,512]{2,1,0:T(8,128)(2,1)S(1)}, u32[]{:S(2)}, u32[]{:S(2)}) collective-permute-start(bf16[16,64,512]{2,1,0:T(8,128)(2,1)S(1)} %bitcast.65), channel_id=1, source_target_pairs={{0,2},{2,4},{4,6},{6,8},{8,10},{10,12},{12,14},{14,16},{16,18},{18... | collective-permute-start | bytes 3145736 | tf_op jit(solution)/shard_map/ppermute | solution.py:230
  123.8 33.2 %attn_bwd.1 = (f32[1024,512]{1,0:T(8,128)}, bf16[2,512,768]{2,1,0:T(8,128)(2,1)}, f32[1,512]{1,0:T(1,128)}, f32[1,512]{1,0:T(1,128)}) custom-call(s32[192,1]{1,0:T(8,128)} %copy.26.idc, s32[3,256]{1,0:T(4,128)} %tile.12.idr, bf16[16,64,512]{2,1,0:T(8,128)(2,1)} %x.1, bf16[2,3,1024,768]{3,2,1,0:T(8,128)(2,1)} %get-tuple-element.27.qkv_ref, ...), custom_call_target="tpu_custom_call" | custom-call | tf_op jit(solution)/shard_map/attn_bwd/pallas_call | solution.py:407
  159.4 13.6 %collective-permute-start.9 = (bf16[256,768]{1,0:T(8,128)(2,1)}, bf16[256,768]{1,0:T(8,128)(2,1)}, u32[]{:S(2)}, u32[]{:S(2)}) collective-permute-start(bf16[256,768]{1,0:T(8,128)(2,1)} %get-tuple-element.63), channel_id=1, source_target_pairs={{0,2},{2,0},{4,6},{6,4},{8,10},{10,8},{12,14},{14,12},{16,18},{18,... | collective-permute-start | bytes 1179656 | tf_op jit(solution)/shard_map/ppermute | solution.py:225
  178.1 2.7 add_convert_fusion
  181.7 2.7 collective-permute-start.21
  184.4 3.9 %collective-permute-done.10 = bf16[256,768]{1,0:T(8,128)(2,1)} collective-permute-done((bf16[256,768]{1,0:T(8,128)(2,1)}, bf16[256,768]{1,0:T(8,128)(2,1)}, u32[]{:S(2)}, u32[]{:S(2)}) %collective-permute-start.10) | collective-permute-done | bytes 393248 | tf_op jit(solution)/shard_map/ppermute | solution.py:225
  192.2 6.7 %collective-permute-done.21 = bf16[576,512]{1,0:T(8,128)(2,1)} collective-permute-done((bf16[576,512]{1,0:T(8,128)(2,1)}, bf16[576,512]{1,0:T(8,128)(2,1)}, u32[]{:S(2)}, u32[]{:S(2)}) %collective-permute-start.21) | collective-permute-done | bytes 589856 | tf_op jit(solution)/shard_map/ppermute | solution.py:225
  202.7 5.5 %collective-permute-done.22 = bf16[288,512]{1,0:T(8,128)(2,1)S(1)} collective-permute-done((bf16[288,512]{1,0:T(8,128)(2,1)S(1)}, bf16[288,512]{1,0:T(8,128)(2,1)S(1)}, u32[]{:S(2)}, u32[]{:S(2)}) %collective-permute-start.22) | collective-permute-done | bytes 294944 | tf_op jit(solution)/shard_map/ppermute | solution.py:225
  208.3 2.8 collective-permute-start.23
  212.8 3.3 %collective-permute-done.23 = bf16[144,512]{1,0:T(8,128)(2,1)S(1)} collective-permute-done((bf16[144,512]{1,0:T(8,128)(2,1)S(1)}, bf16[144,512]{1,0:T(8,128)(2,1)S(1)}, u32[]{:S(2)}, u32[]{:S(2)}) %collective-permute-start.23) | collective-permute-done | bytes 147488 | tf_op jit(solution)/shard_map/ppermute | solution.py:225
  217.4 4.9 %collective-permute-done.24 = bf16[144,512]{1,0:T(8,128)(2,1)S(1)} collective-permute-done((bf16[144,512]{1,0:T(8,128)(2,1)S(1)}, bf16[144,512]{1,0:T(8,128)(2,1)S(1)}, u32[]{:S(2)}, u32[]{:S(2)}) %collective-permute-start.24) | collective-permute-done | bytes 147488 | tf_op jit(solution)/shard_map/ppermute | solution.py:225
  222.4 5.1 %collective-permute-start.25 = (bf16[288,512]{1,0:T(8,128)(2,1)S(1)}, bf16[288,512]{1,0:T(8,128)(2,1)S(1)}, u32[]{:S(2)}, u32[]{:S(2)}) collective-permute-start(bf16[288,512]{1,0:T(8,128)(2,1)S(1)} %pad_maximum_fusion.10), channel_id=1, source_target_pairs={{0,8},{2,10},{4,12},{6,14},{8,0},{10,2},{12,4},{14,6},{16,24},{18,... | collective-permute-start | bytes 884744 | tf_op jit(solution)/shard_map/ppermute | solution.py:225
  229.9 2.9 collective-permute-done.13
  232.8 2.9 collective-permute-start.14
  237.9 3.8 %collective-permute-start.15 = (bf16[64,768]{1,0:T(8,128)(2,1)S(1)}, bf16[64,768]{1,0:T(8,128)(2,1)S(1)}, u32[]{:S(2)}, u32[]{:S(2)}) collective-permute-start(bf16[64,768]{1,0:T(8,128)(2,1)S(1)} %pad_maximum_fusion.12), channel_id=1, source_target_pairs={{0,8},{2,10},{4,12},{6,14},{8,0},{10,2},{12,4},{14,6},{16,24},{18,... | collective-permute-start | bytes 294920 | tf_op jit(solution)/shard_map/ppermute | solution.py:225
  241.7 2.6 collective-permute-done.15
  250.4 40.0 %psum.7 = f32[4,512]{1,0:T(4,128)S(1)} all-reduce(f32[4,512]{1,0:T(4,128)S(1)} %pad_maximum_fusion.13), channel_id=1, replica_groups=mesh['wide'=16,'narrow'=2] {'wide','narrow'}, use_global_device_ids=true, to_apply=%region_0.1 | all-reduce | flops 2048 | bytes 16384 | tf_op jit(solution)/shard_map/psum | solution.py:439
  (148 shorter events, 65.3 us)
Async XLA Ops:
  0.7 36.4 %collective-permute-start.1 = (bf16[16,64,512]{2,1,0:T(8,128)(2,1)}, bf16[16,64,512]{2,1,0:T(8,128)(2,1)}, u32[]{:S(2)}, u32[]{:S(2)}) collective-permute-start(bf16[16,64,512]{2,1,0:T(8,128)(2,1)} %x.1), channel_id=1, source_target_pairs={{2,0},{4,2},{6,4},{8,6},{10,8},{12,10},{14,12},{16,14},{18,16},{20... | collective-permute-start | bytes 3145736 | tf_op jit(solution)/shard_map/ppermute | solution.py:231
  2.1 35.0 %collective-permute-start = (bf16[16,64,512]{2,1,0:T(8,128)(2,1)}, bf16[16,64,512]{2,1,0:T(8,128)(2,1)}, u32[]{:S(2)}, u32[]{:S(2)}) collective-permute-start(bf16[16,64,512]{2,1,0:T(8,128)(2,1)} %x.1), channel_id=1, source_target_pairs={{0,2},{2,4},{4,6},{6,8},{8,10},{10,12},{12,14},{14,16},{16,18},{18... | collective-permute-start | bytes 3145736 | tf_op jit(solution)/shard_map/ppermute | solution.py:230
  7.5 21.4 %collective-permute-start.2 = (bf16[512,3,256]{0,2,1:T(8,128)(2,1)S(1)}, bf16[512,3,256]{0,2,1:T(8,128)(2,1)S(1)}, u32[]{:S(2)}, u32[]{:S(2)}) collective-permute-start(bf16[512,3,256]{0,2,1:T(8,128)(2,1)S(1)} %copy.24), channel_id=1, source_target_pairs={{0,1},{1,0},{2,3},{3,2},{4,5},{5,4},{6,7},{7,6},{8,9},{9,8},{10,11... | collective-permute-start | bytes 2359304 | tf_op jit(solution)/shard_map/ppermute | solution.py:225
  10.6 68.7 %collective-permute-start.4 = (bf16[512,1024]{1,0:T(8,128)(2,1)S(1)}, bf16[512,1024]{1,0:T(8,128)(2,1)S(1)}, u32[]{:S(2)}, u32[]{:S(2)}) collective-permute-start(bf16[512,1024]{1,0:T(8,128)(2,1)S(1)} %copy-done.7), channel_id=1, source_target_pairs={{0,1},{1,0},{2,3},{3,2},{4,5},{5,4},{6,7},{7,6},{8,9},{9,8},{10,11... | collective-permute-start | bytes 3145736 | tf_op jit(solution)/shard_map/ppermute | solution.py:225
  10.7 68.6 %collective-permute-start.5 = (bf16[1024,512]{1,0:T(8,128)(2,1)}, bf16[1024,512]{1,0:T(8,128)(2,1)}, u32[]{:S(2)}, u32[]{:S(2)}) collective-permute-start(bf16[1024,512]{1,0:T(8,128)(2,1)} %wd0.1), channel_id=1, source_target_pairs={{0,1},{1,0},{2,3},{3,2},{4,5},{5,4},{6,7},{7,6},{8,9},{9,8},{10,11... | collective-permute-start | bytes 3145736 | tf_op jit(solution)/shard_map/ppermute | solution.py:225
  29.9 49.4 %collective-permute-start.3 = (bf16[256,512]{1,0:T(8,128)(2,1)S(1)}, bf16[256,512]{1,0:T(8,128)(2,1)S(1)}, u32[]{:S(2)}, u32[]{:S(2)}) collective-permute-start(bf16[256,512]{1,0:T(8,128)(2,1)S(1)} %copy-done.15), channel_id=1, source_target_pairs={{0,1},{1,0},{2,3},{3,2},{4,5},{5,4},{6,7},{7,6},{8,9},{9,8},{10,11... | collective-permute-start | bytes 786440 | tf_op jit(solution)/shard_map/ppermute | solution.py:225
  108.9 12.9 %collective-permute-start.7 = (bf16[16,64,512]{2,1,0:T(8,128)(2,1)S(1)}, bf16[16,64,512]{2,1,0:T(8,128)(2,1)S(1)}, u32[]{:S(2)}, u32[]{:S(2)}) collective-permute-start(bf16[16,64,512]{2,1,0:T(8,128)(2,1)S(1)} %bitcast.64), channel_id=1, source_target_pairs={{2,0},{4,2},{6,4},{8,6},{10,8},{12,10},{14,12},{16,14},{18,16},{20... | collective-permute-start | bytes 3145736 | tf_op jit(solution)/shard_map/ppermute | solution.py:231
  110.5 11.3 %collective-permute-start.6 = (bf16[16,64,512]{2,1,0:T(8,128)(2,1)S(1)}, bf16[16,64,512]{2,1,0:T(8,128)(2,1)S(1)}, u32[]{:S(2)}, u32[]{:S(2)}) collective-permute-start(bf16[16,64,512]{2,1,0:T(8,128)(2,1)S(1)} %bitcast.65), channel_id=1, source_target_pairs={{0,2},{2,4},{4,6},{6,8},{8,10},{10,12},{12,14},{14,16},{16,18},{18... | collective-permute-start | bytes 3145736 | tf_op jit(solution)/shard_map/ppermute | solution.py:230
  120.3 57.8 %collective-permute-start.18 = (bf16[1152,512]{1,0:T(8,128)(2,1)}, bf16[1152,512]{1,0:T(8,128)(2,1)}, u32[]{:S(2)}, u32[]{:S(2)}) collective-permute-start(bf16[1152,512]{1,0:T(8,128)(2,1)} %broadcast_select_fusion.3), channel_id=1, source_target_pairs={{0,2},{2,0},{4,6},{6,4},{8,10},{10,8},{12,14},{14,12},{16,18},{18,... | collective-permute-start | bytes 3538952 | tf_op jit(solution)/shard_map/ppermute | solution.py:225
  120.8 57.3 %collective-permute-start.20 = (bf16[1152,512]{1,0:T(8,128)(2,1)S(1)}, bf16[1152,512]{1,0:T(8,128)(2,1)}, u32[]{:S(2)}, u32[]{:S(2)}) collective-permute-start(bf16[1152,512]{1,0:T(8,128)(2,1)S(1)} %add_convert_fusion.1), channel_id=1, source_target_pairs={{0,1},{1,0},{2,3},{3,2},{4,5},{5,4},{6,7},{7,6},{8,9},{9,8},{10,11... | collective-permute-start | bytes 3538952 | tf_op jit(solution)/shard_map/ppermute | solution.py:225
  159.4 15.3 %collective-permute-start.9 = (bf16[256,768]{1,0:T(8,128)(2,1)}, bf16[256,768]{1,0:T(8,128)(2,1)}, u32[]{:S(2)}, u32[]{:S(2)}) collective-permute-start(bf16[256,768]{1,0:T(8,128)(2,1)} %get-tuple-element.63), channel_id=1, source_target_pairs={{0,2},{2,0},{4,6},{6,4},{8,10},{10,8},{12,14},{14,12},{16,18},{18,... | collective-permute-start | bytes 1179656 | tf_op jit(solution)/shard_map/ppermute | solution.py:225
  173.0 11.4 %collective-permute-start.8 = (bf16[256,768]{1,0:T(8,128)(2,1)}, bf16[256,768]{1,0:T(8,128)(2,1)}, u32[]{:S(2)}, u32[]{:S(2)}) collective-permute-start(bf16[256,768]{1,0:T(8,128)(2,1)} %get-tuple-element.62), channel_id=1, source_target_pairs={{0,2},{2,0},{4,6},{6,4},{8,10},{10,8},{12,14},{14,12},{16,18},{18,... | collective-permute-start | bytes 1179656 | tf_op jit(solution)/shard_map/ppermute | solution.py:225
  176.6 11.7 %collective-permute-start.10 = (bf16[256,768]{1,0:T(8,128)(2,1)}, bf16[256,768]{1,0:T(8,128)(2,1)}, u32[]{:S(2)}, u32[]{:S(2)}) collective-permute-start(bf16[256,768]{1,0:T(8,128)(2,1)} %fusion.25), channel_id=1, source_target_pairs={{0,1},{1,0},{2,3},{3,2},{4,5},{5,4},{6,7},{7,6},{8,9},{9,8},{10,11... | collective-permute-start | bytes 1179656 | tf_op jit(solution)/shard_map/ppermute | solution.py:225
  181.7 17.2 %collective-permute-start.21 = (bf16[576,512]{1,0:T(8,128)(2,1)}, bf16[576,512]{1,0:T(8,128)(2,1)}, u32[]{:S(2)}, u32[]{:S(2)}) collective-permute-start(bf16[576,512]{1,0:T(8,128)(2,1)} %broadcast_select_fusion.6), channel_id=1, source_target_pairs={{0,4},{2,6},{4,0},{6,2},{8,12},{10,14},{12,8},{14,10},{16,20},{18,... | collective-permute-start | bytes 1769480 | tf_op jit(solution)/shard_map/ppermute | solution.py:225
  189.7 13.0 %collective-permute-start.11 = (bf16[128,768]{1,0:T(8,128)(2,1)S(1)}, bf16[128,768]{1,0:T(8,128)(2,1)S(1)}, u32[]{:S(2)}, u32[]{:S(2)}) collective-permute-start(bf16[128,768]{1,0:T(8,128)(2,1)S(1)} %broadcast_select_fusion.14), channel_id=1, source_target_pairs={{0,4},{2,6},{4,0},{6,2},{8,12},{10,14},{12,8},{14,10},{16,20},{18,... | collective-permute-start | bytes 589832 | tf_op jit(solution)/shard_map/ppermute | solution.py:225
  200.3 7.9 %collective-permute-start.22 = (bf16[288,512]{1,0:T(8,128)(2,1)S(1)}, bf16[288,512]{1,0:T(8,128)(2,1)S(1)}, u32[]{:S(2)}, u32[]{:S(2)}) collective-permute-start(bf16[288,512]{1,0:T(8,128)(2,1)S(1)} %broadcast_select_fusion.11), channel_id=1, source_target_pairs={{0,8},{2,10},{4,12},{6,14},{8,0},{10,2},{12,4},{14,6},{16,24},{18,... | collective-permute-start | bytes 884744 | tf_op jit(solution)/shard_map/ppermute | solution.py:225
  208.3 7.8 %collective-permute-start.23 = (bf16[144,512]{1,0:T(8,128)(2,1)S(1)}, bf16[144,512]{1,0:T(8,128)(2,1)S(1)}, u32[]{:S(2)}, u32[]{:S(2)}) collective-permute-start(bf16[144,512]{1,0:T(8,128)(2,1)S(1)} %broadcast_select_fusion.17), channel_id=1, source_target_pairs={{0,16},{2,18},{4,20},{6,22},{8,24},{10,26},{12,28},{14,30},{16,0},... | collective-permute-start | bytes 442376 | tf_op jit(solution)/shard_map/ppermute | solution.py:225
  211.1 6.3 %collective-permute-start.12 = (bf16[64,768]{1,0:T(8,128)(2,1)S(1)}, bf16[64,768]{1,0:T(8,128)(2,1)S(1)}, u32[]{:S(2)}, u32[]{:S(2)}) collective-permute-start(bf16[64,768]{1,0:T(8,128)(2,1)S(1)} %broadcast_select_fusion.20), channel_id=1, source_target_pairs={{0,8},{2,10},{4,12},{6,14},{8,0},{10,2},{12,4},{14,6},{16,24},{18,... | collective-permute-start | bytes 294920 | tf_op jit(solution)/shard_map/ppermute | solution.py:225
  216.2 6.1 %collective-permute-start.24 = (bf16[144,512]{1,0:T(8,128)(2,1)S(1)}, bf16[144,512]{1,0:T(8,128)(2,1)S(1)}, u32[]{:S(2)}, u32[]{:S(2)}) collective-permute-start(bf16[144,512]{1,0:T(8,128)(2,1)S(1)} %add_convert_fusion.7), channel_id=1, source_target_pairs={{0,16},{2,18},{4,20},{6,22},{8,24},{10,26},{12,28},{14,30},{16,0},... | collective-permute-start | bytes 442376 | tf_op jit(solution)/shard_map/ppermute | solution.py:225
  222.4 13.4 %collective-permute-start.25 = (bf16[288,512]{1,0:T(8,128)(2,1)S(1)}, bf16[288,512]{1,0:T(8,128)(2,1)S(1)}, u32[]{:S(2)}, u32[]{:S(2)}) collective-permute-start(bf16[288,512]{1,0:T(8,128)(2,1)S(1)} %pad_maximum_fusion.10), channel_id=1, source_target_pairs={{0,8},{2,10},{4,12},{6,14},{8,0},{10,2},{12,4},{14,6},{16,24},{18,... | collective-permute-start | bytes 884744 | tf_op jit(solution)/shard_map/ppermute | solution.py:225
  235.9 10.8 %collective-permute-start.26 = (bf16[576,512]{1,0:T(8,128)(2,1)S(1)}, bf16[576,512]{1,0:T(8,128)(2,1)S(1)}, u32[]{:S(2)}, u32[]{:S(2)}) collective-permute-start(bf16[576,512]{1,0:T(8,128)(2,1)S(1)} %pad_maximum_fusion.8), channel_id=1, source_target_pairs={{0,4},{2,6},{4,0},{6,2},{8,12},{10,14},{12,8},{14,10},{16,20},{18,... | collective-permute-start | bytes 1769480 | tf_op jit(solution)/shard_map/ppermute | solution.py:225
  237.9 6.4 %collective-permute-start.15 = (bf16[64,768]{1,0:T(8,128)(2,1)S(1)}, bf16[64,768]{1,0:T(8,128)(2,1)S(1)}, u32[]{:S(2)}, u32[]{:S(2)}) collective-permute-start(bf16[64,768]{1,0:T(8,128)(2,1)S(1)} %pad_maximum_fusion.12), channel_id=1, source_target_pairs={{0,8},{2,10},{4,12},{6,14},{8,0},{10,2},{12,4},{14,6},{16,24},{18,... | collective-permute-start | bytes 294920 | tf_op jit(solution)/shard_map/ppermute | solution.py:225
  248.1 45.2 %collective-permute-start.27 = (bf16[1152,512]{1,0:T(8,128)(2,1)}, bf16[1152,512]{1,0:T(8,128)(2,1)}, u32[]{:S(2)}, u32[]{:S(2)}) collective-permute-start(bf16[1152,512]{1,0:T(8,128)(2,1)} %pad_maximum_fusion.6), channel_id=1, source_target_pairs={{0,2},{2,0},{4,6},{6,4},{8,10},{10,8},{12,14},{14,12},{16,18},{18,... | collective-permute-start | bytes 3538952 | tf_op jit(solution)/shard_map/ppermute | solution.py:225
  250.3 40.7 %collective-permute-start.17 = (bf16[256,768]{1,0:T(8,128)(2,1)S(1)}, bf16[256,768]{1,0:T(8,128)(2,1)S(1)}, u32[]{:S(2)}, u32[]{:S(2)}) collective-permute-start(bf16[256,768]{1,0:T(8,128)(2,1)S(1)} %pad_maximum_fusion.9), channel_id=1, source_target_pairs={{0,2},{2,0},{4,6},{6,4},{8,10},{10,8},{12,14},{14,12},{16,18},{18,... | collective-permute-start | bytes 1179656 | tf_op jit(solution)/shard_map/ppermute | solution.py:225
  (30 other events, 175.4 us)

commit v2 on v1

--- a/solution.py
+++ b/solution.py
@@ -436,10 +436,12 @@
             for p in pieces_of([qkv_grads[h].reshape(width, 3, GROUP_COLS) for h in range(2)], 2)
         ]
     qkv_grad = reduce_pieces(qkv_pieces, "wide", "narrow").reshape(width, 3, head_cols).astype(F32)
-    norm_sums = lax.psum(
-        jnp.concatenate([gain1_grad, shift1_grad, gain2_grad, shift2_grad], axis=0),
-        ("wide", "narrow"),
-    )
+    norm_sums = jnp.concatenate([gain1_grad, shift1_grad, gain2_grad, shift2_grad], axis=0)
+    for axis in ("wide", "narrow"):
+        bit = 1
+        while bit < lax.axis_size(axis):
+            norm_sums = norm_sums + swap(norm_sums, axis, bit)
+            bit *= 2
     return (
         block_out.reshape(feats, samp, width),
         input_grad.reshape(feats, samp, width),

time: 300 us -> 303 us (1.010)
  waiting for transfers between devices: 80.2 us -> 134 us
  blocking collectives: 40 us -> 0 us
  starting transfers between devices: 64 us -> 53.5 us
    ppermute x24 -> x29, waiting for transfers between devices: 80.2 us -> 134 us  [swap(): return lax.ppermute(x, axis, [(i, i ^ bit) for i in range(count)])]
    psum x1 -> x0, blocking collectives: 40 us -> none  [local(): lax.psum(jnp.concatenate([gain1_grad, shift1_grad, gain2_grad, shift2_gra...]
    ppermute x24 -> x29, starting transfers between devices: 53.7 us -> 43.2 us  [swap(): return lax.ppermute(x, axis, [(i, i ^ bit) for i in range(count)])]
    unnamed x54 -> x68, local copies, waits for them, and re-layouts: 7.06 us -> 7.85 us
  transfers between devices with their start and end apart: 28 -> 33, of which waited for: 13 -> 18; matrix products, arithmetic and copies ran while one was open for 9% -> 9% of each run, Pallas kernels for 16% -> 16%
where the time goes in v2:
time: 303 us
  waiting for transfers between devices  134 us (44%)
  Pallas kernels  71.4 us (24%)
  starting transfers between devices  53.5 us (18%)
  other arithmetic  20.9 us (7%)
  local copies, waits for them, and re-layouts  14.3 us (5%)
  matrix products  8.07 us (3%)
    ppermute x29, waiting for transfers between devices, swap(): return lax.ppermute(x, axis, [(i, i ^ bit) for i in range(count)])  134 us
    ppermute x29, starting transfers between devices, swap(): return lax.ppermute(x, axis, [(i, i ^ bit) for i in range(count)])  43.2 us
    pallas_call x1, Pallas kernels, local(): pl.pallas_call(attn_bwd_kernel, grid=(steps,), in_specs=[whole(id_col), w...  33.2 us
    pallas_call x1, Pallas kernels, local(): pl.pallas_call(chain_kernel, grid=(steps,), in_specs=[flat, flat, flat] +...  23.8 us
    pallas_call x1, Pallas kernels, local(): pl.pallas_call(attn_fwd_kernel, grid=(steps,), in_specs=[whole(id_col), w...  14.4 us
    dot_general x6, matrix products, dot_tn(): lax.dot_general(a, b, (((0,), (0,)), ((), ())), preferred_element_type=F32)  8.07 us
    unnamed x68, local copies, waits for them, and re-layouts  7.85 us
    ppermute x2, starting transfers between devices, halo(): prev = lax.ppermute(x, axis, [(i, i + 1) for i in range(count - 1)])  7.3 us
  transfers between devices with their start and end apart: 33, of which 18 were waited for; matrix products, arithmetic and copies ran while one was open for 9% of the time, Pallas kernels for 16%

profile of v2, /device:TPU:0, one launch (start us, length us, event | category | flops | bytes accessed | tf_op | source)
XLA Modules:
  0.0 303.0 jit_solution(11460384707799437744)
XLA Ops:
  2.1 4.0 %collective-permute-start = (bf16[16,64,512]{2,1,0:T(8,128)(2,1)}, bf16[16,64,512]{2,1,0:T(8,128)(2,1)}, u32[]{:S(2)}, u32[]{:S(2)}) collective-permute-start(bf16[16,64,512]{2,1,0:T(8,128)(2,1)} %x.1), channel_id=1, source_target_pairs={{0,2},{2,4},{4,6},{6,8},{8,10},{10,12},{12,14},{14,16},{16,18},{18... | collective-permute-start | bytes 3145736 | tf_op jit(solution)/shard_map/ppermute | solution.py:230
  7.5 3.0 %collective-permute-start.2 = (bf16[512,3,256]{0,2,1:T(8,128)(2,1)S(1)}, bf16[512,3,256]{0,2,1:T(8,128)(2,1)S(1)}, u32[]{:S(2)}, u32[]{:S(2)}) collective-permute-start(bf16[512,3,256]{0,2,1:T(8,128)(2,1)S(1)} %copy.24), channel_id=1, source_target_pairs={{0,1},{1,0},{2,3},{3,2},{4,5},{5,4},{6,7},{7,6},{8,9},{9,8},{10,11... | collective-permute-start | bytes 2359304 | tf_op jit(solution)/shard_map/ppermute | solution.py:225
  12.6 16.4 %collective-permute-done.2 = bf16[512,3,256]{0,2,1:T(8,128)(2,1)S(1)} collective-permute-done((bf16[512,3,256]{0,2,1:T(8,128)(2,1)S(1)}, bf16[512,3,256]{0,2,1:T(8,128)(2,1)S(1)}, u32[]{:S(2)}, u32[]{:S(2)}) %collective-permute-start.2) | collective-permute-done | bytes 786464 | tf_op jit(solution)/shard_map/ppermute | solution.py:225
  37.1 14.4 %attn_fwd.1 = (bf16[2,3,1024,768]{3,2,1,0:T(8,128)(2,1)}, bf16[16,64,512]{2,1,0:T(8,128)(2,1)}) custom-call(s32[192,1]{1,0:T(8,128)} %copy.26.idc, s32[3,256]{1,0:T(4,128)} %tile.12.idr, bf16[16,64,512]{2,1,0:T(8,128)(2,1)} %collective-permute-done.xp, bf16[16,64,512]{2,1,0:T(8,128)(2,1)} %x.1, bf16[16,64,512]{2,1,0:T(8,128)(2,1)} %collective-permute-done.1.xn, ...), custom_call_target="tpu_custom_call" | custom-call | tf_op jit(solution)/shard_map/attn_fwd/pallas_call | solution.py:347
  51.5 27.8 %collective-permute-done.3.wo1 = bf16[256,512]{1,0:T(8,128)(2,1)S(1)} collective-permute-done((bf16[256,512]{1,0:T(8,128)(2,1)S(1)}, bf16[256,512]{1,0:T(8,128)(2,1)S(1)}, u32[]{:S(2)}, u32[]{:S(2)}) %collective-permute-start.3) | collective-permute-done | bytes 262176 | tf_op jit(solution)/shard_map/ppermute | solution.py:225
  80.3 23.8 %chain.1 = (bf16[1024,512]{1,0:T(8,128)(2,1)}, bf16[1024,512]{1,0:T(8,128)(2,1)}, bf16[2,1024,1024]{2,1,0:T(8,128)(2,1)}, bf16[2,1024,1024]{2,1,0:T(8,128)(2,1)}...) custom-call(bf16[1024,512]{1,0:T(8,128)(2,1)} %bitcast.54, ...), custom_call_target="tpu_custom_call" | custom-call | tf_op jit(solution)/shard_map/chain/pallas_call | solution.py:368
  104.2 3.3 %fusion.21 = bf16[512,1024]{1,0:T(8,128)(2,1)S(1)} fusion(bf16[1024,512]{1,0:T(8,128)(2,1)} %get-tuple-element.38, bf16[2,1024,1024]{2,1,0:T(8,128)(2,1)} %get-tuple-element.39), kind=kOutput, calls=%fused_computation.18 | convolution fusion | flops 1074266112 | bytes 4194304 | tf_op jit(solution)/shard_map/dot_general | solution.py:27
  110.4 3.3 %collective-permute-start.6 = (bf16[16,64,512]{2,1,0:T(8,128)(2,1)S(1)}, bf16[16,64,512]{2,1,0:T(8,128)(2,1)S(1)}, u32[]{:S(2)}, u32[]{:S(2)}) collective-permute-start(bf16[16,64,512]{2,1,0:T(8,128)(2,1)S(1)} %bitcast.65), channel_id=1, source_target_pairs={{0,2},{2,4},{4,6},{6,8},{8,10},{10,12},{12,14},{14,16},{16,18},{18... | collective-permute-start | bytes 3145736 | tf_op jit(solution)/shard_map/ppermute | solution.py:230
  123.4 33.2 %attn_bwd.1 = (f32[1024,512]{1,0:T(8,128)}, bf16[2,512,768]{2,1,0:T(8,128)(2,1)}, f32[1,512]{1,0:T(1,128)}, f32[1,512]{1,0:T(1,128)}) custom-call(s32[192,1]{1,0:T(8,128)} %copy.26.idc, s32[3,256]{1,0:T(4,128)} %tile.12.idr, bf16[16,64,512]{2,1,0:T(8,128)(2,1)} %x.1, bf16[2,3,1024,768]{3,2,1,0:T(8,128)(2,1)} %get-tuple-element.27.qkv_ref, ...), custom_call_target="tpu_custom_call" | custom-call | tf_op jit(solution)/shard_map/attn_bwd/pallas_call | solution.py:407
  158.9 14.0 %collective-permute-start.14 = (bf16[256,768]{1,0:T(8,128)(2,1)S(1)}, bf16[256,768]{1,0:T(8,128)(2,1)S(1)}, u32[]{:S(2)}, u32[]{:S(2)}) collective-permute-start(bf16[256,768]{1,0:T(8,128)(2,1)S(1)} %get-tuple-element.63), channel_id=1, source_target_pairs={{0,2},{2,0},{4,6},{6,4},{8,10},{10,8},{12,14},{14,12},{16,18},{18,... | collective-permute-start | bytes 1179656 | tf_op jit(solution)/shard_map/ppermute | solution.py:225
  172.9 2.8 add_convert_fusion.1
  179.8 32.6 %collective-permute-done.15 = bf16[256,768]{1,0:T(8,128)(2,1)} collective-permute-done((bf16[256,768]{1,0:T(8,128)(2,1)}, bf16[256,768]{1,0:T(8,128)(2,1)}, u32[]{:S(2)}, u32[]{:S(2)}) %collective-permute-start.15) | collective-permute-done | bytes 393248 | tf_op jit(solution)/shard_map/ppermute | solution.py:225
  213.8 2.8 collective-permute-start.16
  219.0 2.8 collective-permute-done.16
  223.6 10.2 %collective-permute-done.26 = bf16[576,512]{1,0:T(8,128)(2,1)S(1)} collective-permute-done((bf16[576,512]{1,0:T(8,128)(2,1)S(1)}, bf16[576,512]{1,0:T(8,128)(2,1)S(1)}, u32[]{:S(2)}, u32[]{:S(2)}) %collective-permute-start.26) | collective-permute-done | bytes 589856 | tf_op jit(solution)/shard_map/ppermute | solution.py:225
  235.8 6.0 %collective-permute-done.27 = bf16[288,512]{1,0:T(8,128)(2,1)S(1)} collective-permute-done((bf16[288,512]{1,0:T(8,128)(2,1)S(1)}, bf16[288,512]{1,0:T(8,128)(2,1)S(1)}, u32[]{:S(2)}, u32[]{:S(2)}) %collective-permute-start.27) | collective-permute-done | bytes 294944 | tf_op jit(solution)/shard_map/ppermute | solution.py:225
  242.0 2.7 collective-permute-start.28
  245.0 6.3 %collective-permute-done.28 = bf16[144,512]{1,0:T(8,128)(2,1)S(1)} collective-permute-done((bf16[144,512]{1,0:T(8,128)(2,1)S(1)}, bf16[144,512]{1,0:T(8,128)(2,1)S(1)}, u32[]{:S(2)}, u32[]{:S(2)}) %collective-permute-start.28) | collective-permute-done | bytes 147488 | tf_op jit(solution)/shard_map/ppermute | solution.py:225
  254.4 5.2 %collective-permute-done.29 = bf16[144,512]{1,0:T(8,128)(2,1)S(1)} collective-permute-done((bf16[144,512]{1,0:T(8,128)(2,1)S(1)}, bf16[144,512]{1,0:T(8,128)(2,1)S(1)}, u32[]{:S(2)}, u32[]{:S(2)}) %collective-permute-start.29) | collective-permute-done | bytes 147488 | tf_op jit(solution)/shard_map/ppermute | solution.py:225
  260.2 6.4 %collective-permute-done.30 = bf16[288,512]{1,0:T(8,128)(2,1)S(1)} collective-permute-done((bf16[288,512]{1,0:T(8,128)(2,1)S(1)}, bf16[288,512]{1,0:T(8,128)(2,1)S(1)}, u32[]{:S(2)}, u32[]{:S(2)}) %collective-permute-start.30) | collective-permute-done | bytes 294944 | tf_op jit(solution)/shard_map/ppermute | solution.py:225
  266.7 2.7 collective-permute-start.31
  269.6 4.5 %collective-permute-done.20 = bf16[64,768]{1,0:T(8,128)(2,1)S(1)} collective-permute-done((bf16[64,768]{1,0:T(8,128)(2,1)S(1)}, bf16[64,768]{1,0:T(8,128)(2,1)S(1)}, u32[]{:S(2)}, u32[]{:S(2)}) %collective-permute-start.20) | collective-permute-done | bytes 98336 | tf_op jit(solution)/shard_map/ppermute | solution.py:225
  274.3 5.6 %collective-permute-done.31 = bf16[576,512]{1,0:T(8,128)(2,1)S(1)} collective-permute-done((bf16[576,512]{1,0:T(8,128)(2,1)S(1)}, bf16[576,512]{1,0:T(8,128)(2,1)S(1)}, u32[]{:S(2)}, u32[]{:S(2)}) %collective-permute-start.31) | collective-permute-done | bytes 589856 | tf_op jit(solution)/shard_map/ppermute | solution.py:225
  283.0 3.0 collective-permute-done.10
  (176 shorter events, 65.0 us)
Async XLA Ops:
  0.7 36.4 %collective-permute-start.1 = (bf16[16,64,512]{2,1,0:T(8,128)(2,1)}, bf16[16,64,512]{2,1,0:T(8,128)(2,1)}, u32[]{:S(2)}, u32[]{:S(2)}) collective-permute-start(bf16[16,64,512]{2,1,0:T(8,128)(2,1)} %x.1), channel_id=1, source_target_pairs={{2,0},{4,2},{6,4},{8,6},{10,8},{12,10},{14,12},{16,14},{18,16},{20... | collective-permute-start | bytes 3145736 | tf_op jit(solution)/shard_map/ppermute | solution.py:231
  2.1 35.0 %collective-permute-start = (bf16[16,64,512]{2,1,0:T(8,128)(2,1)}, bf16[16,64,512]{2,1,0:T(8,128)(2,1)}, u32[]{:S(2)}, u32[]{:S(2)}) collective-permute-start(bf16[16,64,512]{2,1,0:T(8,128)(2,1)} %x.1), channel_id=1, source_target_pairs={{0,2},{2,4},{4,6},{6,8},{8,10},{10,12},{12,14},{14,16},{16,18},{18... | collective-permute-start | bytes 3145736 | tf_op jit(solution)/shard_map/ppermute | solution.py:230
  7.5 21.4 %collective-permute-start.2 = (bf16[512,3,256]{0,2,1:T(8,128)(2,1)S(1)}, bf16[512,3,256]{0,2,1:T(8,128)(2,1)S(1)}, u32[]{:S(2)}, u32[]{:S(2)}) collective-permute-start(bf16[512,3,256]{0,2,1:T(8,128)(2,1)S(1)} %copy.24), channel_id=1, source_target_pairs={{0,1},{1,0},{2,3},{3,2},{4,5},{5,4},{6,7},{7,6},{8,9},{9,8},{10,11... | collective-permute-start | bytes 2359304 | tf_op jit(solution)/shard_map/ppermute | solution.py:225
  10.6 68.7 %collective-permute-start.4 = (bf16[512,1024]{1,0:T(8,128)(2,1)S(1)}, bf16[512,1024]{1,0:T(8,128)(2,1)S(1)}, u32[]{:S(2)}, u32[]{:S(2)}) collective-permute-start(bf16[512,1024]{1,0:T(8,128)(2,1)S(1)} %copy-done.11), channel_id=1, source_target_pairs={{0,1},{1,0},{2,3},{3,2},{4,5},{5,4},{6,7},{7,6},{8,9},{9,8},{10,11... | collective-permute-start | bytes 3145736 | tf_op jit(solution)/shard_map/ppermute | solution.py:225
  10.7 68.6 %collective-permute-start.5 = (bf16[1024,512]{1,0:T(8,128)(2,1)}, bf16[1024,512]{1,0:T(8,128)(2,1)}, u32[]{:S(2)}, u32[]{:S(2)}) collective-permute-start(bf16[1024,512]{1,0:T(8,128)(2,1)} %wd0.1), channel_id=1, source_target_pairs={{0,1},{1,0},{2,3},{3,2},{4,5},{5,4},{6,7},{7,6},{8,9},{9,8},{10,11... | collective-permute-start | bytes 3145736 | tf_op jit(solution)/shard_map/ppermute | solution.py:225
  29.9 49.4 %collective-permute-start.3 = (bf16[256,512]{1,0:T(8,128)(2,1)S(1)}, bf16[256,512]{1,0:T(8,128)(2,1)S(1)}, u32[]{:S(2)}, u32[]{:S(2)}) collective-permute-start(bf16[256,512]{1,0:T(8,128)(2,1)S(1)} %copy-done.22), channel_id=1, source_target_pairs={{0,1},{1,0},{2,3},{3,2},{4,5},{5,4},{6,7},{7,6},{8,9},{9,8},{10,11... | collective-permute-start | bytes 786440 | tf_op jit(solution)/shard_map/ppermute | solution.py:225
  108.9 12.5 %collective-permute-start.7 = (bf16[16,64,512]{2,1,0:T(8,128)(2,1)S(1)}, bf16[16,64,512]{2,1,0:T(8,128)(2,1)S(1)}, u32[]{:S(2)}, u32[]{:S(2)}) collective-permute-start(bf16[16,64,512]{2,1,0:T(8,128)(2,1)S(1)} %bitcast.64), channel_id=1, source_target_pairs={{2,0},{4,2},{6,4},{8,6},{10,8},{12,10},{14,12},{16,14},{18,16},{20... | collective-permute-start | bytes 3145736 | tf_op jit(solution)/shard_map/ppermute | solution.py:231
  110.4 11.0 %collective-permute-start.6 = (bf16[16,64,512]{2,1,0:T(8,128)(2,1)S(1)}, bf16[16,64,512]{2,1,0:T(8,128)(2,1)S(1)}, u32[]{:S(2)}, u32[]{:S(2)}) collective-permute-start(bf16[16,64,512]{2,1,0:T(8,128)(2,1)S(1)} %bitcast.65), channel_id=1, source_target_pairs={{0,2},{2,4},{4,6},{6,8},{8,10},{10,12},{12,14},{14,16},{16,18},{18... | collective-permute-start | bytes 3145736 | tf_op jit(solution)/shard_map/ppermute | solution.py:230
  117.5 55.3 %collective-permute-start.24 = (bf16[1152,512]{1,0:T(8,128)(2,1)}, bf16[1152,512]{1,0:T(8,128)(2,1)}, u32[]{:S(2)}, u32[]{:S(2)}) collective-permute-start(bf16[1152,512]{1,0:T(8,128)(2,1)} %broadcast_select_fusion.2), channel_id=1, source_target_pairs={{0,2},{2,0},{4,6},{6,4},{8,10},{10,8},{12,14},{14,12},{16,18},{18,... | collective-permute-start | bytes 3538952 | tf_op jit(solution)/shard_map/ppermute | solution.py:225
  121.4 95.2 %collective-permute-start.23 = (bf16[1152,512]{1,0:T(8,128)(2,1)}, bf16[1152,512]{1,0:T(8,128)(2,1)}, u32[]{:S(2)}, u32[]{:S(2)}) collective-permute-start(bf16[1152,512]{1,0:T(8,128)(2,1)} %broadcast_select_fusion.3), channel_id=1, source_target_pairs={{0,2},{2,0},{4,6},{6,4},{8,10},{10,8},{12,14},{14,12},{16,18},{18,... | collective-permute-start | bytes 3538952 | tf_op jit(solution)/shard_map/ppermute | solution.py:225
  158.9 18.3 %collective-permute-start.14 = (bf16[256,768]{1,0:T(8,128)(2,1)S(1)}, bf16[256,768]{1,0:T(8,128)(2,1)S(1)}, u32[]{:S(2)}, u32[]{:S(2)}) collective-permute-start(bf16[256,768]{1,0:T(8,128)(2,1)S(1)} %get-tuple-element.63), channel_id=1, source_target_pairs={{0,2},{2,0},{4,6},{6,4},{8,10},{10,8},{12,14},{14,12},{16,18},{18,... | collective-permute-start | bytes 1179656 | tf_op jit(solution)/shard_map/ppermute | solution.py:225
  175.7 40.9 %collective-permute-start.25 = (bf16[1152,512]{1,0:T(8,128)(2,1)}, bf16[1152,512]{1,0:T(8,128)(2,1)}, u32[]{:S(2)}, u32[]{:S(2)}) collective-permute-start(bf16[1152,512]{1,0:T(8,128)(2,1)} %add_convert_fusion.1), channel_id=1, source_target_pairs={{0,1},{1,0},{2,3},{3,2},{4,5},{5,4},{6,7},{7,6},{8,9},{9,8},{10,11... | collective-permute-start | bytes 3538952 | tf_op jit(solution)/shard_map/ppermute | solution.py:225
  178.1 34.4 %collective-permute-start.15 = (bf16[256,768]{1,0:T(8,128)(2,1)}, bf16[256,768]{1,0:T(8,128)(2,1)}, u32[]{:S(2)}, u32[]{:S(2)}) collective-permute-start(bf16[256,768]{1,0:T(8,128)(2,1)} %fusion.25), channel_id=1, source_target_pairs={{0,1},{1,0},{2,3},{3,2},{4,5},{5,4},{6,7},{7,6},{8,9},{9,8},{10,11... | collective-permute-start | bytes 1179656 | tf_op jit(solution)/shard_map/ppermute | solution.py:225
  213.8 8.1 %collective-permute-start.16 = (bf16[128,768]{1,0:T(8,128)(2,1)S(1)}, bf16[128,768]{1,0:T(8,128)(2,1)S(1)}, u32[]{:S(2)}, u32[]{:S(2)}) collective-permute-start(bf16[128,768]{1,0:T(8,128)(2,1)S(1)} %broadcast_select_fusion.14), channel_id=1, source_target_pairs={{0,4},{2,6},{4,0},{6,2},{8,12},{10,14},{12,8},{14,10},{16,20},{18,... | collective-permute-start | bytes 589832 | tf_op jit(solution)/shard_map/ppermute | solution.py:225
  218.9 14.9 %collective-permute-start.26 = (bf16[576,512]{1,0:T(8,128)(2,1)S(1)}, bf16[576,512]{1,0:T(8,128)(2,1)S(1)}, u32[]{:S(2)}, u32[]{:S(2)}) collective-permute-start(bf16[576,512]{1,0:T(8,128)(2,1)S(1)} %broadcast_select_fusion.6), channel_id=1, source_target_pairs={{0,4},{2,6},{4,0},{6,2},{8,12},{10,14},{12,8},{14,10},{16,20},{18,... | collective-permute-start | bytes 1769480 | tf_op jit(solution)/shard_map/ppermute | solution.py:225
  222.0 13.8 %collective-permute-start.17 = (bf16[64,768]{1,0:T(8,128)(2,1)S(1)}, bf16[64,768]{1,0:T(8,128)(2,1)S(1)}, u32[]{:S(2)}, u32[]{:S(2)}) collective-permute-start(bf16[64,768]{1,0:T(8,128)(2,1)S(1)} %broadcast_select_fusion.20), channel_id=1, source_target_pairs={{0,8},{2,10},{4,12},{6,14},{8,0},{10,2},{12,4},{14,6},{16,24},{18,... | collective-permute-start | bytes 294920 | tf_op jit(solution)/shard_map/ppermute | solution.py:225
  242.0 9.3 %collective-permute-start.28 = (bf16[144,512]{1,0:T(8,128)(2,1)S(1)}, bf16[144,512]{1,0:T(8,128)(2,1)S(1)}, u32[]{:S(2)}, u32[]{:S(2)}) collective-permute-start(bf16[144,512]{1,0:T(8,128)(2,1)S(1)} %broadcast_select_fusion.17), channel_id=1, source_target_pairs={{0,16},{2,18},{4,20},{6,22},{8,24},{10,26},{12,28},{14,30},{16,0},... | collective-permute-start | bytes 442376 | tf_op jit(solution)/shard_map/ppermute | solution.py:225
  251.4 8.3 %collective-permute-start.29 = (bf16[144,512]{1,0:T(8,128)(2,1)S(1)}, bf16[144,512]{1,0:T(8,128)(2,1)S(1)}, u32[]{:S(2)}, u32[]{:S(2)}) collective-permute-start(bf16[144,512]{1,0:T(8,128)(2,1)S(1)} %add_convert_fusion.7), channel_id=1, source_target_pairs={{0,16},{2,18},{4,20},{6,22},{8,24},{10,26},{12,28},{14,30},{16,0},... | collective-permute-start | bytes 442376 | tf_op jit(solution)/shard_map/ppermute | solution.py:225
  259.9 9.6 %collective-permute-start.8 = (f32[4,512]{1,0:T(4,128)S(1)}, f32[4,512]{1,0:T(4,128)S(1)}, u32[]{:S(2)}, u32[]{:S(2)}) collective-permute-start(f32[4,512]{1,0:T(4,128)S(1)} %pad_maximum_fusion.13), channel_id=1, source_target_pairs={{0,2},{2,0},{4,6},{6,4},{8,10},{10,8},{12,14},{14,12},{16,18},{18,... | collective-permute-start | bytes 24584 | tf_op jit(solution)/shard_map/ppermute | solution.py:225
  266.7 13.1 %collective-permute-start.31 = (bf16[576,512]{1,0:T(8,128)(2,1)S(1)}, bf16[576,512]{1,0:T(8,128)(2,1)S(1)}, u32[]{:S(2)}, u32[]{:S(2)}) collective-permute-start(bf16[576,512]{1,0:T(8,128)(2,1)S(1)} %pad_maximum_fusion.8), channel_id=1, source_target_pairs={{0,4},{2,6},{4,0},{6,2},{8,12},{10,14},{12,8},{14,10},{16,20},{18,... | collective-permute-start | bytes 1769480 | tf_op jit(solution)/shard_map/ppermute | solution.py:225
  269.5 12.7 %collective-permute-start.9 = (f32[4,512]{1,0:T(4,128)S(1)}, f32[4,512]{1,0:T(4,128)S(1)}, u32[]{:S(2)}, u32[]{:S(2)}) collective-permute-start(f32[4,512]{1,0:T(4,128)S(1)} %fusion.29), channel_id=1, source_target_pairs={{0,4},{2,6},{4,0},{6,2},{8,12},{10,14},{12,8},{14,10},{16,20},{18,... | collective-permute-start | bytes 24584 | tf_op jit(solution)/shard_map/ppermute | solution.py:225
  274.2 7.9 %collective-permute-start.21 = (bf16[128,768]{1,0:T(8,128)(2,1)S(1)}, bf16[128,768]{1,0:T(8,128)(2,1)S(1)}, u32[]{:S(2)}, u32[]{:S(2)}) collective-permute-start(bf16[128,768]{1,0:T(8,128)(2,1)S(1)} %pad_maximum_fusion.11), channel_id=1, source_target_pairs={{0,4},{2,6},{4,0},{6,2},{8,12},{10,14},{12,8},{14,10},{16,20},{18,... | collective-permute-start | bytes 589832 | tf_op jit(solution)/shard_map/ppermute | solution.py:225
  281.3 15.9 %collective-permute-start.32 = (bf16[1152,512]{1,0:T(8,128)(2,1)}, bf16[1152,512]{1,0:T(8,128)(2,1)}, u32[]{:S(2)}, u32[]{:S(2)}) collective-permute-start(bf16[1152,512]{1,0:T(8,128)(2,1)} %pad_maximum_fusion.6), channel_id=1, source_target_pairs={{0,2},{2,0},{4,6},{6,4},{8,10},{10,8},{12,14},{14,12},{16,18},{18,... | collective-permute-start | bytes 3538952 | tf_op jit(solution)/shard_map/ppermute | solution.py:225
  282.2 12.6 %collective-permute-start.22 = (bf16[256,768]{1,0:T(8,128)(2,1)S(1)}, bf16[256,768]{1,0:T(8,128)(2,1)S(1)}, u32[]{:S(2)}, u32[]{:S(2)}) collective-permute-start(bf16[256,768]{1,0:T(8,128)(2,1)S(1)} %pad_maximum_fusion.9), channel_id=1, source_target_pairs={{0,2},{2,0},{4,6},{6,4},{8,10},{10,8},{12,14},{14,12},{16,18},{18,... | collective-permute-start | bytes 1179656 | tf_op jit(solution)/shard_map/ppermute | solution.py:225
  (42 other events, 350.2 us)

commit v3 on v1

v3 whole, which is shorter than its diff:
```python
import functools

import jax
import jax.numpy as jnp
import numpy as np
from jax import lax
from jax.experimental import pallas as pl
from jax.experimental.pallas import tpu as pltpu
from jax.sharding import PartitionSpec as P

HEAD_DIM = 64
HEADS_PER_GROUP = 4
GROUP_COLS = HEAD_DIM * HEADS_PER_GROUP
EPS = 1e-05
SCALE = HEAD_DIM ** (-0.5)
F32 = jnp.float32
BF16 = jnp.bfloat16
NEG = -1e30
CHUNK = 256


def dot_nn(a, b):
    return lax.dot_general(a, b, (((1,), (0,)), ((), ())), preferred_element_type=F32)


def dot_nt(a, b):
    return lax.dot_general(a, b, (((1,), (1,)), ((), ())), preferred_element_type=F32)


def dot_tn(a, b):
    return lax.dot_general(a, b, (((0,), (0,)), ((), ())), preferred_element_type=F32)


def norm_parts(z):
    mean = jnp.mean(z, axis=-1, keepdims=True)
    centred = z - mean
    var = jnp.mean(centred * centred, axis=-1, keepdims=True)
    rstd = lax.rsqrt(var + EPS)
    return centred * rstd, rstd


def norm_back(grad, xhat, rstd, gain):
    gg = grad * gain
    m1 = jnp.mean(gg, axis=-1, keepdims=True)
    m2 = jnp.mean(gg * xhat, axis=-1, keepdims=True)
    return rstd * (gg - m1 - xhat * m2)


def lane_head(rows, dtype):
    lane = lax.broadcasted_iota(jnp.int32, (rows, GROUP_COLS), 1)
    return [
        ((lane >= h * HEAD_DIM) & (lane < (h + 1) * HEAD_DIM)).astype(F32).astype(dtype)
        for h in range(HEADS_PER_GROUP)
    ]


def block_diag(rows, masks):
    return jnp.concatenate([rows * m for m in masks], axis=0)


def pick_heads(full, masks, rows):
    out = full[0:rows] * masks[0]
    for h in range(1, HEADS_PER_GROUP):
        out = out + full[h * rows : (h + 1) * rows] * masks[h]
    return out


def rows_at(index, size):
    return pl.ds(pl.multiple_of(index * size, size), size)


def each(count, body, unroll=1):
    lax.fori_loop(0, count, lambda i, carry: (body(i), carry)[1], 0, unroll=unroll)


def attn_fwd_kernel(idc, idr, xp, xo, xn, w0, w1, gain, shift, *rest):
    qkv_ref, att_ref = rest[-2:]
    feats, samp, width = xo.shape
    rows = feats * samp
    x = jnp.concatenate(
        [xp[...].reshape(rows, width), xo[...].reshape(rows, width), xn[...].reshape(rows, width)],
        axis=0,
    ).astype(F32)
    xhat, _ = norm_parts(x)
    normed = (xhat * gain[...] + shift[...]).astype(BF16)
    for hg, w in enumerate((w0, w1)):
        qkv = dot_nn(normed, w[...]).astype(BF16)
        qkv_ref[hg] = qkv.reshape(3, rows, 3 * GROUP_COLS)
    allowed = idc[...] == idr[1:2, :]
    m16 = lane_head(1, BF16)
    m32 = lane_head(1, F32)

    def column(f):
        sl = rows_at(f, samp)
        for hg in range(2):
            q = qkv_ref[hg, 1, sl, 0:GROUP_COLS]
            k = jnp.concatenate(
                [qkv_ref[hg, w, sl, GROUP_COLS : 2 * GROUP_COLS] for w in range(3)], axis=0
            )
            v = jnp.concatenate(
                [qkv_ref[hg, w, sl, 2 * GROUP_COLS : 3 * GROUP_COLS] for w in range(3)], axis=0
            )
            s = dot_nt(k, block_diag(q, m16)) * SCALE
            s = jnp.where(allowed, s, NEG)
            top = jnp.max(s, axis=0, keepdims=True)
            e = jnp.exp(s - top)
            total = jnp.sum(e, axis=0, keepdims=True)
            p = (e * (1.0 / total)).astype(BF16)
            o = pick_heads(dot_tn(p, v), m32, samp)
            att_ref[f, :, hg * GROUP_COLS : (hg + 1) * GROUP_COLS] = o.astype(BF16)

    each(feats, column, 2)


def phi_parts(u):
    e = jnp.exp(-0.5 * (u * u))
    t = 1.0 / (1.0 + (0.3275911 * 0.7071067811865476) * jnp.abs(u))
    poly = t * (
        0.127414796
        + t * (-0.142248368 + t * (0.7107068705 + t * (-0.7265760135 + t * 0.5307027145)))
    )
    tail = poly * e
    cdf = jnp.where(u < 0, tail, 1.0 - tail)
    return cdf, u * (e * 0.3989422804014327)


def chain_kernel(others, inpack, ordered, *refs):
    table, x, att, cot, gain, shift, up_own, down_own, out_own = refs[:9]
    refs = refs[9:]
    packs, refs = refs[: 2 * others], refs[2 * others :]
    if inpack:
        extra = packs
    else:
        extra, refs = refs[: 2 * others], refs[2 * others :]
    count = 2 if ordered else 3
    out_ref, hgrad_ref, dat_ref, g2_ref, s2_ref = refs[:5]
    packed, refs = refs[5 : 5 + count], refs[5 + count :]
    (wo, upb, downb, hidden, normed, mlp, dn2, act, pre, res, gd, gu, go) = refs
    tokens, width = x.shape
    slot = upb.shape[1]
    narrow_rows = out_own.shape[0]
    half_rows = narrow_rows // 2
    chunks = tokens // CHUNK
    step = pl.program_id(0)
    core = table[0]

    def bases(unit):
        for j in range(1, others + 1):
            yield 2 * j - 2, 2 * j + core
            yield 2 * j - 1, 2 * j + 1 - core

    @pl.when(step == 0)
    def _():
        wo[:narrow_rows] = out_own[...]
        for i, base in bases(half_rows):
            wo[rows_at(base, half_rows)] = packs[i][2 * slot : 2 * slot + half_rows] if inpack else packs[i][slot : slot + half_rows]
        g2_ref[...] = jnp.zeros_like(g2_ref)
        s2_ref[...] = jnp.zeros_like(s2_ref)

        def start(i):
            sl = rows_at(i, CHUNK)
            h = x[sl].astype(F32) + dot_nn(att[sl], wo[...])
            hidden[sl] = h
            xhat, _ = norm_parts(h)
            normed[sl] = (xhat * gain[...] + shift[...]).astype(BF16)
            mlp[sl] = jnp.zeros((CHUNK, width), F32)
            dn2[sl] = jnp.zeros((CHUNK, width), F32)

        each(chunks, start)

    for i in range(2 * others + 2):

        @pl.when(step == i)
        def _(i=i):
            if i < 2:
                upb[...] = up_own[:, i * slot : (i + 1) * slot]
                downb[...] = down_own[i * slot : (i + 1) * slot]
            elif inpack:
                upb[...] = packs[i - 2][:slot]
                downb[...] = packs[i - 2][slot : 2 * slot]
            else:
                upb[...] = extra[i - 2][...]
                downb[...] = packs[i - 2][:slot]

    def tokens_of(i):
        sl = rows_at(i, CHUNK)
        u = dot_nn(normed[sl], upb[...])
        cdf, upd = phi_parts(u)
        a = (u * cdf).astype(BF16)
        act[sl] = a
        p = (dot_nt(cot[sl], downb[...]) * (cdf + upd)).astype(BF16)
        pre[sl] = p
        mlp[sl] += dot_nn(a, downb[...])
        dn2[sl] += dot_nt(p, upb[...])

    each(chunks, tokens_of)
    swapped = jnp.where(step % 2 == 0, core, 1 - core)
    base = jnp.where(step < 2, step, step - step % 2 + swapped)
    at = rows_at(base, slot)
    gd[at] = dot_tn(act[...], cot[...]).astype(BF16)
    gu[at] = dot_tn(pre[...], normed[...]).astype(BF16)

    @pl.when(step == 2 * others + 1)
    def _():
        def finish(i):
            sl = rows_at(i, CHUNK)
            h = hidden[sl]
            out_ref[sl] = (h + mlp[sl]).astype(BF16)
            xhat, rstd = norm_parts(h)
            d = dn2[sl]
            g2_ref[...] += jnp.sum(d * xhat, axis=0, keepdims=True)
            s2_ref[...] += jnp.sum(d, axis=0, keepdims=True)
            hgrad = cot[sl].astype(F32) + norm_back(d, xhat, rstd, gain[...])
            hgrad_ref[sl] = hgrad
            r = hgrad.astype(BF16)
            res[sl] = r
            dat_ref[sl] = dot_nt(r, wo[...]).astype(BF16)

        each(chunks, finish)
        go[...] = dot_tn(att[...], res[...]).astype(BF16)
        if ordered:
            blocks = (table.shape[0] - 1) // 2
            n_ff = gd.shape[0] // (2 * blocks)
            n_out = go.shape[0] // (2 * blocks)
            size = 2 * n_ff + n_out
            for side in range(2):
                for b in range(blocks):
                    src = table[1 + side * blocks + b]
                    ref = packed[side]
                    ref[b * size : b * size + n_ff] = gd[rows_at(src, n_ff)]
                    ref[b * size + n_ff : b * size + 2 * n_ff] = gu[rows_at(src, n_ff)]
                    ref[b * size + 2 * n_ff : (b + 1) * size] = go[rows_at(src, n_out)]
        else:
            packed[0][...] = gd[...]
            packed[1][...] = gu[...]
            packed[2][...] = go[...]


def attn_bwd_kernel(idc, idr, qkv_ref, dp_ref, do_ref, dn_ref, *rest):
    dqkv = rest[-1]
    feats, samp, width = do_ref.shape
    m16 = lane_head(1, BF16)
    m32 = lane_head(1, F32)
    spans = ((0, 2), (0, 3), (1, 3))
    masks = [idc[a * samp : b * samp, :] == idr[g : g + 1, :] for g, (a, b) in enumerate(spans)]
    grads = (dp_ref, do_ref, dn_ref)

    def column(f):
        sl = rows_at(f, samp)
        for hg in range(2):
            cols = slice(hg * GROUP_COLS, (hg + 1) * GROUP_COLS)
            k = jnp.concatenate(
                [qkv_ref[hg, w, sl, GROUP_COLS : 2 * GROUP_COLS] for w in range(3)], axis=0
            )
            v = jnp.concatenate(
                [qkv_ref[hg, w, sl, 2 * GROUP_COLS : 3 * GROUP_COLS] for w in range(3)], axis=0
            )
            dk = jnp.zeros((samp, GROUP_COLS), F32)
            dv = jnp.zeros((samp, GROUP_COLS), F32)
            for g, (a, b) in enumerate(spans):
                ks = k[a * samp : b * samp]
                vs = v[a * samp : b * samp]
                qbd = block_diag(qkv_ref[hg, g, sl, 0:GROUP_COLS], m16)
                dbd = block_diag(grads[g][f, :, cols], m16)
                s = dot_nt(ks, qbd) * SCALE
                s = jnp.where(masks[g], s, NEG)
                top = jnp.max(s, axis=0, keepdims=True)
                e = jnp.exp(s - top)
                total = jnp.sum(e, axis=0, keepdims=True)
                p = e * (1.0 / total)
                dp = dot_nt(vs, dbd)
                pd = p * dp
                delta = jnp.sum(pd, axis=0, keepdims=True)
                ds = (pd - p * delta).astype(BF16)
                own = slice((1 - a) * samp, (2 - a) * samp)
                dk = dk + dot_nn(ds[own], qbd)
                dv = dv + dot_nn(p[own].astype(BF16), dbd)
                if g == 1:
                    dq = pick_heads(dot_tn(ds, ks), m32, samp)
            dqkv[hg, sl, 0:GROUP_COLS] = (dq * SCALE).astype(BF16)
            dqkv[hg, sl, GROUP_COLS : 2 * GROUP_COLS] = (dk * SCALE).astype(BF16)
            dqkv[hg, sl, 2 * GROUP_COLS : 3 * GROUP_COLS] = dv.astype(BF16)

    each(feats, column, 2)


def qkv_grad_kernel(ordered, table, x, dqkv, gain, shift, *refs):
    normed, gq = refs[-2:]
    outs = refs[:-2]
    tokens, width = x.shape

    def start(i):
        sl = rows_at(i, CHUNK)
        xhat, _ = norm_parts(x[sl].astype(F32))
        normed[sl] = (xhat * gain[...] + shift[...]).astype(BF16)

    each(tokens // CHUNK, start)
    cols = dqkv.shape[2]
    for hg in range(2):
        gq[hg * cols : (hg + 1) * cols] = dot_tn(dqkv[hg], normed[...]).astype(BF16)
    if ordered:
        blocks = (table.shape[0] - 1) // 2
        size = gq.shape[0] // (2 * blocks)
        for side in range(2):
            for b in range(blocks):
                outs[side][b * size : (b + 1) * size] = gq[rows_at(table[1 + side * blocks + b], size)]
    else:
        outs[0][...] = gq[...]


def input_grad_kernel(x, hgrad, dqkv, w0, w1, gain, igrad_ref, g1_ref, s1_ref):
    xhat, rstd = norm_parts(x[...].astype(F32))
    dn1 = dot_nt(dqkv[0], w0[...]) + dot_nt(dqkv[1], w1[...])

    @pl.when(pl.program_id(0) == 0)
    def _():
        g1_ref[...] = jnp.zeros_like(g1_ref)
        s1_ref[...] = jnp.zeros_like(s1_ref)

    g1_ref[...] += jnp.sum(dn1 * xhat, axis=0, keepdims=True)
    s1_ref[...] += jnp.sum(dn1, axis=0, keepdims=True)
    igrad_ref[...] = hgrad[...] + norm_back(dn1, xhat, rstd, gain[...])


def ffn_out_kernel(n_ff, n_out, table, mine, got, up_ref, down_ref, out_ref, turned):
    size = 2 * n_ff + n_out
    blocks = mine.shape[0] // size
    for side, ref in enumerate((mine, got)):
        for b in range(blocks):
            to = table[side * blocks + b]
            down_ref[rows_at(to, n_ff)] = ref[b * size : b * size + n_ff].astype(F32)
            turned[rows_at(to, n_ff)] = ref[b * size + n_ff : b * size + 2 * n_ff].astype(F32)
            out_ref[rows_at(to, n_out)] = ref[b * size + 2 * n_ff : (b + 1) * size].astype(F32)
    up_ref[...] = turned[...].T


def qkv_out_kernel(table, mine, got, out_ref, turned):
    blocks = table.shape[0] // 2
    size = mine.shape[0] // blocks
    for side, ref in enumerate((mine, got)):
        for b in range(blocks):
            turned[rows_at(table[side * blocks + b], size)] = ref[b * size : (b + 1) * size].astype(F32)
    out_ref[...] = turned[...].T


def swap(x, axis, bit):
    count = lax.axis_size(axis)
    return lax.ppermute(x, axis, [(i, i ^ bit) for i in range(count)])


def halo(x, axis):
    count = lax.axis_size(axis)
    prev = lax.ppermute(x, axis, [(i, i + 1) for i in range(count - 1)])
    nxt = lax.ppermute(x, axis, [(i + 1, i) for i in range(count - 1)])
    return prev, nxt


def gather_pieces(x, axis):
    pieces = [x]
    bit = 1
    while bit < lax.axis_size(axis):
        pieces = pieces + [swap(p, axis, bit) for p in pieces]
        bit *= 2
    return pieces


def tied(*arrays):
    return lax.optimization_barrier(arrays)


class Plan:

    def __init__(self, wide, narrow):
        self.wide, self.narrow = wide, narrow
        nb = [("narrow", 1 << i) for i in range(narrow.bit_length() - 1)][::-1]
        wb = [("wide", 1 << i) for i in range(1, wide.bit_length() - 1)]
        first = nb + wb
        second = wb[1:2] + nb + wb[:1] + wb[2:]
        self.orders = (first, second)
        self.steps = len(first)
        self.blocks = 1 << self.steps
        self.back = [[s for s in o if s[0] == "wide"][::-1] for o in self.orders]
        self.me = lax.axis_index("wide")
        self.core = self.me % 2

    def rel(self, order):
        j = np.zeros(self.blocks, np.int32)
        r = np.zeros(self.blocks, np.int32)
        for s, (axis, bit) in enumerate(order):
            has = (np.arange(self.blocks) >> (self.steps - 1 - s)) & 1
            if axis == "narrow":
                j += has * bit
            else:
                r += has * bit
        return j, r

    def by_core(self, a, b):
        return jnp.where(self.core == 0, jnp.asarray(a, jnp.int32), jnp.asarray(b, jnp.int32))

    def sources(self):
        (j0, r0), (j1, r1) = (self.rel(o) for o in self.orders)
        high = self.me - self.core
        n0, n1 = j0 * self.wide, j1 * self.wide
        mine = self.by_core(n0, n1) + (self.by_core(r0, r1) ^ high) + self.core
        send = self.by_core(n1, n0) + (self.by_core(r1, r0) ^ high) + 1 - self.core
        return jnp.concatenate([self.core[None], mine, send]).astype(jnp.int32)

    def targets(self):
        rels = []
        for o in self.orders:
            j, r = self.rel(o)
            rels.append(r[j == 0])
        high = self.me - self.core
        mine = (self.by_core(rels[0], rels[1]) ^ high) + self.core
        got = (self.by_core(rels[1], rels[0]) ^ high) + 1 - self.core
        return jnp.concatenate([mine, got]).astype(jnp.int32)

    def mixed(self, x, steps):
        pairs = []
        for w in range(self.wide):
            axis, bit = steps[w % 2]
            for n in range(self.narrow):
                to = (w, n ^ bit) if axis == "narrow" else (w ^ bit, n)
                pairs.append((w * self.narrow + n, to[0] * self.narrow + to[1]))
        return lax.ppermute(x, ("wide", "narrow"), pairs)


class Reduction:

    def __init__(self, plan, mine, send):
        self.plan, self.parts, self.operand, self.at = plan, [mine], send, 0
        self.rows = mine.shape[0]

    def total(self, low, high):
        out = self.parts[0][low:high].astype(F32)
        for p in self.parts[1:]:
            out = out + p[low:high].astype(F32)
        return out.astype(BF16)

    def advance(self):
        plan, at = self.plan, self.at
        back = len(plan.back[0])
        if at == 0:
            got = swap(self.operand, "wide", 1)
        elif at <= plan.steps:
            got = plan.mixed(self.operand, [o[at - 1] for o in plan.orders])
        elif at <= plan.steps + back:
            got = plan.mixed(self.operand, [o[at - plan.steps - 1] for o in plan.back])
        else:
            got = swap(self.operand, "wide", 1)
        self.at = at + 1
        if at <= plan.steps:
            self.parts.append(got)
            if at == plan.steps:
                self.operand = self.total(0, self.rows >> at)
            else:
                self.operand = self.total(self.rows >> (at + 1), self.rows >> at)
        elif at <= plan.steps + back:
            self.operand = jnp.concatenate([self.operand, got], axis=0)
        else:
            self.result = (self.operand, got)

    @property
    def left(self):
        return self.plan.steps + len(self.plan.back[0]) + 2 - self.at


def lockstep(*chains):
    live = [c for c in chains if c.left > 0]
    if len(live) > 1:
        for c, o in zip(live, tied(*[c.operand for c in live])):
            c.operand = o
    for c in live:
        c.advance()


class SmallSum:
    def __init__(self, value):
        self.operand = value
        self.bits = [(a, 1 << i) for a in ("wide", "narrow") for i in range(lax.axis_size(a).bit_length() - 1)]

    def advance(self):
        self.operand = self.operand + swap(self.operand, *self.bits.pop(0))

    @property
    def left(self):
        return len(self.bits)


def local(
    inputs, segment_ids, norm1_gain, norm1_shift, w_qkv, w_out,
    norm2_gain, norm2_shift, w_up, w_down, cotangent,
):
    feats, samp, width = inputs.shape
    tokens = feats * samp
    narrow = lax.axis_size("narrow")
    wide = lax.axis_size("wide")
    plan = Plan(wide, narrow)
    core = plan.core
    part = feats // 2
    group = max(g for g in (1, 2, 4) if part % g == 0)
    steps = part // group
    rows = group * samp
    head_cols = w_qkv.shape[2]
    own_ff = w_up.shape[1]
    slot = own_ff // 2
    ff = own_ff * narrow
    inpack = slot == 512
    n_ff, n_out, n_qkv = own_ff // wide, w_out.shape[0] // wide, 3 * head_cols // wide
    ordered = narrow == 2 and n_ff % 16 == 0 and n_out % 16 == 0 and n_qkv % 16 == 0
    blocks = plan.blocks

    def core_half(a, axis):
        size = a.shape[axis] // 2
        return lax.dynamic_slice_in_dim(a, core * size, size, axis)

    halves_in = [inputs[:part], inputs[part:]]
    qkv_mine = gather_pieces(core_half(w_qkv.reshape(width, 3 * head_cols), 0), "narrow")[1:]
    prev0, next0 = halo(halves_in[0], "wide")
    up_half = core_half(w_up, 1)
    small = jnp.concatenate(
        [up_half.reshape(-1, 512), core_half(w_down, 0), core_half(w_out, 0)], axis=0
    )
    held = tied(small, *qkv_mine)
    small, qkv_mine = held[0], list(held[1:])
    pack_mine = gather_pieces(small, "narrow")[1:]
    qkv_got = [swap(p, "wide", 1) for p in qkv_mine]
    late, prev0, next0 = tied(halves_in[1], prev0, next0)
    prev1, next1 = halo(late, "wide")

    def whole_of(mine, got):
        first = jnp.where(core == 0, mine, got)
        second = jnp.where(core == 0, got, mine)
        return jnp.concatenate([first, second], axis=0)

    pieces = [w_qkv] + [
        whole_of(m, g).reshape(width, 3, head_cols) for m, g in zip(qkv_mine, qkv_got)
    ]
    cut = narrow // 2
    w0, w1 = (
        (p[0] if len(p) == 1 else jnp.concatenate(p, axis=2)).reshape(width, 3 * GROUP_COLS)
        for p in (pieces[:cut], pieces[cut:])
    )

    id_rim = jnp.full((samp,), -1, jnp.int32)
    padded_ids = jnp.concatenate([id_rim, segment_ids, id_rim])
    window_ids = lax.dynamic_slice_in_dim(padded_ids, plan.me * samp, 3 * samp, 0)
    id_col = window_ids[:, None]
    id_row = jnp.tile(window_ids.reshape(3, samp), (1, HEADS_PER_GROUP))
    gain1, shift1 = norm1_gain[None, :], norm1_shift[None, :]
    gain2, shift2 = norm2_gain[None, :], norm2_shift[None, :]
    sources, targets = plan.sources(), plan.targets()

    def whole(a):
        return pl.BlockSpec(a.shape, lambda i: (0,) * a.ndim, pipeline_mode=pl.Buffered(1))

    def cube(offset):
        return pl.BlockSpec((group, samp, width), lambda i: (i + offset, 0, 0))

    smem = pl.BlockSpec(memory_space=pltpu.SMEM)
    anywhere = pl.BlockSpec(memory_space=pl.ANY)
    line = pl.BlockSpec((1, width), lambda i: (0, 0))
    vec = jax.ShapeDtypeStruct((1, width), F32)

    def tok(dtype):
        return jax.ShapeDtypeStruct((tokens, width), dtype)

    def cost(flops, size):
        return pl.CostEstimate(flops=flops, bytes_accessed=size, transcendentals=0)

    def qkv_block(offset):
        return pl.BlockSpec((2, 3, rows, 3 * GROUP_COLS), lambda i: (0, 0, i + offset, 0))

    done = None
    for h, (before, after) in enumerate(((prev0, next0), (prev1, next1))):
        off = h * steps
        args = [id_col, id_row, before, inputs, after, w0, w1, gain1, shift1]
        specs = [whole(id_col), whole(id_row), cube(0), cube(off), cube(0)]
        specs += [whole(a) for a in (w0, w1, gain1, shift1)]
        alias = {}
        if done is not None:
            alias = {len(args): 0, len(args) + 1: 1}
            args += done
            specs += [anywhere, anywhere]
        done = pl.pallas_call(
            attn_fwd_kernel,
            grid=(steps,),
            in_specs=specs,
            out_specs=[qkv_block(off), cube(off)],
            out_shape=[
                jax.ShapeDtypeStruct((2, 3, tokens, 3 * GROUP_COLS), BF16),
                jax.ShapeDtypeStruct((feats, samp, width), BF16),
            ],
            input_output_aliases=alias,
            cost_estimate=cost(6 * 10**9 // 2, 12 << 20),
            name=f"attn_fwd_{h}",
        )(*args)
        if h == 0:
            pack_mine = list(tied(done[1], *pack_mine))[1:]
            pack_got = [swap(p, "wide", 1) for p in pack_mine]
    qkv, attended = done

    x_flat = inputs.reshape(tokens, width)
    cot_flat = cotangent.reshape(tokens, width)
    att_flat = attended.reshape(tokens, width)
    packs = [a for pair in zip(pack_mine, pack_got) for a in pair]
    args = [sources, x_flat, att_flat, cot_flat, gain2, shift2, w_up, w_down, w_out]
    if inpack:
        args += packs
    else:
        up_rows = width * slot // 512
        args += [p[up_rows:] for p in packs]
        args += [p[:up_rows].reshape(width, slot) for p in packs]
    if ordered:
        size = blocks * (2 * n_ff + n_out)
        sums = [(size, 512)] * 2
    else:
        sums = [(ff, width), (ff, width), (width, width)]
    outs = [tok(BF16), tok(F32), tok(BF16), vec, vec]
    outs += [jax.ShapeDtypeStruct(s, BF16) for s in sums]
    scratch = [
        ((width, width), BF16), ((width, slot), BF16), ((slot, width), BF16),
        ((tokens, width), F32), ((tokens, width), BF16), ((tokens, width), F32), ((tokens, width), F32),
        ((tokens, slot), BF16), ((tokens, slot), BF16), ((tokens, width), BF16),
        ((ff, width), BF16), ((ff, width), BF16), ((width, width), BF16),
    ]
    block_out, hidden_grad, dattended, gain2_grad, shift2_grad, *packed = pl.pallas_call(
        functools.partial(chain_kernel, narrow - 1, inpack, ordered),
        grid=(2 * narrow,),
        in_specs=[smem] + [whole(a) for a in args[1:]],
        out_specs=[whole(o) for o in outs],
        out_shape=outs,
        scratch_shapes=[pltpu.VMEM(*s) for s in scratch],
        cost_estimate=cost(15 * 10**9, 20 << 20),
        name="chain",
    )(*args)

    def arranged(natural):
        flat = natural.reshape(narrow * wide, natural.shape[2], 512)
        places = sources[1:].reshape(2, blocks)
        return [jnp.take(flat, places[s], axis=0).reshape(-1, 512) for s in range(2)]

    if not ordered:
        down, up, out = (p.reshape(narrow, wide, -1, 512) for p in packed)
        packed = arranged(jnp.concatenate([down, up, out], axis=2))
    big = Reduction(plan, packed[0], packed[1])

    datt = dattended.reshape(feats, samp, width)
    around = [halo(datt[:part], "wide")]
    lockstep(big)
    first, *around[0] = tied(datt[part:], *around[0])
    around.append(halo(first, "wide"))
    dqkv = None
    for h in range(2):
        off = h * steps
        before, after = around[h]
        before, after, big.operand = tied(before, after, big.operand)
        args = [id_col, id_row, qkv, before, datt, after]
        specs = [whole(id_col), whole(id_row), qkv_block(off), cube(0), cube(off), cube(0)]
        alias = {}
        if dqkv is not None:
            alias = {len(args): 0}
            args.append(dqkv)
            specs.append(anywhere)
        lockstep(big)
        dqkv = pl.pallas_call(
            attn_bwd_kernel,
            grid=(steps,),
            in_specs=specs,
            out_specs=pl.BlockSpec((2, rows, 3 * GROUP_COLS), lambda i, off=off: (0, i + off, 0)),
            out_shape=jax.ShapeDtypeStruct((2, tokens, 3 * GROUP_COLS), BF16),
            input_output_aliases=alias,
            cost_estimate=cost(10 * 10**9, 12 << 20),
            name=f"attn_bwd_{h}",
        )(*args)
    dqkv, big.operand = tied(dqkv, big.operand)
    lockstep(big)

    natural = (6 * GROUP_COLS, width)
    outs = [jax.ShapeDtypeStruct((blocks * n_qkv, 512), BF16)] * 2
    if not ordered:
        outs = [jax.ShapeDtypeStruct(natural, BF16)]
    args = [sources, x_flat, dqkv, gain1, shift1]
    packed = pl.pallas_call(
        functools.partial(qkv_grad_kernel, ordered),
        grid=(1,),
        in_specs=[smem] + [whole(a) for a in args[1:]],
        out_specs=[whole(o) for o in outs],
        out_shape=outs,
        scratch_shapes=[pltpu.VMEM((tokens, width), BF16), pltpu.VMEM(natural, BF16)],
        cost_estimate=cost(2 * 10**9, 6 << 20),
        name="qkv_grad",
    )(*args)
    if not ordered:
        turned = packed[0].reshape(2, 3, narrow // 2, head_cols, width).transpose(0, 2, 1, 3, 4)
        packed = arranged(turned.reshape(narrow, wide, n_qkv, width))
    last = Reduction(plan, packed[0], packed[1])

    flat = pl.BlockSpec((CHUNK, width), lambda i: (i, 0))
    dqkv, last.operand = tied(dqkv, last.operand)
    input_grad, gain1_grad, shift1_grad = pl.pallas_call(
        input_grad_kernel,
        grid=(tokens // CHUNK,),
        in_specs=[flat, flat, pl.BlockSpec((2, CHUNK, 3 * GROUP_COLS), lambda i: (0, i, 0))]
        + [whole(a) for a in (w0, w1, gain1)],
        out_specs=[flat, line, line],
        out_shape=[tok(F32), vec, vec],
        cost_estimate=cost(2 * 10**9, 8 << 20),
        name="input_grad",
    )(x_flat, hidden_grad, dqkv, w0, w1, gain1)
    norms = SmallSum(jnp.concatenate([gain1_grad, shift1_grad, gain2_grad, shift2_grad], axis=0))

    lockstep(last, big)
    lockstep(last, big)
    while last.left > 0 or big.left > 0 or norms.left > 0:
        lockstep(last, big, norms)

    down_rows, out_rows, qkv_rows = own_ff, w_out.shape[0], 3 * head_cols
    if ordered:
        shapes = [jax.ShapeDtypeStruct(s, F32) for s in (w_up.shape, w_down.shape, w_out.shape)]
        up_grad, down_grad, out_grad = pl.pallas_call(
            functools.partial(ffn_out_kernel, n_ff, n_out),
            grid=(1,),
            in_specs=[smem] + [whole(a) for a in big.result],
            out_specs=[whole(s) for s in shapes],
            out_shape=shapes,
            scratch_shapes=[pltpu.VMEM((own_ff, width), F32)],
            cost_estimate=cost(0, 8 << 20),
            name="ffn_out",
        )(targets, *big.result)
        shape = jax.ShapeDtypeStruct((width, qkv_rows), F32)
        qkv_grad = pl.pallas_call(
            qkv_out_kernel,
            grid=(1,),
            in_specs=[smem] + [whole(a) for a in last.result],
            out_specs=whole(shape),
            out_shape=shape,
            scratch_shapes=[pltpu.VMEM((qkv_rows, width), F32)],
            cost_estimate=cost(0, 3 << 20),
            name="qkv_out",
        )(targets, *last.result)
    else:

        def natural_rows(pair, count):
            both = jnp.concatenate(pair, axis=0).reshape(wide, -1, 512)
            places = jnp.zeros((wide,), jnp.int32).at[targets].set(jnp.arange(wide, dtype=jnp.int32))
            return jnp.take(both, places, axis=0).astype(F32)

        full = natural_rows(big.result, wide)
        down_grad = full[:, :n_ff].reshape(w_down.shape)
        up_grad = full[:, n_ff : 2 * n_ff].reshape(own_ff, width).T
        out_grad = full[:, 2 * n_ff :].reshape(w_out.shape)
        qkv_grad = natural_rows(last.result, wide).reshape(qkv_rows, width).T
    norm_sums = norms.operand
    return (
        block_out.reshape(feats, samp, width),
        input_grad.reshape(feats, samp, width),
        norm_sums[0],
        norm_sums[1],
        qkv_grad.reshape(width, 3, head_cols),
        out_grad,
        norm_sums[2],
        norm_sums[3],
        up_grad,
        down_grad,
    )


def solution(mesh):
    rows = P("narrow", "wide", None)
    placed = (
        rows, P(), P(), P(), P(None, None, "narrow"), P("narrow", None),
        P(), P(), P(None, "narrow"), P("narrow", None), rows,
    )
    outs = (
        rows, rows, P(), P(), P(None, None, "narrow"), P("narrow", None),
        P(), P(), P(None, "narrow"), P("narrow", None),
    )
    return jax.shard_map(local, mesh=mesh, in_specs=placed, out_specs=outs, check_vma=False)
```

time: 300 us -> 270 us (0.900)
  blocking collectives: 40 us -> 0 us
  Pallas kernels: 71.4 us -> 109 us
  waiting for transfers between devices: 80.2 us -> 62 us
  matrix products: 8.12 us -> 0 us
  other arithmetic: 20.8 us -> 13.9 us
  local copies, waits for them, and re-layouts: 13.5 us -> 17.7 us
    ppermute x24 -> x13, waiting for transfers between devices: 80.2 us -> 33.3 us  [swap(): return lax.ppermute(x, axis, [(i, i ^ bit) for i in range(count)])]
    psum x1 -> x0, blocking collectives: 40 us -> none  [local(): lax.psum(jnp.concatenate([gain1_grad, shift1_grad, gain2_grad, shift2_gra...]
    pallas_call x3 -> x9, Pallas kernels: 71.4 us -> 109 us  [the longest x1 35.2 us: local(): pl.pallas_call(functools.partial(chain_kernel, narrow - 1, inpack, ordere...]
    ppermute x24 -> x13, starting transfers between devices: 53.7 us -> 18.8 us  [swap(): return lax.ppermute(x, axis, [(i, i ^ bit) for i in range(count)])]
    ppermute x0 -> x14, starting transfers between devices: none -> 22 us  [mixed(): return lax.ppermute(x, ('wide', 'narrow'), pairs)]
    ppermute x0 -> x14, waiting for transfers between devices: none -> 21.6 us  [mixed(): return lax.ppermute(x, ('wide', 'narrow'), pairs)]
    ppermute x2 -> x4, starting transfers between devices: 7.31 us -> 19.7 us  [halo(): prev = lax.ppermute(x, axis, [(i, i + 1) for i in range(count - 1)])]
    dot_general x6 -> x0, matrix products: 8.12 us -> none  [dot_tn(): lax.dot_general(a, b, (((0,), (0,)), ((), ())), preferred_element_type=F32)]
  transfers between devices with their start and end apart: 28 -> 35, of which waited for: 13 -> 15; matrix products, arithmetic and copies ran while one was open for 9% -> 7% of each run, Pallas kernels for 16% -> 26%
where the time goes in v3:
time: 270 us
  Pallas kernels  109 us (40%)
  starting transfers between devices  65.8 us (24%)
  waiting for transfers between devices  62 us (23%)
  local copies, waits for them, and re-layouts  17.7 us (7%)
  other arithmetic  13.9 us (5%)
    pallas_call x1, Pallas kernels, local(): pl.pallas_call(functools.partial(chain_kernel, narrow - 1, inpack, ordere...  35.2 us
    ppermute x13, waiting for transfers between devices, swap(): return lax.ppermute(x, axis, [(i, i ^ bit) for i in range(count)])  33.3 us
    pallas_call x2, Pallas kernels, local(): pl.pallas_call(attn_bwd_kernel, grid=(steps,), in_specs=specs, out_specs=...  30.9 us
    pallas_call x2, Pallas kernels, local(): pl.pallas_call(attn_fwd_kernel, grid=(steps,), in_specs=specs, out_specs=...  22.1 us
    ppermute x14, starting transfers between devices, mixed(): return lax.ppermute(x, ('wide', 'narrow'), pairs)  22 us
    ppermute x14, waiting for transfers between devices, mixed(): return lax.ppermute(x, ('wide', 'narrow'), pairs)  21.6 us
    ppermute x4, starting transfers between devices, halo(): prev = lax.ppermute(x, axis, [(i, i + 1) for i in range(count - 1)])  19.7 us
    ppermute x13, starting transfers between devices, swap(): return lax.ppermute(x, axis, [(i, i ^ bit) for i in range(count)])  18.8 us
  transfers between devices with their start and end apart: 35, of which 15 were waited for; matrix products, arithmetic and copies ran while one was open for 7% of the time, Pallas kernels for 26%

profile of v3, /device:TPU:0, one launch (start us, length us, event | category | flops | bytes accessed | tf_op | source)
XLA Modules:
  0.0 269.6 jit_solution(11674758339934166791)
XLA Ops:
  2.8 3.2 %collective-permute-start = (bf16[8,64,512]{2,1,0:T(8,128)(2,1)}, bf16[8,64,512]{2,1,0:T(8,128)(2,1)}, u32[]{:S(2)}, u32[]{:S(2)}) collective-permute-start(bf16[8,64,512]{2,1,0:T(8,128)(2,1)} %get-tuple-element.142), channel_id=1, source_target_pairs={{0,2},{2,4},{4,6},{6,8},{8,10},{10,12},{12,14},{14,16},{16,18},{18... | collective-permute-start | bytes 1572872 | tf_op jit(solution)/shard_map/ppermute | solution.py:353
  13.2 7.0 %collective-permute-done.4 = bf16[256,768]{1,0:T(8,128)(2,1)} collective-permute-done((bf16[256,768]{1,0:T(8,128)(2,1)}, bf16[256,768]{1,0:T(8,128)(2,1)}, u32[]{:S(2)}, u32[]{:S(2)}) %collective-permute-start.4) | collective-permute-done | bytes 393248 | tf_op jit(solution)/shard_map/ppermute | solution.py:348
  26.6 11.1 %attn_fwd_0.1 = (bf16[2,3,1024,768]{3,2,1,0:T(8,128)(2,1)}, bf16[16,64,512]{2,1,0:T(8,128)(2,1)}) custom-call(s32[192,1]{1,0:T(8,128)} %copy.42.idc, s32[3,256]{1,0:T(4,128)} %tile.12.idr, bf16[8,64,512]{2,1,0:T(8,128)(2,1)} %collective-permute-done.xp, bf16[16,64,512]{2,1,0:T(8,128)(2,1)} %xo.3, bf16[8,64,512]{2,1,0:T(8,128)(2,1)} %collective-permute-done.1.xn, ...), custom_call_target="tpu_custom_call" | custom-call | flops 3000000000 | bytes 12582912 | tf_op jit(solution)/shard_map/attn_fwd_0/pallas_call | solution.py:585
  37.7 11.7 %collective-permute-done.6.refs_9_ = bf16[1152,512]{1,0:T(8,128)(2,1)} collective-permute-done((bf16[1152,512]{1,0:T(8,128)(2,1)S(1)}, bf16[1152,512]{1,0:T(8,128)(2,1)}, u32[]{:S(2)}, u32[]{:S(2)}) %collective-permute-start.6) | collective-permute-done | bytes 1179680 | tf_op jit(solution)/shard_map/ppermute | solution.py:348
  57.2 11.1 %attn_fwd_1.1 = (bf16[2,3,1024,768]{3,2,1,0:T(8,128)(2,1)}, bf16[16,64,512]{2,1,0:T(8,128)(2,1)}) custom-call(s32[192,1]{1,0:T(8,128)} %copy.42.idc, s32[3,256]{1,0:T(4,128)} %tile.12.idr, bf16[8,64,512]{2,1,0:T(8,128)(2,1)} %copy-done.10, bf16[16,64,512]{2,1,0:T(8,128)(2,1)} %xo.3, ...), custom_call_target="tpu_custom_call", output_to_operand_aliasing={{0}: (9, {}), {1}: (10, {})} | custom-call | flops 3000000000 | bytes 12582912 | tf_op jit(solution)/shard_map/attn_fwd_1/pallas_call | solution.py:585
  69.2 35.2 %chain.1 = (bf16[1024,512]{1,0:T(8,128)(2,1)}, f32[1024,512]{1,0:T(8,128)}, bf16[1024,512]{1,0:T(8,128)(2,1)}, f32[1,512]{1,0:T(1,128)}, f32[1,512]{1,0:T(1,128)...) custom-call(s32[33]{0:T(128)} %pad_add_fusion.refs_0_.table, bf16[1024,512]{1,0:T(8,128)(2,1)} %bitcast.20, ...), custom_call_target="tpu_custom_call" | custom-call | flops 15000000512 | bytes 20971520 | tf_op jit(solution)/shard_map/chain/pallas_call | solution.py:627
  104.5 8.6 %collective-permute-start.12 = (bf16[2304,512]{1,0:T(8,128)(2,1)}, bf16[2304,512]{1,0:T(8,128)(2,1)S(1)}, u32[]{:S(2)}, u32[]{:S(2)}) collective-permute-start(bf16[2304,512]{1,0:T(8,128)(2,1)} %get-tuple-element.80), channel_id=1, source_target_pairs={{0,2},{2,0},{4,6},{6,4},{8,10},{10,8},{12,14},{14,12},{16,18},{18,... | collective-permute-start | bytes 7077896 | tf_op jit(solution)/shard_map/ppermute | solution.py:348
  118.6 4.3 %collective-permute-done.9.dn_ref = bf16[8,64,512]{2,1,0:T(8,128)(2,1)S(1)} collective-permute-done((bf16[8,64,512]{2,1,0:T(8,128)(2,1)S(1)}, bf16[8,64,512]{2,1,0:T(8,128)(2,1)S(1)}, u32[]{:S(2)}, u32[]{:S(2)}) %collective-permute-start.9) | collective-permute-done | bytes 524320 | tf_op jit(solution)/shard_map/ppermute | solution.py:354
  127.7 12.1 %collective-permute-start.10 = (bf16[8,64,512]{2,1,0:T(8,128)(2,1)}, bf16[8,64,512]{2,1,0:T(8,128)(2,1)}, u32[]{:S(2)}, u32[]{:S(2)}) collective-permute-start(bf16[8,64,512]{2,1,0:T(8,128)(2,1)} %bitcast.11), channel_id=1, source_target_pairs={{0,2},{2,4},{4,6},{6,8},{8,10},{10,12},{12,14},{14,16},{16,18},{18... | collective-permute-start | bytes 1572872 | tf_op jit(solution)/shard_map/ppermute | solution.py:353
  141.3 15.5 %attn_bwd_0.1.rest_0_ = bf16[2,1024,768]{2,1,0:T(8,128)(2,1)} custom-call(s32[192,1]{1,0:T(8,128)} %copy.42.idc, s32[3,256]{1,0:T(4,128)} %tile.12.idr, bf16[2,3,1024,768]{3,2,1,0:T(8,128)(2,1)} %get-tuple-element.76.qkv_ref, bf16[8,64,512]{2,1,0:T(8,128)(2,1)} %copy-done.26, bf16[16,64,512]{2,1,0:T(8,128)(2,1)} %bitcast.26, bf16[8,64,512]{2,1,0:T(8,128)(2,1)} %copy-done.27), custom_call_target="tpu_custom_call" | custom-call | flops 10000000000 | bytes 12582912 | tf_op jit(solution)/shard_map/attn_bwd_0/pallas_call | solution.py:666
  158.3 3.2 %collective-permute-start.14 = (bf16[576,512]{1,0:T(8,128)(2,1)S(1)}, bf16[576,512]{1,0:T(8,128)(2,1)S(1)}, u32[]{:S(2)}, u32[]{:S(2)}) collective-permute-start(bf16[576,512]{1,0:T(8,128)(2,1)S(1)} %add_convert_fusion.1), channel_id=1, source_target_pairs={{0,4},{1,5},{2,3},{3,2},{4,0},{5,1},{6,7},{7,6},{8,12},{9,13},{10,... | collective-permute-start | bytes 1769480 | tf_op jit(solution)/shard_map/ppermute | solution.py:425
  161.5 15.3 %attn_bwd_1.1.dqkv = bf16[2,1024,768]{2,1,0:T(8,128)(2,1)} custom-call(s32[192,1]{1,0:T(8,128)} %copy.42.idc, s32[3,256]{1,0:T(4,128)} %tile.12.idr, bf16[2,3,1024,768]{3,2,1,0:T(8,128)(2,1)} %get-tuple-element.76.qkv_ref, bf16[8,64,512]{2,1,0:T(8,128)(2,1)} %collective-permute-done.10.dp_ref, ...), custom_call_target="tpu_custom_call", output_to_operand_aliasing={{}: (6, {})} | custom-call | flops 10000000000 | bytes 12582912 | tf_op jit(solution)/shard_map/attn_bwd_1/pallas_call | solution.py:666
  180.5 6.2 %qkv_grad.1 = (bf16[768,512]{1,0:T(8,128)(2,1)}, bf16[768,512]{1,0:T(8,128)(2,1)}) custom-call(s32[33]{0:T(128)} %pad_add_fusion.refs_0_.table, bf16[1024,512]{1,0:T(8,128)(2,1)} %bitcast.21, bf16[2,1024,768]{2,1,0:T(8,128)(2,1)} %attn_bwd_1.1.dqkv, f32[1,512]{1,0:T(1,128)} %bitcast.33, f32[1,512]{1,0:T(1,128)} %bitcast.37), custom_call_target="tpu_custom_call" | custom-call | flops 2000000000 | bytes 6291456 | tf_op jit(solution)/shard_map/qkv_grad/pallas_call | solution.py:684
  189.9 8.6 %collective-permute-done.17 = bf16[144,512]{1,0:T(8,128)(2,1)S(1)} collective-permute-done((bf16[144,512]{1,0:T(8,128)(2,1)S(1)}, bf16[144,512]{1,0:T(8,128)(2,1)S(1)}, u32[]{:S(2)}, u32[]{:S(2)}) %collective-permute-start.17) | collective-permute-done | bytes 147488 | tf_op jit(solution)/shard_map/ppermute | solution.py:425
  201.3 7.1 %input_grad.1 = (f32[1024,512]{1,0:T(8,128)}, f32[1,512]{1,0:T(1,128)}, f32[1,512]{1,0:T(1,128)}) custom-call(bf16[1024,512]{1,0:T(8,128)(2,1)} %bitcast.22, f32[1024,512]{1,0:T(8,128)} %get-tuple-element.75.hgrad, bf16[2,1024,768]{2,1,0:T(8,128)(2,1)} %attn_bwd_1.1.dqkv, bf16[512,768]{1,0:T(8,128)(2,1)} %copy-done, bf16[512,768]{1,0:T(8,128)(2,1)} %pad_maximum_fusion.2.w1, ...), custom_call_target="tpu_custom_call" | custom-call | flops 2000000000 | bytes 8388608 | tf_op jit(solution)/shard_map/input_grad/pallas_call | solution.py:701
  209.4 3.1 %collective-permute-start.21 = (bf16[288,512]{1,0:T(8,128)(2,1)S(1)}, bf16[288,512]{1,0:T(8,128)(2,1)S(1)}, u32[]{:S(2)}, u32[]{:S(2)}) collective-permute-start(bf16[288,512]{1,0:T(8,128)(2,1)S(1)} %pad_maximum_fusion.4), channel_id=1, source_target_pairs={{0,8},{1,9},{2,6},{3,7},{4,12},{5,13},{6,2},{7,3},{8,0},{9,1},{10,... | collective-permute-start | bytes 884744 | tf_op jit(solution)/shard_map/ppermute | solution.py:425
  222.3 6.1 %collective-permute-done.25 = f32[4,512]{1,0:T(4,128)S(1)} collective-permute-done((f32[4,512]{1,0:T(4,128)S(1)}, f32[4,512]{1,0:T(4,128)S(1)}, u32[]{:S(2)}, u32[]{:S(2)}) %collective-permute-start.25) | collective-permute-done | bytes 8224 | tf_op jit(solution)/shard_map/ppermute | solution.py:348
  228.6 3.0 %collective-permute-start.26 = (bf16[48,512]{1,0:T(8,128)(2,1)S(1)}, bf16[48,512]{1,0:T(8,128)(2,1)S(1)}, u32[]{:S(2)}, u32[]{:S(2)}) collective-permute-start(bf16[48,512]{1,0:T(8,128)(2,1)S(1)} %add_convert_fusion.9), channel_id=1, source_target_pairs={{0,16},{1,17},{2,18},{3,19},{4,20},{5,21},{6,22},{7,23},{8,24},{9,... | collective-permute-start | bytes 147464 | tf_op jit(solution)/shard_map/ppermute | solution.py:425
  232.4 2.8 %collective-permute-done.27 = f32[4,512]{1,0:T(4,128)S(1)} collective-permute-done((f32[4,512]{1,0:T(4,128)S(1)}, f32[4,512]{1,0:T(4,128)S(1)}, u32[]{:S(2)}, u32[]{:S(2)}) %collective-permute-start.27) | collective-permute-done | bytes 8224 | tf_op jit(solution)/shard_map/ppermute | solution.py:348
  239.1 2.9 %collective-permute-done.29 = f32[4,512]{1,0:T(4,128)S(1)} collective-permute-done((f32[4,512]{1,0:T(4,128)S(1)}, f32[4,512]{1,0:T(4,128)S(1)}, u32[]{:S(2)}, u32[]{:S(2)}) %collective-permute-start.29) | collective-permute-done | bytes 8224 | tf_op jit(solution)/shard_map/ppermute | solution.py:348
  243.0 4.6 %collective-permute-done.31 = bf16[96,512]{1,0:T(8,128)(2,1)S(1)} collective-permute-done((bf16[96,512]{1,0:T(8,128)(2,1)S(1)}, bf16[96,512]{1,0:T(8,128)(2,1)S(1)}, u32[]{:S(2)}, u32[]{:S(2)}) %collective-permute-start.31) | collective-permute-done | bytes 98336 | tf_op jit(solution)/shard_map/ppermute | solution.py:425
  248.4 4.9 %collective-permute-done.32 = bf16[192,512]{1,0:T(8,128)(2,1)S(1)} collective-permute-done((bf16[192,512]{1,0:T(8,128)(2,1)S(1)}, bf16[192,512]{1,0:T(8,128)(2,1)S(1)}, u32[]{:S(2)}, u32[]{:S(2)}) %collective-permute-start.32) | collective-permute-done | bytes 196640 | tf_op jit(solution)/shard_map/ppermute | solution.py:425
  258.6 2.8 %qkv_out.1 = f32[512,768]{1,0:T(8,128)} custom-call(s32[16]{0:T(128)} %pad_add_fusion.1.table, bf16[384,512]{1,0:T(8,128)(2,1)} %copy-done.8, bf16[384,512]{1,0:T(8,128)(2,1)} %copy-done.12), custom_call_target="tpu_custom_call" | custom-call | bytes 3145728 | tf_op jit(solution)/shard_map/qkv_out/pallas_call | solution.py:732
  265.0 4.6 %ffn_out.1 = (f32[512,1024]{1,0:T(8,128)}, f32[1024,512]{1,0:T(8,128)}, f32[256,512]{1,0:T(8,128)}) custom-call(s32[16]{0:T(128)} %pad_add_fusion.1.table, bf16[1152,512]{1,0:T(8,128)(2,1)} %copy-done.1, bf16[1152,512]{1,0:T(8,128)(2,1)} %collective-permute-done.34.got), custom_call_target="tpu_custom_call" | custom-call | bytes 8388608 | tf_op jit(solution)/shard_map/ffn_out/pallas_call | solution.py:721
  (159 shorter events, 73.3 us)
Async XLA Ops:
  2.8 21.7 %collective-permute-start = (bf16[8,64,512]{2,1,0:T(8,128)(2,1)}, bf16[8,64,512]{2,1,0:T(8,128)(2,1)}, u32[]{:S(2)}, u32[]{:S(2)}) collective-permute-start(bf16[8,64,512]{2,1,0:T(8,128)(2,1)} %get-tuple-element.142), channel_id=1, source_target_pairs={{0,2},{2,4},{4,6},{6,8},{8,10},{10,12},{12,14},{14,16},{16,18},{18... | collective-permute-start | bytes 1572872 | tf_op jit(solution)/shard_map/ppermute | solution.py:353
  6.0 18.5 %collective-permute-start.1 = (bf16[8,64,512]{2,1,0:T(8,128)(2,1)}, bf16[8,64,512]{2,1,0:T(8,128)(2,1)}, u32[]{:S(2)}, u32[]{:S(2)}) collective-permute-start(bf16[8,64,512]{2,1,0:T(8,128)(2,1)} %get-tuple-element.142), channel_id=1, source_target_pairs={{2,0},{4,2},{6,4},{8,6},{10,8},{12,10},{14,12},{16,14},{18,16},{20... | collective-permute-start | bytes 1572872 | tf_op jit(solution)/shard_map/ppermute | solution.py:354
  8.7 11.5 %collective-permute-start.4 = (bf16[256,768]{1,0:T(8,128)(2,1)}, bf16[256,768]{1,0:T(8,128)(2,1)}, u32[]{:S(2)}, u32[]{:S(2)}) collective-permute-start(bf16[256,768]{1,0:T(8,128)(2,1)} %constant_dynamic-slice_fusion), channel_id=1, source_target_pairs={{0,1},{1,0},{2,3},{3,2},{4,5},{5,4},{6,7},{7,6},{8,9},{9,8},{10,11... | collective-permute-start | bytes 1179656 | tf_op jit(solution)/shard_map/ppermute | solution.py:348
  20.2 29.2 %collective-permute-start.6 = (bf16[1152,512]{1,0:T(8,128)(2,1)S(1)}, bf16[1152,512]{1,0:T(8,128)(2,1)}, u32[]{:S(2)}, u32[]{:S(2)}) collective-permute-start(bf16[1152,512]{1,0:T(8,128)(2,1)S(1)} %pad_maximum_fusion), channel_id=1, source_target_pairs={{0,1},{1,0},{2,3},{3,2},{4,5},{5,4},{6,7},{7,6},{8,9},{9,8},{10,11... | collective-permute-start | bytes 3538952 | tf_op jit(solution)/shard_map/ppermute | solution.py:348
  49.4 18.8 %collective-permute-start.7 = (bf16[1152,512]{1,0:T(8,128)(2,1)}, bf16[1152,512]{1,0:T(8,128)(2,1)S(1)}, u32[]{:S(2)}, u32[]{:S(2)}) collective-permute-start(bf16[1152,512]{1,0:T(8,128)(2,1)} %collective-permute-done.6.refs_9_), channel_id=1, source_target_pairs={{0,2},{2,0},{4,6},{6,4},{8,10},{10,8},{12,14},{14,12},{16,18},{18,... | collective-permute-start | bytes 3538952 | tf_op jit(solution)/shard_map/ppermute | solution.py:348
  104.5 18.4 %collective-permute-start.12 = (bf16[2304,512]{1,0:T(8,128)(2,1)}, bf16[2304,512]{1,0:T(8,128)(2,1)S(1)}, u32[]{:S(2)}, u32[]{:S(2)}) collective-permute-start(bf16[2304,512]{1,0:T(8,128)(2,1)} %get-tuple-element.80), channel_id=1, source_target_pairs={{0,2},{2,0},{4,6},{6,4},{8,10},{10,8},{12,14},{14,12},{16,18},{18,... | collective-permute-start | bytes 7077896 | tf_op jit(solution)/shard_map/ppermute | solution.py:348
  117.1 5.8 %collective-permute-start.9 = (bf16[8,64,512]{2,1,0:T(8,128)(2,1)S(1)}, bf16[8,64,512]{2,1,0:T(8,128)(2,1)S(1)}, u32[]{:S(2)}, u32[]{:S(2)}) collective-permute-start(bf16[8,64,512]{2,1,0:T(8,128)(2,1)S(1)} %bitcast.29), channel_id=1, source_target_pairs={{2,0},{4,2},{6,4},{8,6},{10,8},{12,10},{14,12},{16,14},{18,16},{20... | collective-permute-start | bytes 1572872 | tf_op jit(solution)/shard_map/ppermute | solution.py:354
  126.1 30.7 %collective-permute-start.13 = (bf16[1152,512]{1,0:T(8,128)(2,1)S(1)}, bf16[1152,512]{1,0:T(8,128)(2,1)}, u32[]{:S(2)}, u32[]{:S(2)}) collective-permute-start(bf16[1152,512]{1,0:T(8,128)(2,1)S(1)} %add_convert_fusion), channel_id=1, source_target_pairs={{0,1},{1,0},{2,10},{3,11},{4,5},{5,4},{6,14},{7,15},{8,9},{9,8},{1... | collective-permute-start | bytes 3538952 | tf_op jit(solution)/shard_map/ppermute | solution.py:425
  127.7 30.6 %collective-permute-start.10 = (bf16[8,64,512]{2,1,0:T(8,128)(2,1)}, bf16[8,64,512]{2,1,0:T(8,128)(2,1)}, u32[]{:S(2)}, u32[]{:S(2)}) collective-permute-start(bf16[8,64,512]{2,1,0:T(8,128)(2,1)} %bitcast.11), channel_id=1, source_target_pairs={{0,2},{2,4},{4,6},{6,8},{8,10},{10,12},{12,14},{14,16},{16,18},{18... | collective-permute-start | bytes 1572872 | tf_op jit(solution)/shard_map/ppermute | solution.py:353
  139.8 18.5 %collective-permute-start.11 = (bf16[8,64,512]{2,1,0:T(8,128)(2,1)}, bf16[8,64,512]{2,1,0:T(8,128)(2,1)}, u32[]{:S(2)}, u32[]{:S(2)}) collective-permute-start(bf16[8,64,512]{2,1,0:T(8,128)(2,1)} %bitcast.11), channel_id=1, source_target_pairs={{2,0},{4,2},{6,4},{8,6},{10,8},{12,10},{14,12},{16,14},{18,16},{20... | collective-permute-start | bytes 1572872 | tf_op jit(solution)/shard_map/ppermute | solution.py:354
  158.3 18.5 %collective-permute-start.14 = (bf16[576,512]{1,0:T(8,128)(2,1)S(1)}, bf16[576,512]{1,0:T(8,128)(2,1)S(1)}, u32[]{:S(2)}, u32[]{:S(2)}) collective-permute-start(bf16[576,512]{1,0:T(8,128)(2,1)S(1)} %add_convert_fusion.1), channel_id=1, source_target_pairs={{0,4},{1,5},{2,3},{3,2},{4,0},{5,1},{6,7},{7,6},{8,12},{9,13},{10,... | collective-permute-start | bytes 1769480 | tf_op jit(solution)/shard_map/ppermute | solution.py:425
  179.0 7.8 %collective-permute-start.15 = (bf16[288,512]{1,0:T(8,128)(2,1)}, bf16[288,512]{1,0:T(8,128)(2,1)S(1)}, u32[]{:S(2)}, u32[]{:S(2)}) collective-permute-start(bf16[288,512]{1,0:T(8,128)(2,1)} %add_convert_fusion.3), channel_id=1, source_target_pairs={{0,8},{1,9},{2,6},{3,7},{4,12},{5,13},{6,2},{7,3},{8,0},{9,1},{10,... | collective-permute-start | bytes 884744 | tf_op jit(solution)/shard_map/ppermute | solution.py:425
  188.1 11.6 %collective-permute-start.16 = (bf16[768,512]{1,0:T(8,128)(2,1)}, bf16[768,512]{1,0:T(8,128)(2,1)S(1)}, u32[]{:S(2)}, u32[]{:S(2)}) collective-permute-start(bf16[768,512]{1,0:T(8,128)(2,1)} %get-tuple-element.96), channel_id=1, source_target_pairs={{0,2},{2,0},{4,6},{6,4},{8,10},{10,8},{12,14},{14,12},{16,18},{18,... | collective-permute-start | bytes 2359304 | tf_op jit(solution)/shard_map/ppermute | solution.py:348
  188.2 10.3 %collective-permute-start.17 = (bf16[144,512]{1,0:T(8,128)(2,1)S(1)}, bf16[144,512]{1,0:T(8,128)(2,1)S(1)}, u32[]{:S(2)}, u32[]{:S(2)}) collective-permute-start(bf16[144,512]{1,0:T(8,128)(2,1)S(1)} %add_convert_fusion.6), channel_id=1, source_target_pairs={{0,16},{1,17},{2,18},{3,19},{4,20},{5,21},{6,22},{7,23},{8,24},{9,... | collective-permute-start | bytes 442376 | tf_op jit(solution)/shard_map/ppermute | solution.py:425
  200.7 8.5 %collective-permute-start.18 = (bf16[384,512]{1,0:T(8,128)(2,1)S(1)}, bf16[384,512]{1,0:T(8,128)(2,1)S(1)}, u32[]{:S(2)}, u32[]{:S(2)}) collective-permute-start(bf16[384,512]{1,0:T(8,128)(2,1)S(1)} %add_convert_fusion.2), channel_id=1, source_target_pairs={{0,1},{1,0},{2,10},{3,11},{4,5},{5,4},{6,14},{7,15},{8,9},{9,8},{1... | collective-permute-start | bytes 1179656 | tf_op jit(solution)/shard_map/ppermute | solution.py:425
  201.3 7.8 %collective-permute-start.19 = (bf16[144,512]{1,0:T(8,128)(2,1)S(1)}, bf16[144,512]{1,0:T(8,128)(2,1)S(1)}, u32[]{:S(2)}, u32[]{:S(2)}) collective-permute-start(bf16[144,512]{1,0:T(8,128)(2,1)S(1)} %add_convert_fusion.5), channel_id=1, source_target_pairs={{0,16},{1,17},{2,18},{3,19},{4,20},{5,21},{6,22},{7,23},{8,24},{9,... | collective-permute-start | bytes 442376 | tf_op jit(solution)/shard_map/ppermute | solution.py:425
  209.3 6.7 %collective-permute-start.20 = (bf16[192,512]{1,0:T(8,128)(2,1)S(1)}, bf16[192,512]{1,0:T(8,128)(2,1)S(1)}, u32[]{:S(2)}, u32[]{:S(2)}) collective-permute-start(bf16[192,512]{1,0:T(8,128)(2,1)S(1)} %add_convert_fusion.4), channel_id=1, source_target_pairs={{0,4},{1,5},{2,3},{3,2},{4,0},{5,1},{6,7},{7,6},{8,12},{9,13},{10,... | collective-permute-start | bytes 589832 | tf_op jit(solution)/shard_map/ppermute | solution.py:425
  209.4 7.8 %collective-permute-start.21 = (bf16[288,512]{1,0:T(8,128)(2,1)S(1)}, bf16[288,512]{1,0:T(8,128)(2,1)S(1)}, u32[]{:S(2)}, u32[]{:S(2)}) collective-permute-start(bf16[288,512]{1,0:T(8,128)(2,1)S(1)} %pad_maximum_fusion.4), channel_id=1, source_target_pairs={{0,8},{1,9},{2,6},{3,7},{4,12},{5,13},{6,2},{7,3},{8,0},{9,1},{10,... | collective-permute-start | bytes 884744 | tf_op jit(solution)/shard_map/ppermute | solution.py:425
  217.2 11.3 %collective-permute-start.24 = (bf16[576,512]{1,0:T(8,128)(2,1)S(1)}, bf16[576,512]{1,0:T(8,128)(2,1)S(1)}, u32[]{:S(2)}, u32[]{:S(2)}) collective-permute-start(bf16[576,512]{1,0:T(8,128)(2,1)S(1)} %pad_maximum_fusion.3), channel_id=1, source_target_pairs={{0,4},{1,5},{2,10},{3,11},{4,0},{5,1},{6,14},{7,15},{8,12},{9,13},... | collective-permute-start | bytes 1769480 | tf_op jit(solution)/shard_map/ppermute | solution.py:425
  219.2 9.2 %collective-permute-start.23 = (bf16[96,512]{1,0:T(8,128)(2,1)S(1)}, bf16[96,512]{1,0:T(8,128)(2,1)S(1)}, u32[]{:S(2)}, u32[]{:S(2)}) collective-permute-start(bf16[96,512]{1,0:T(8,128)(2,1)S(1)} %add_convert_fusion.7), channel_id=1, source_target_pairs={{0,8},{1,9},{2,6},{3,7},{4,12},{5,13},{6,2},{7,3},{8,0},{9,1},{10,... | collective-permute-start | bytes 294920 | tf_op jit(solution)/shard_map/ppermute | solution.py:425
  221.2 7.1 %collective-permute-start.25 = (f32[4,512]{1,0:T(4,128)S(1)}, f32[4,512]{1,0:T(4,128)S(1)}, u32[]{:S(2)}, u32[]{:S(2)}) collective-permute-start(f32[4,512]{1,0:T(4,128)S(1)} %add.180), channel_id=1, source_target_pairs={{0,4},{2,6},{4,0},{6,2},{8,12},{10,14},{12,8},{14,10},{16,20},{18,... | collective-permute-start | bytes 24584 | tf_op jit(solution)/shard_map/ppermute | solution.py:348
  228.6 6.7 %collective-permute-start.26 = (bf16[48,512]{1,0:T(8,128)(2,1)S(1)}, bf16[48,512]{1,0:T(8,128)(2,1)S(1)}, u32[]{:S(2)}, u32[]{:S(2)}) collective-permute-start(bf16[48,512]{1,0:T(8,128)(2,1)S(1)} %add_convert_fusion.9), channel_id=1, source_target_pairs={{0,16},{1,17},{2,18},{3,19},{4,20},{5,21},{6,22},{7,23},{8,24},{9,... | collective-permute-start | bytes 147464 | tf_op jit(solution)/shard_map/ppermute | solution.py:425
  236.1 5.9 %collective-permute-start.28 = (bf16[48,512]{1,0:T(8,128)(2,1)S(1)}, bf16[48,512]{1,0:T(8,128)(2,1)S(1)}, u32[]{:S(2)}, u32[]{:S(2)}) collective-permute-start(bf16[48,512]{1,0:T(8,128)(2,1)S(1)} %add_convert_fusion.8), channel_id=1, source_target_pairs={{0,16},{1,17},{2,18},{3,19},{4,20},{5,21},{6,22},{7,23},{8,24},{9,... | collective-permute-start | bytes 147464 | tf_op jit(solution)/shard_map/ppermute | solution.py:425
  239.1 25.9 %collective-permute-start.34 = (bf16[1152,512]{1,0:T(8,128)(2,1)S(1)}, bf16[1152,512]{1,0:T(8,128)(2,1)}, u32[]{:S(2)}, u32[]{:S(2)}) collective-permute-start(bf16[1152,512]{1,0:T(8,128)(2,1)S(1)} %pad_maximum_fusion.1.mine), channel_id=1, source_target_pairs={{0,2},{2,0},{4,6},{6,4},{8,10},{10,8},{12,14},{14,12},{16,18},{18,... | collective-permute-start | bytes 3538952 | tf_op jit(solution)/shard_map/ppermute | solution.py:348
  (39 other events, 354.0 us)

commit v4 on v3

--- a/solution.py
+++ b/solution.py
@@ -17,6 +17,7 @@
 BF16 = jnp.bfloat16
 NEG = -1e30
 CHUNK = 256
+UNROLL = 4
 
 
 def dot_nn(a, b):
@@ -109,7 +110,7 @@
             o = pick_heads(dot_tn(p, v), m32, samp)
             att_ref[f, :, hg * GROUP_COLS : (hg + 1) * GROUP_COLS] = o.astype(BF16)
 
-    each(feats, column, 2)
+    each(feats, column, UNROLL)
 
 
 def phi_parts(u):
@@ -236,55 +237,76 @@
             packed[2][...] = go[...]
 
 
-def attn_bwd_kernel(idc, idr, qkv_ref, dp_ref, do_ref, dn_ref, *rest):
-    dqkv = rest[-1]
+def bwd_pieces(qkv_ref, hg, sl):
+    k = jnp.concatenate(
+        [qkv_ref[hg, w, sl, GROUP_COLS : 2 * GROUP_COLS] for w in range(3)], axis=0
+    )
+    v = jnp.concatenate(
+        [qkv_ref[hg, w, sl, 2 * GROUP_COLS : 3 * GROUP_COLS] for w in range(3)], axis=0
+    )
+    return k, v
+
+
+def score_grads(ks, vs, qbd, dbd, mask):
+    s = dot_nt(ks, qbd) * SCALE
+    s = jnp.where(mask, s, NEG)
+    top = jnp.max(s, axis=0, keepdims=True)
+    e = jnp.exp(s - top)
+    total = jnp.sum(e, axis=0, keepdims=True)
+    p = e * (1.0 / total)
+    pd = p * dot_nt(vs, dbd)
+    delta = jnp.sum(pd, axis=0, keepdims=True)
+    return (pd - p * delta).astype(BF16), p
+
+
+def attn_bwd_own_kernel(idc, idr, qkv_ref, do_ref, dq_ref, dkv_ref):
     feats, samp, width = do_ref.shape
     m16 = lane_head(1, BF16)
     m32 = lane_head(1, F32)
-    spans = ((0, 2), (0, 3), (1, 3))
-    masks = [idc[a * samp : b * samp, :] == idr[g : g + 1, :] for g, (a, b) in enumerate(spans)]
-    grads = (dp_ref, do_ref, dn_ref)
+    mask = idc[...] == idr[1:2, :]
 
     def column(f):
         sl = rows_at(f, samp)
         for hg in range(2):
-            cols = slice(hg * GROUP_COLS, (hg + 1) * GROUP_COLS)
-            k = jnp.concatenate(
-                [qkv_ref[hg, w, sl, GROUP_COLS : 2 * GROUP_COLS] for w in range(3)], axis=0
-            )
-            v = jnp.concatenate(
-                [qkv_ref[hg, w, sl, 2 * GROUP_COLS : 3 * GROUP_COLS] for w in range(3)], axis=0
-            )
-            dk = jnp.zeros((samp, GROUP_COLS), F32)
-            dv = jnp.zeros((samp, GROUP_COLS), F32)
-            for g, (a, b) in enumerate(spans):
-                ks = k[a * samp : b * samp]
-                vs = v[a * samp : b * samp]
+            k, v = bwd_pieces(qkv_ref, hg, sl)
+            qbd = block_diag(qkv_ref[hg, 1, sl, 0:GROUP_COLS], m16)
+            dbd = block_diag(do_ref[f, :, hg * GROUP_COLS : (hg + 1) * GROUP_COLS], m16)
+            ds, p = score_grads(k, v, qbd, dbd, mask)
+            dq = pick_heads(dot_tn(ds, k), m32, samp)
+            dq_ref[hg, sl, :] = (dq * SCALE).astype(BF16)
+            dkv_ref[hg, sl, 0:GROUP_COLS] = dot_nn(ds[samp : 2 * samp], qbd)
+            dkv_ref[hg, sl, GROUP_COLS : 2 * GROUP_COLS] = dot_nn(p[samp : 2 * samp].astype(BF16), dbd)
+
+    each(feats, column, UNROLL)
+
+
+def attn_bwd_near_kernel(idc, idr, qkv_ref, dp_ref, dn_ref, sum_ref, dkv_ref):
+    feats, samp, width = dp_ref.shape
+    m16 = lane_head(1, BF16)
+    near = ((0, 0, dp_ref), (2, 1, dn_ref))
+    masks = [idc[a * samp : (a + 2) * samp, :] == idr[g : g + 1, :] for g, a, _ in near]
+
+    def column(f):
+        sl = rows_at(f, samp)
+        for hg in range(2):
+            k, v = bwd_pieces(qkv_ref, hg, sl)
+            dk = sum_ref[hg, sl, 0:GROUP_COLS]
+            dv = sum_ref[hg, sl, GROUP_COLS : 2 * GROUP_COLS]
+            for mask, (g, a, ref) in zip(masks, near):
+                span = slice(a * samp, (a + 2) * samp)
                 qbd = block_diag(qkv_ref[hg, g, sl, 0:GROUP_COLS], m16)
-                dbd = block_diag(grads[g][f, :, cols], m16)
-                s = dot_nt(ks, qbd) * SCALE
-                s = jnp.where(masks[g], s, NEG)
-                top = jnp.max(s, axis=0, keepdims=True)
-                e = jnp.exp(s - top)
-                total = jnp.sum(e, axis=0, keepdims=True)
-                p = e * (1.0 / total)
-                dp = dot_nt(vs, dbd)
-                pd = p * dp
-                delta = jnp.sum(pd, axis=0, keepdims=True)
-                ds = (pd - p * delta).astype(BF16)
+                dbd = block_diag(ref[f, :, hg * GROUP_COLS : (hg + 1) * GROUP_COLS], m16)
+                ds, p = score_grads(k[span], v[span], qbd, dbd, mask)
                 own = slice((1 - a) * samp, (2 - a) * samp)
                 dk = dk + dot_nn(ds[own], qbd)
                 dv = dv + dot_nn(p[own].astype(BF16), dbd)
-                if g == 1:
-                    dq = pick_heads(dot_tn(ds, ks), m32, samp)
-            dqkv[hg, sl, 0:GROUP_COLS] = (dq * SCALE).astype(BF16)
-            dqkv[hg, sl, GROUP_COLS : 2 * GROUP_COLS] = (dk * SCALE).astype(BF16)
-            dqkv[hg, sl, 2 * GROUP_COLS : 3 * GROUP_COLS] = dv.astype(BF16)
-
-    each(feats, column, 2)
-
-
-def qkv_grad_kernel(ordered, table, x, dqkv, gain, shift, *refs):
+            dkv_ref[hg, sl, 0:GROUP_COLS] = (dk * SCALE).astype(BF16)
+            dkv_ref[hg, sl, GROUP_COLS : 2 * GROUP_COLS] = dv.astype(BF16)
+
+    each(feats, column, UNROLL)
+
+
+def qkv_grad_kernel(ordered, table, x, dq, dkv, gain, shift, *refs):
     normed, gq = refs[-2:]
     outs = refs[:-2]
     tokens, width = x.shape
@@ -295,9 +317,10 @@
         normed[sl] = (xhat * gain[...] + shift[...]).astype(BF16)
 
     each(tokens // CHUNK, start)
-    cols = dqkv.shape[2]
     for hg in range(2):
-        gq[hg * cols : (hg + 1) * cols] = dot_tn(dqkv[hg], normed[...]).astype(BF16)
+        low = 3 * hg * GROUP_COLS
+        gq[low : low + GROUP_COLS] = dot_tn(dq[hg], normed[...]).astype(BF16)
+        gq[low + GROUP_COLS : low + 3 * GROUP_COLS] = dot_tn(dkv[hg], normed[...]).astype(BF16)
     if ordered:
         blocks = (table.shape[0] - 1) // 2
         size = gq.shape[0] // (2 * blocks)
@@ -308,9 +331,10 @@
         outs[0][...] = gq[...]
 
 
-def input_grad_kernel(x, hgrad, dqkv, w0, w1, gain, igrad_ref, g1_ref, s1_ref):
+def input_grad_kernel(x, hgrad, dq, dkv, w0, w1, gain, igrad_ref, g1_ref, s1_ref):
     xhat, rstd = norm_parts(x[...].astype(F32))
-    dn1 = dot_nt(dqkv[0], w0[...]) + dot_nt(dqkv[1], w1[...])
+    dn1 = dot_nt(dq[0], w0[:, :GROUP_COLS]) + dot_nt(dq[1], w1[:, :GROUP_COLS])
+    dn1 = dn1 + dot_nt(dkv[0], w0[:, GROUP_COLS:]) + dot_nt(dkv[1], w1[:, GROUP_COLS:])
 
     @pl.when(pl.program_id(0) == 0)
     def _():
@@ -340,7 +364,9 @@
     for side, ref in enumerate((mine, got)):
         for b in range(blocks):
             turned[rows_at(table[side * blocks + b], size)] = ref[b * size : (b + 1) * size].astype(F32)
-    out_ref[...] = turned[...].T
+    for j in range(3):
+        cols = turned.shape[0] // 3
+        out_ref[j] = turned[j * cols : (j + 1) * cols].T
 
 
 def swap(x, axis, bit):
@@ -514,9 +540,10 @@
         size = a.shape[axis] // 2
         return lax.dynamic_slice_in_dim(a, core * size, size, axis)
 
-    halves_in = [inputs[:part], inputs[part:]]
-    qkv_mine = gather_pieces(core_half(w_qkv.reshape(width, 3 * head_cols), 0), "narrow")[1:]
-    prev0, next0 = halo(halves_in[0], "wide")
+    qkv_half = core_half(w_qkv.reshape(width, 3 * head_cols), 0)
+    qkv_half, early = tied(qkv_half, inputs[:part])
+    qkv_mine = gather_pieces(qkv_half, "narrow")[1:]
+    prev0, next0 = halo(early, "wide")
     up_half = core_half(w_up, 1)
     small = jnp.concatenate(
         [up_half.reshape(-1, 512), core_half(w_down, 0), core_half(w_out, 0)], axis=0
@@ -525,8 +552,8 @@
     small, qkv_mine = held[0], list(held[1:])
     pack_mine = gather_pieces(small, "narrow")[1:]
     qkv_got = [swap(p, "wide", 1) for p in qkv_mine]
-    late, prev0, next0 = tied(halves_in[1], prev0, next0)
-    prev1, next1 = halo(late, "wide")
+    late, prev0, next0 = tied(inputs, prev0, next0)
+    prev1, next1 = halo(late[part:], "wide")
 
     def whole_of(mine, got):
         first = jnp.where(core == 0, mine, got)
@@ -595,9 +622,9 @@
             cost_estimate=cost(6 * 10**9 // 2, 12 << 20),
             name=f"attn_fwd_{h}",
         )(*args)
-        if h == 0:
-            pack_mine = list(tied(done[1], *pack_mine))[1:]
-            pack_got = [swap(p, "wide", 1) for p in pack_mine]
+    held = tied(done[1], *pack_mine)
+    done, pack_mine = [done[0], held[0]], list(held[1:])
+    pack_got = [swap(p, "wide", 1) for p in pack_mine]
     qkv, attended = done
 
     x_flat = inputs.reshape(tokens, width)
@@ -646,41 +673,45 @@
     big = Reduction(plan, packed[0], packed[1])
 
     datt = dattended.reshape(feats, samp, width)
-    around = [halo(datt[:part], "wide")]
+    d_prev, d_next = halo(datt, "wide")
     lockstep(big)
-    first, *around[0] = tied(datt[part:], *around[0])
-    around.append(halo(first, "wide"))
-    dqkv = None
-    for h in range(2):
-        off = h * steps
-        before, after = around[h]
-        before, after, big.operand = tied(before, after, big.operand)
-        args = [id_col, id_row, qkv, before, datt, after]
-        specs = [whole(id_col), whole(id_row), qkv_block(off), cube(0), cube(off), cube(0)]
-        alias = {}
-        if dqkv is not None:
-            alias = {len(args): 0}
-            args.append(dqkv)
-            specs.append(anywhere)
-        lockstep(big)
-        dqkv = pl.pallas_call(
-            attn_bwd_kernel,
-            grid=(steps,),
-            in_specs=specs,
-            out_specs=pl.BlockSpec((2, rows, 3 * GROUP_COLS), lambda i, off=off: (0, i + off, 0)),
-            out_shape=jax.ShapeDtypeStruct((2, tokens, 3 * GROUP_COLS), BF16),
-            input_output_aliases=alias,
-            cost_estimate=cost(10 * 10**9, 12 << 20),
-            name=f"attn_bwd_{h}",
-        )(*args)
-    dqkv, big.operand = tied(dqkv, big.operand)
+    group2 = group
+    all_steps = feats // group2
+
+    def pair_block(cols):
+        return pl.BlockSpec((2, rows, cols), lambda i: (0, i, 0))
+
+    dq, dkv_own = pl.pallas_call(
+        attn_bwd_own_kernel,
+        grid=(all_steps,),
+        in_specs=[whole(id_col), whole(id_row), qkv_block(0), cube(0)],
+        out_specs=[pair_block(GROUP_COLS), pair_block(2 * GROUP_COLS)],
+        out_shape=[
+            jax.ShapeDtypeStruct((2, tokens, GROUP_COLS), BF16),
+            jax.ShapeDtypeStruct((2, tokens, 2 * GROUP_COLS), F32),
+        ],
+        cost_estimate=cost(10 * 10**9, 14 << 20),
+        name="attn_bwd_own",
+    )(id_col, id_row, qkv, datt)
+    dkv_own, big.operand = tied(dkv_own, big.operand)
+    lockstep(big)
+    dkv = pl.pallas_call(
+        attn_bwd_near_kernel,
+        grid=(all_steps,),
+        in_specs=[whole(id_col), whole(id_row), qkv_block(0), cube(0), cube(0), pair_block(2 * GROUP_COLS)],
+        out_specs=pair_block(2 * GROUP_COLS),
+        out_shape=jax.ShapeDtypeStruct((2, tokens, 2 * GROUP_COLS), BF16),
+        cost_estimate=cost(10 * 10**9, 14 << 20),
+        name="attn_bwd_near",
+    )(id_col, id_row, qkv, d_prev, d_next, dkv_own)
+    dkv, big.operand = tied(dkv, big.operand)
     lockstep(big)
 
     natural = (6 * GROUP_COLS, width)
     outs = [jax.ShapeDtypeStruct((blocks * n_qkv, 512), BF16)] * 2
     if not ordered:
         outs = [jax.ShapeDtypeStruct(natural, BF16)]
-    args = [sources, x_flat, dqkv, gain1, shift1]
+    args = [sources, x_flat, dq, dkv, gain1, shift1]
     packed = pl.pallas_call(
         functools.partial(qkv_grad_kernel, ordered),
         grid=(1,),
@@ -697,24 +728,24 @@
     last = Reduction(plan, packed[0], packed[1])
 
     flat = pl.BlockSpec((CHUNK, width), lambda i: (i, 0))
-    dqkv, last.operand = tied(dqkv, last.operand)
+    dkv, last.operand = tied(dkv, last.operand)
     input_grad, gain1_grad, shift1_grad = pl.pallas_call(
         input_grad_kernel,
         grid=(tokens // CHUNK,),
-        in_specs=[flat, flat, pl.BlockSpec((2, CHUNK, 3 * GROUP_COLS), lambda i: (0, i, 0))]
+        in_specs=[flat, flat]
+        + [pl.BlockSpec((2, CHUNK, n * GROUP_COLS), lambda i: (0, i, 0)) for n in (1, 2)]
         + [whole(a) for a in (w0, w1, gain1)],
         out_specs=[flat, line, line],
         out_shape=[tok(F32), vec, vec],
         cost_estimate=cost(2 * 10**9, 8 << 20),
         name="input_grad",
-    )(x_flat, hidden_grad, dqkv, w0, w1, gain1)
+    )(x_flat, hidden_grad, dq, dkv, w0, w1, gain1)
     norms = SmallSum(jnp.concatenate([gain1_grad, shift1_grad, gain2_grad, shift2_grad], axis=0))
 
     lockstep(last, big)
     lockstep(last, big)
-    while last.left > 0 or big.left > 0 or norms.left > 0:
+    while big.left > 0:
         lockstep(last, big, norms)
-
     down_rows, out_rows, qkv_rows = own_ff, w_out.shape[0], 3 * head_cols
     if ordered:
         shapes = [jax.ShapeDtypeStruct(s, F32) for s in (w_up.shape, w_down.shape, w_out.shape)]
@@ -728,7 +759,13 @@
             cost_estimate=cost(0, 8 << 20),
             name="ffn_out",
         )(targets, *big.result)
-        shape = jax.ShapeDtypeStruct((width, qkv_rows), F32)
+    while last.left > 0 or norms.left > 0:
+        if ordered and last.left == 1:
+            last.operand, out_grad = tied(last.operand, out_grad)
+        lockstep(last, norms)
+
+    if ordered:
+        shape = jax.ShapeDtypeStruct((3, width, head_cols), F32)
         qkv_grad = pl.pallas_call(
             qkv_out_kernel,
             grid=(1,),
@@ -739,6 +776,7 @@
             cost_estimate=cost(0, 3 << 20),
             name="qkv_out",
         )(targets, *last.result)
+        qkv_grad = qkv_grad.transpose(1, 0, 2)
     else:
 
         def natural_rows(pair, count):
@@ -750,14 +788,14 @@
         down_grad = full[:, :n_ff].reshape(w_down.shape)
         up_grad = full[:, n_ff : 2 * n_ff].reshape(own_ff, width).T
         out_grad = full[:, 2 * n_ff :].reshape(w_out.shape)
-        qkv_grad = natural_rows(last.result, wide).reshape(qkv_rows, width).T
+        qkv_grad = natural_rows(last.result, wide).reshape(qkv_rows, width).T.reshape(width, 3, head_cols)
     norm_sums = norms.operand
     return (
         block_out.reshape(feats, samp, width),
         input_grad.reshape(feats, samp, width),
         norm_sums[0],
         norm_sums[1],
-        qkv_grad.reshape(width, 3, head_cols),
+        qkv_grad,
         out_grad,
         norm_sums[2],
         norm_sums[3],

time: 270 us -> 240 us (0.89)
  waiting for transfers between devices: 62 us -> 44.7 us
  starting transfers between devices: 65.8 us -> 49.5 us
  local copies, waits for them, and re-layouts: 17.7 us -> 11.2 us
  Pallas kernels: 109 us -> 114 us
  other arithmetic: 13.9 us -> 18.7 us
    ppermute x13, waiting for transfers between devices: 33.3 us -> 21.9 us  [swap(): return lax.ppermute(x, axis, [(i, i ^ bit) for i in range(count)])]
    pallas_call x2, Pallas kernels: 30.9 us -> 40 us  [the longest x1 23.2 us: local(): pl.pallas_call(attn_bwd_near_kernel, grid=(all_steps,), in_specs=[whole(i...]
    ppermute x4 -> x3, starting transfers between devices: 19.7 us -> 10.9 us  [halo(): prev = lax.ppermute(x, axis, [(i, i + 1) for i in range(count - 1)])]
    ppermute x4 -> x3, waiting for transfers between devices: 6.87 us -> 0.01 us  [halo(): nxt = lax.ppermute(x, axis, [(i + 1, i) for i in range(count - 1)])]
    ppermute x13, starting transfers between devices: 18.8 us -> 12.2 us  [swap(): return lax.ppermute(x, axis, [(i, i ^ bit) for i in range(count)])]
    pallas_call x2, Pallas kernels: 22.1 us -> 17.6 us  [local(): pl.pallas_call(attn_fwd_kernel, grid=(steps,), in_specs=specs, out_specs=...]
    convert_element_type x10, other arithmetic: 9.7 us -> 13.4 us  [total(): return out.astype(BF16)]
    slice x2, local copies, waits for them, and re-layouts: 4.22 us -> 1.19 us  [the longest x1 1.16 us: local(): qkv_half, early = tied(qkv_half, inputs[:part])]
  transfers between devices with their start and end apart: 35 -> 33, of which waited for: 15 -> 15; matrix products, arithmetic and copies ran while one was open for 7% -> 7% of each run, Pallas kernels for 26% -> 30%
where the time goes in v4:
time: 240 us; the launch traced here: 239 us
  Pallas kernels  114 us (48%)
  starting transfers between devices  49.5 us (21%)
  waiting for transfers between devices  44.7 us (19%)
  other arithmetic  18.7 us (8%)
  local copies, waits for them, and re-layouts  11.2 us (5%)
    pallas_call x1, Pallas kernels, local(): pl.pallas_call(functools.partial(chain_kernel, narrow - 1, inpack, ordere...  35.2 us
    pallas_call x1, Pallas kernels, local(): pl.pallas_call(attn_bwd_near_kernel, grid=(all_steps,), in_specs=[whole(i...  23.2 us
    ppermute x14, waiting for transfers between devices, mixed(): return lax.ppermute(x, ('wide', 'narrow'), pairs)  22.8 us
    ppermute x14, starting transfers between devices, mixed(): return lax.ppermute(x, ('wide', 'narrow'), pairs)  22.5 us
    ppermute x13, waiting for transfers between devices, swap(): return lax.ppermute(x, axis, [(i, i ^ bit) for i in range(count)])  21.9 us
    pallas_call x2, Pallas kernels, local(): pl.pallas_call(attn_fwd_kernel, grid=(steps,), in_specs=specs, out_specs=...  17.6 us
    pallas_call x1, Pallas kernels, local(): pl.pallas_call(attn_bwd_own_kernel, grid=(all_steps,), in_specs=[whole(id...  16.8 us
    convert_element_type x10, other arithmetic, total(): return out.astype(BF16)  13.4 us
  transfers between devices with their start and end apart: 33, of which 15 were waited for; matrix products, arithmetic and copies ran while one was open for 7% of the time, Pallas kernels for 30%

profile of v4, /device:TPU:0, one launch (start us, length us, event | category | flops | bytes accessed | tf_op | source)
XLA Modules:
  0.0 238.7 jit_solution(10270640965673873768)
XLA Ops:
  4.7 3.8 %collective-permute-start = (bf16[8,64,512]{2,1,0:T(8,128)(2,1)S(1)}, bf16[8,64,512]{2,1,0:T(8,128)(2,1)}, u32[]{:S(2)}, u32[]{:S(2)}) collective-permute-start(bf16[8,64,512]{2,1,0:T(8,128)(2,1)S(1)} %slice.132), channel_id=1, source_target_pairs={{0,2},{2,4},{4,6},{6,8},{8,10},{10,12},{12,14},{14,16},{16,18},{18... | collective-permute-start | bytes 1572872 | tf_op jit(solution)/shard_map/ppermute | solution.py:379
  8.5 3.0 %collective-permute-start.4 = (bf16[256,768]{1,0:T(8,128)(2,1)}, bf16[256,768]{1,0:T(8,128)(2,1)}, u32[]{:S(2)}, u32[]{:S(2)}) collective-permute-start(bf16[256,768]{1,0:T(8,128)(2,1)} %constant_dynamic-slice_fusion.3), channel_id=1, source_target_pairs={{0,1},{1,0},{2,3},{3,2},{4,5},{5,4},{6,7},{7,6},{8,9},{9,8},{10,11... | collective-permute-start | bytes 1179656 | tf_op jit(solution)/shard_map/ppermute | solution.py:374
  14.9 6.8 %collective-permute-done.4 = bf16[256,768]{1,0:T(8,128)(2,1)} collective-permute-done((bf16[256,768]{1,0:T(8,128)(2,1)}, bf16[256,768]{1,0:T(8,128)(2,1)}, u32[]{:S(2)}, u32[]{:S(2)}) %collective-permute-start.4) | collective-permute-done | bytes 393248 | tf_op jit(solution)/shard_map/ppermute | solution.py:374
  26.3 3.1 %collective-permute-start.2 = (bf16[8,64,512]{2,1,0:T(8,128)(2,1)S(1)}, bf16[8,64,512]{2,1,0:T(8,128)(2,1)S(1)}, u32[]{:S(2)}, u32[]{:S(2)}) collective-permute-start(bf16[8,64,512]{2,1,0:T(8,128)(2,1)S(1)} %slice.133), channel_id=1, source_target_pairs={{0,2},{2,4},{4,6},{6,8},{8,10},{10,12},{12,14},{14,16},{16,18},{18... | collective-permute-start | bytes 1572872 | tf_op jit(solution)/shard_map/ppermute | solution.py:379
  31.4 8.8 %attn_fwd_0.1 = (bf16[2,3,1024,768]{3,2,1,0:T(8,128)(2,1)}, bf16[16,64,512]{2,1,0:T(8,128)(2,1)}) custom-call(s32[192,1]{1,0:T(8,128)} %copy.40.idc, s32[3,256]{1,0:T(4,128)} %tile.12.idr, bf16[8,64,512]{2,1,0:T(8,128)(2,1)} %collective-permute-done.xp, bf16[16,64,512]{2,1,0:T(8,128)(2,1)} %xo.3, bf16[8,64,512]{2,1,0:T(8,128)(2,1)} %collective-permute-done.1.xn, ...), custom_call_target="tpu_custom_call" | custom-call | flops 3000000000 | bytes 12582912 | tf_op jit(solution)/shard_map/attn_fwd_0/pallas_call | solution.py:612
  41.2 8.8 %attn_fwd_1.1 = (bf16[2,3,1024,768]{3,2,1,0:T(8,128)(2,1)}, bf16[16,64,512]{2,1,0:T(8,128)(2,1)}) custom-call(s32[192,1]{1,0:T(8,128)} %copy.40.idc, s32[3,256]{1,0:T(4,128)} %tile.12.idr, bf16[8,64,512]{2,1,0:T(8,128)(2,1)} %copy-done.9, bf16[16,64,512]{2,1,0:T(8,128)(2,1)} %xo.3, ...), custom_call_target="tpu_custom_call", output_to_operand_aliasing={{0}: (9, {}), {1}: (10, {})} | custom-call | flops 3000000000 | bytes 12582912 | tf_op jit(solution)/shard_map/attn_fwd_1/pallas_call | solution.py:612
  55.2 35.2 %chain.1 = (bf16[1024,512]{1,0:T(8,128)(2,1)}, f32[1024,512]{1,0:T(8,128)}, bf16[1024,512]{1,0:T(8,128)(2,1)}, f32[1,512]{1,0:T(1,128)}, f32[1,512]{1,0:T(1,128)...) custom-call(s32[33]{0:T(128)} %pad_add_fusion.refs_0_.table, bf16[1024,512]{1,0:T(8,128)(2,1)} %bitcast.18, ...), custom_call_target="tpu_custom_call" | custom-call | flops 15000000512 | bytes 20971520 | tf_op jit(solution)/shard_map/chain/pallas_call | solution.py:654
  92.1 4.0 %collective-permute-start.8 = (bf16[16,64,512]{2,1,0:T(8,128)(2,1)}, bf16[16,64,512]{2,1,0:T(8,128)(2,1)}, u32[]{:S(2)}, u32[]{:S(2)}) collective-permute-start(bf16[16,64,512]{2,1,0:T(8,128)(2,1)} %bitcast.39), channel_id=1, source_target_pairs={{0,2},{2,4},{4,6},{6,8},{8,10},{10,12},{12,14},{14,16},{16,18},{18... | collective-permute-start | bytes 3145736 | tf_op jit(solution)/shard_map/ppermute | solution.py:379
  96.1 16.8 %attn_bwd_own.1 = (bf16[2,1024,256]{2,1,0:T(8,128)(2,1)}, f32[2,1024,512]{2,1,0:T(8,128)}) custom-call(s32[192,1]{1,0:T(8,128)} %copy.40.idc, s32[3,256]{1,0:T(4,128)} %tile.12.idr, bf16[2,3,1024,768]{3,2,1,0:T(8,128)(2,1)} %get-tuple-element.80.qkv_ref, bf16[16,64,512]{2,1,0:T(8,128)(2,1)} %bitcast.40), custom_call_target="tpu_custom_call" | custom-call | flops 10000000000 | bytes 14680064 | tf_op jit(solution)/shard_map/attn_bwd_own/pallas_call | solution.py:684
  115.2 23.2 %attn_bwd_near.1.dkv = bf16[2,1024,512]{2,1,0:T(8,128)(2,1)} custom-call(s32[192,1]{1,0:T(8,128)} %copy.40.idc, s32[3,256]{1,0:T(4,128)} %tile.12.idr, bf16[2,3,1024,768]{3,2,1,0:T(8,128)(2,1)} %get-tuple-element.80.qkv_ref, bf16[16,64,512]{2,1,0:T(8,128)(2,1)} %collective-permute-done.8.dp_ref, bf16[16,64,512]{2,1,0:T(8,128)(2,1)} %collective-permute-done.9.dn_ref, ...), custom_call_target="tpu_custom_call" | custom-call | flops 10000000000 | bytes 14680064 | tf_op jit(solution)/shard_map/attn_bwd_near/pallas_call | solution.py:698
  138.4 2.3 add_convert_fusion.1
  140.8 6.4 %collective-permute-start.12 = (bf16[576,512]{1,0:T(8,128)(2,1)}, bf16[576,512]{1,0:T(8,128)(2,1)}, u32[]{:S(2)}, u32[]{:S(2)}) collective-permute-start(bf16[576,512]{1,0:T(8,128)(2,1)} %add_convert_fusion.1), channel_id=1, source_target_pairs={{0,4},{1,5},{2,3},{3,2},{4,0},{5,1},{6,7},{7,6},{8,12},{9,13},{10,... | collective-permute-start | bytes 1769480 | tf_op jit(solution)/shard_map/ppermute | solution.py:451
  147.2 6.3 %qkv_grad.1 = (bf16[768,512]{1,0:T(8,128)(2,1)}, bf16[768,512]{1,0:T(8,128)(2,1)}) custom-call(s32[33]{0:T(128)} %pad_add_fusion.refs_0_.table, bf16[1024,512]{1,0:T(8,128)(2,1)} %bitcast.19, bf16[2,1024,256]{2,1,0:T(8,128)(2,1)} %get-tuple-element.82.dq, bf16[2,1024,512]{2,1,0:T(8,128)(2,1)} %attn_bwd_near.1.dkv, f32[1,512]{1,0:T(1,128)} %bitcast.27, ...), custom_call_target="tpu_custom_call" | custom-call | flops 2000000000 | bytes 6291456 | tf_op jit(solution)/shard_map/qkv_grad/pallas_call | solution.py:715
  158.4 5.1 %collective-permute-done.14 = bf16[288,512]{1,0:T(8,128)(2,1)S(1)} collective-permute-done((bf16[288,512]{1,0:T(8,128)(2,1)S(1)}, bf16[288,512]{1,0:T(8,128)(2,1)S(1)}, u32[]{:S(2)}, u32[]{:S(2)}) %collective-permute-start.14) | collective-permute-done | bytes 294944 | tf_op jit(solution)/shard_map/ppermute | solution.py:451
  166.5 2.7 %collective-permute-start.16 = (bf16[144,512]{1,0:T(8,128)(2,1)}, bf16[144,512]{1,0:T(8,128)(2,1)}, u32[]{:S(2)}, u32[]{:S(2)}) collective-permute-start(bf16[144,512]{1,0:T(8,128)(2,1)} %add_convert_fusion.6), channel_id=1, source_target_pairs={{0,16},{1,17},{2,18},{3,19},{4,20},{5,21},{6,22},{7,23},{8,24},{9,... | collective-permute-start | bytes 442376 | tf_op jit(solution)/shard_map/ppermute | solution.py:451
  169.7 7.0 %input_grad.1 = (f32[1024,512]{1,0:T(8,128)}, f32[1,512]{1,0:T(1,128)}, f32[1,512]{1,0:T(1,128)}) custom-call(bf16[1024,512]{1,0:T(8,128)(2,1)} %bitcast.20, f32[1024,512]{1,0:T(8,128)} %get-tuple-element.79.hgrad, bf16[2,1024,256]{2,1,0:T(8,128)(2,1)} %get-tuple-element.82.dq, bf16[2,1024,512]{2,1,0:T(8,128)(2,1)} %attn_bwd_near.1.dkv, ...), custom_call_target="tpu_custom_call" | custom-call | flops 2000000000 | bytes 8388608 | tf_op jit(solution)/shard_map/input_grad/pallas_call | solution.py:732
  183.5 5.3 %collective-permute-done.18 = bf16[144,512]{1,0:T(8,128)(2,1)S(1)} collective-permute-done((bf16[144,512]{1,0:T(8,128)(2,1)S(1)}, bf16[144,512]{1,0:T(8,128)(2,1)S(1)}, u32[]{:S(2)}, u32[]{:S(2)}) %collective-permute-start.18) | collective-permute-done | bytes 147488 | tf_op jit(solution)/shard_map/ppermute | solution.py:451
  201.7 3.2 %collective-permute-done.25 = f32[4,512]{1,0:T(4,128)S(1)} collective-permute-done((f32[4,512]{1,0:T(4,128)S(1)}, f32[4,512]{1,0:T(4,128)S(1)}, u32[]{:S(2)}, u32[]{:S(2)}) %collective-permute-start.25) | collective-permute-done | bytes 8224 | tf_op jit(solution)/shard_map/ppermute | solution.py:374
  211.5 3.0 %collective-permute-done.27 = f32[4,512]{1,0:T(4,128)S(1)} collective-permute-done((f32[4,512]{1,0:T(4,128)S(1)}, f32[4,512]{1,0:T(4,128)S(1)}, u32[]{:S(2)}, u32[]{:S(2)}) %collective-permute-start.27) | collective-permute-done | bytes 8224 | tf_op jit(solution)/shard_map/ppermute | solution.py:374
  215.5 3.7 %collective-permute-done.29 = bf16[96,512]{1,0:T(8,128)(2,1)S(1)} collective-permute-done((bf16[96,512]{1,0:T(8,128)(2,1)S(1)}, bf16[96,512]{1,0:T(8,128)(2,1)S(1)}, u32[]{:S(2)}, u32[]{:S(2)}) %collective-permute-start.29) | collective-permute-done | bytes 98336 | tf_op jit(solution)/shard_map/ppermute | solution.py:451
  221.4 3.6 %collective-permute-done.30 = bf16[192,512]{1,0:T(8,128)(2,1)S(1)} collective-permute-done((bf16[192,512]{1,0:T(8,128)(2,1)S(1)}, bf16[192,512]{1,0:T(8,128)(2,1)S(1)}, u32[]{:S(2)}, u32[]{:S(2)}) %collective-permute-start.30) | collective-permute-done | bytes 196640 | tf_op jit(solution)/shard_map/ppermute | solution.py:451
  226.2 4.6 %ffn_out.1 = (f32[512,1024]{1,0:T(8,128)}, f32[1024,512]{1,0:T(8,128)}, f32[256,512]{1,0:T(8,128)}) custom-call(s32[16]{0:T(128)} %pad_add_fusion.1.table, bf16[1152,512]{1,0:T(8,128)(2,1)} %copy-done.2, bf16[1152,512]{1,0:T(8,128)(2,1)} %copy-done.5), custom_call_target="tpu_custom_call" | custom-call | bytes 8388608 | tf_op jit(solution)/shard_map/ffn_out/pallas_call | solution.py:752
  231.4 3.1 %collective-permute-done.28 = f32[4,512]{1,0:T(4,128)S(1)} collective-permute-done((f32[4,512]{1,0:T(4,128)S(1)}, f32[4,512]{1,0:T(4,128)S(1)}, u32[]{:S(2)}, u32[]{:S(2)}) %collective-permute-start.28) | collective-permute-done | bytes 8224 | tf_op jit(solution)/shard_map/ppermute | solution.py:374
  235.9 2.8 %qkv_out.1 = f32[3,512,256]{2,1,0:T(8,128)} custom-call(s32[16]{0:T(128)} %pad_add_fusion.1.table, bf16[384,512]{1,0:T(8,128)(2,1)} %copy-done.4, bf16[384,512]{1,0:T(8,128)(2,1)} %copy-done.10), custom_call_target="tpu_custom_call" | custom-call | bytes 3145728 | tf_op jit(solution)/shard_map/qkv_out/pallas_call | solution.py:769
  (139 shorter events, 64.7 us)
Async XLA Ops:
  3.4 21.5 %collective-permute-start.1 = (bf16[8,64,512]{2,1,0:T(8,128)(2,1)S(1)}, bf16[8,64,512]{2,1,0:T(8,128)(2,1)}, u32[]{:S(2)}, u32[]{:S(2)}) collective-permute-start(bf16[8,64,512]{2,1,0:T(8,128)(2,1)S(1)} %slice.132), channel_id=1, source_target_pairs={{2,0},{4,2},{6,4},{8,6},{10,8},{12,10},{14,12},{16,14},{18,16},{20... | collective-permute-start | bytes 1572872 | tf_op jit(solution)/shard_map/ppermute | solution.py:380
  4.7 20.2 %collective-permute-start = (bf16[8,64,512]{2,1,0:T(8,128)(2,1)S(1)}, bf16[8,64,512]{2,1,0:T(8,128)(2,1)}, u32[]{:S(2)}, u32[]{:S(2)}) collective-permute-start(bf16[8,64,512]{2,1,0:T(8,128)(2,1)S(1)} %slice.132), channel_id=1, source_target_pairs={{0,2},{2,4},{4,6},{6,8},{8,10},{10,12},{12,14},{14,16},{16,18},{18... | collective-permute-start | bytes 1572872 | tf_op jit(solution)/shard_map/ppermute | solution.py:379
  8.5 13.2 %collective-permute-start.4 = (bf16[256,768]{1,0:T(8,128)(2,1)}, bf16[256,768]{1,0:T(8,128)(2,1)}, u32[]{:S(2)}, u32[]{:S(2)}) collective-permute-start(bf16[256,768]{1,0:T(8,128)(2,1)} %constant_dynamic-slice_fusion.3), channel_id=1, source_target_pairs={{0,1},{1,0},{2,3},{3,2},{4,5},{5,4},{6,7},{7,6},{8,9},{9,8},{10,11... | collective-permute-start | bytes 1179656 | tf_op jit(solution)/shard_map/ppermute | solution.py:374
  21.7 7.6 %collective-permute-start.5 = (bf16[256,768]{1,0:T(8,128)(2,1)}, bf16[256,768]{1,0:T(8,128)(2,1)S(1)}, u32[]{:S(2)}, u32[]{:S(2)}) collective-permute-start(bf16[256,768]{1,0:T(8,128)(2,1)} %collective-permute-done.4), channel_id=1, source_target_pairs={{0,2},{2,0},{4,6},{6,4},{8,10},{10,8},{12,14},{14,12},{16,18},{18,... | collective-permute-start | bytes 1179656 | tf_op jit(solution)/shard_map/ppermute | solution.py:374
  21.8 28.6 %collective-permute-start.6 = (bf16[1152,512]{1,0:T(8,128)(2,1)}, bf16[1152,512]{1,0:T(8,128)(2,1)}, u32[]{:S(2)}, u32[]{:S(2)}) collective-permute-start(bf16[1152,512]{1,0:T(8,128)(2,1)} %pad_maximum_fusion), channel_id=1, source_target_pairs={{0,1},{1,0},{2,3},{3,2},{4,5},{5,4},{6,7},{7,6},{8,9},{9,8},{10,11... | collective-permute-start | bytes 3538952 | tf_op jit(solution)/shard_map/ppermute | solution.py:374
  25.0 15.2 %collective-permute-start.3 = (bf16[8,64,512]{2,1,0:T(8,128)(2,1)S(1)}, bf16[8,64,512]{2,1,0:T(8,128)(2,1)S(1)}, u32[]{:S(2)}, u32[]{:S(2)}) collective-permute-start(bf16[8,64,512]{2,1,0:T(8,128)(2,1)S(1)} %slice.133), channel_id=1, source_target_pairs={{2,0},{4,2},{6,4},{8,6},{10,8},{12,10},{14,12},{16,14},{18,16},{20... | collective-permute-start | bytes 1572872 | tf_op jit(solution)/shard_map/ppermute | solution.py:380
  26.3 13.9 %collective-permute-start.2 = (bf16[8,64,512]{2,1,0:T(8,128)(2,1)S(1)}, bf16[8,64,512]{2,1,0:T(8,128)(2,1)S(1)}, u32[]{:S(2)}, u32[]{:S(2)}) collective-permute-start(bf16[8,64,512]{2,1,0:T(8,128)(2,1)S(1)} %slice.133), channel_id=1, source_target_pairs={{0,2},{2,4},{4,6},{6,8},{8,10},{10,12},{12,14},{14,16},{16,18},{18... | collective-permute-start | bytes 1572872 | tf_op jit(solution)/shard_map/ppermute | solution.py:379
  90.4 22.5 %collective-permute-start.10 = (bf16[2304,512]{1,0:T(8,128)(2,1)}, bf16[2304,512]{1,0:T(8,128)(2,1)}, u32[]{:S(2)}, u32[]{:S(2)}) collective-permute-start(bf16[2304,512]{1,0:T(8,128)(2,1)} %get-tuple-element.85), channel_id=1, source_target_pairs={{0,2},{2,0},{4,6},{6,4},{8,10},{10,8},{12,14},{14,12},{16,18},{18,... | collective-permute-start | bytes 7077896 | tf_op jit(solution)/shard_map/ppermute | solution.py:374
  90.8 24.4 %collective-permute-start.9 = (bf16[16,64,512]{2,1,0:T(8,128)(2,1)}, bf16[16,64,512]{2,1,0:T(8,128)(2,1)}, u32[]{:S(2)}, u32[]{:S(2)}) collective-permute-start(bf16[16,64,512]{2,1,0:T(8,128)(2,1)} %bitcast.38), channel_id=1, source_target_pairs={{2,0},{4,2},{6,4},{8,6},{10,8},{12,10},{14,12},{16,14},{18,16},{20... | collective-permute-start | bytes 3145736 | tf_op jit(solution)/shard_map/ppermute | solution.py:380
  92.1 23.1 %collective-permute-start.8 = (bf16[16,64,512]{2,1,0:T(8,128)(2,1)}, bf16[16,64,512]{2,1,0:T(8,128)(2,1)}, u32[]{:S(2)}, u32[]{:S(2)}) collective-permute-start(bf16[16,64,512]{2,1,0:T(8,128)(2,1)} %bitcast.39), channel_id=1, source_target_pairs={{0,2},{2,4},{4,6},{6,8},{8,10},{10,12},{12,14},{14,16},{16,18},{18... | collective-permute-start | bytes 3145736 | tf_op jit(solution)/shard_map/ppermute | solution.py:379
  114.5 23.9 %collective-permute-start.11 = (bf16[1152,512]{1,0:T(8,128)(2,1)S(1)}, bf16[1152,512]{1,0:T(8,128)(2,1)}, u32[]{:S(2)}, u32[]{:S(2)}) collective-permute-start(bf16[1152,512]{1,0:T(8,128)(2,1)S(1)} %add_convert_fusion), channel_id=1, source_target_pairs={{0,1},{1,0},{2,10},{3,11},{4,5},{5,4},{6,14},{7,15},{8,9},{9,8},{1... | collective-permute-start | bytes 3538952 | tf_op jit(solution)/shard_map/ppermute | solution.py:451
  140.8 14.6 %collective-permute-start.12 = (bf16[576,512]{1,0:T(8,128)(2,1)}, bf16[576,512]{1,0:T(8,128)(2,1)}, u32[]{:S(2)}, u32[]{:S(2)}) collective-permute-start(bf16[576,512]{1,0:T(8,128)(2,1)} %add_convert_fusion.1), channel_id=1, source_target_pairs={{0,4},{1,5},{2,3},{3,2},{4,0},{5,1},{6,7},{7,6},{8,12},{9,13},{10,... | collective-permute-start | bytes 1769480 | tf_op jit(solution)/shard_map/ppermute | solution.py:451
  156.6 8.8 %collective-permute-start.13 = (bf16[768,512]{1,0:T(8,128)(2,1)}, bf16[768,512]{1,0:T(8,128)(2,1)}, u32[]{:S(2)}, u32[]{:S(2)}) collective-permute-start(bf16[768,512]{1,0:T(8,128)(2,1)} %get-tuple-element.95), channel_id=1, source_target_pairs={{0,2},{2,0},{4,6},{6,4},{8,10},{10,8},{12,14},{14,12},{16,18},{18,... | collective-permute-start | bytes 2359304 | tf_op jit(solution)/shard_map/ppermute | solution.py:374
  156.7 6.8 %collective-permute-start.14 = (bf16[288,512]{1,0:T(8,128)(2,1)S(1)}, bf16[288,512]{1,0:T(8,128)(2,1)S(1)}, u32[]{:S(2)}, u32[]{:S(2)}) collective-permute-start(bf16[288,512]{1,0:T(8,128)(2,1)S(1)} %add_convert_fusion.3), channel_id=1, source_target_pairs={{0,8},{1,9},{2,6},{3,7},{4,12},{5,13},{6,2},{7,3},{8,0},{9,1},{10,... | collective-permute-start | bytes 884744 | tf_op jit(solution)/shard_map/ppermute | solution.py:451
  166.5 10.9 %collective-permute-start.16 = (bf16[144,512]{1,0:T(8,128)(2,1)}, bf16[144,512]{1,0:T(8,128)(2,1)}, u32[]{:S(2)}, u32[]{:S(2)}) collective-permute-start(bf16[144,512]{1,0:T(8,128)(2,1)} %add_convert_fusion.6), channel_id=1, source_target_pairs={{0,16},{1,17},{2,18},{3,19},{4,20},{5,21},{6,22},{7,23},{8,24},{9,... | collective-permute-start | bytes 442376 | tf_op jit(solution)/shard_map/ppermute | solution.py:451
  169.2 9.6 %collective-permute-start.15 = (bf16[384,512]{1,0:T(8,128)(2,1)S(1)}, bf16[384,512]{1,0:T(8,128)(2,1)}, u32[]{:S(2)}, u32[]{:S(2)}) collective-permute-start(bf16[384,512]{1,0:T(8,128)(2,1)S(1)} %add_convert_fusion.2), channel_id=1, source_target_pairs={{0,1},{1,0},{2,10},{3,11},{4,5},{5,4},{6,14},{7,15},{8,9},{9,8},{1... | collective-permute-start | bytes 1179656 | tf_op jit(solution)/shard_map/ppermute | solution.py:451
  179.9 8.9 %collective-permute-start.18 = (bf16[144,512]{1,0:T(8,128)(2,1)S(1)}, bf16[144,512]{1,0:T(8,128)(2,1)S(1)}, u32[]{:S(2)}, u32[]{:S(2)}) collective-permute-start(bf16[144,512]{1,0:T(8,128)(2,1)S(1)} %add_convert_fusion.5), channel_id=1, source_target_pairs={{0,16},{1,17},{2,18},{3,19},{4,20},{5,21},{6,22},{7,23},{8,24},{9,... | collective-permute-start | bytes 442376 | tf_op jit(solution)/shard_map/ppermute | solution.py:451
  180.3 8.6 %collective-permute-start.17 = (bf16[192,512]{1,0:T(8,128)(2,1)S(1)}, bf16[192,512]{1,0:T(8,128)(2,1)S(1)}, u32[]{:S(2)}, u32[]{:S(2)}) collective-permute-start(bf16[192,512]{1,0:T(8,128)(2,1)S(1)} %add_convert_fusion.4), channel_id=1, source_target_pairs={{0,4},{1,5},{2,3},{3,2},{4,0},{5,1},{6,7},{7,6},{8,12},{9,13},{10,... | collective-permute-start | bytes 589832 | tf_op jit(solution)/shard_map/ppermute | solution.py:451
  189.9 5.8 %collective-permute-start.20 = (bf16[96,512]{1,0:T(8,128)(2,1)S(1)}, bf16[96,512]{1,0:T(8,128)(2,1)S(1)}, u32[]{:S(2)}, u32[]{:S(2)}) collective-permute-start(bf16[96,512]{1,0:T(8,128)(2,1)S(1)} %add_convert_fusion.7), channel_id=1, source_target_pairs={{0,8},{1,9},{2,6},{3,7},{4,12},{5,13},{6,2},{7,3},{8,0},{9,1},{10,... | collective-permute-start | bytes 294920 | tf_op jit(solution)/shard_map/ppermute | solution.py:451
  189.9 7.8 %collective-permute-start.21 = (bf16[288,512]{1,0:T(8,128)(2,1)S(1)}, bf16[288,512]{1,0:T(8,128)(2,1)S(1)}, u32[]{:S(2)}, u32[]{:S(2)}) collective-permute-start(bf16[288,512]{1,0:T(8,128)(2,1)S(1)} %pad_maximum_fusion.5), channel_id=1, source_target_pairs={{0,8},{1,9},{2,6},{3,7},{4,12},{5,13},{6,2},{7,3},{8,0},{9,1},{10,... | collective-permute-start | bytes 884744 | tf_op jit(solution)/shard_map/ppermute | solution.py:451
  197.8 9.9 %collective-permute-start.24 = (bf16[576,512]{1,0:T(8,128)(2,1)S(1)}, bf16[576,512]{1,0:T(8,128)(2,1)S(1)}, u32[]{:S(2)}, u32[]{:S(2)}) collective-permute-start(bf16[576,512]{1,0:T(8,128)(2,1)S(1)} %pad_maximum_fusion.3), channel_id=1, source_target_pairs={{0,4},{1,5},{2,10},{3,11},{4,0},{5,1},{6,14},{7,15},{8,12},{9,13},... | collective-permute-start | bytes 1769480 | tf_op jit(solution)/shard_map/ppermute | solution.py:451
  207.8 17.3 %collective-permute-start.31 = (bf16[1152,512]{1,0:T(8,128)(2,1)S(1)}, bf16[1152,512]{1,0:T(8,128)(2,1)S(1)}, u32[]{:S(2)}, u32[]{:S(2)}) collective-permute-start(bf16[1152,512]{1,0:T(8,128)(2,1)S(1)} %pad_maximum_fusion.1.mine), channel_id=1, source_target_pairs={{0,2},{2,0},{4,6},{6,4},{8,10},{10,8},{12,14},{14,12},{16,18},{18,... | collective-permute-start | bytes 3538952 | tf_op jit(solution)/shard_map/ppermute | solution.py:374
  208.6 5.9 %collective-permute-start.26 = (bf16[48,512]{1,0:T(8,128)(2,1)S(1)}, bf16[48,512]{1,0:T(8,128)(2,1)S(1)}, u32[]{:S(2)}, u32[]{:S(2)}) collective-permute-start(bf16[48,512]{1,0:T(8,128)(2,1)S(1)} %add_convert_fusion.8), channel_id=1, source_target_pairs={{0,16},{1,17},{2,18},{3,19},{4,20},{5,21},{6,22},{7,23},{8,24},{9,... | collective-permute-start | bytes 147464 | tf_op jit(solution)/shard_map/ppermute | solution.py:451
  219.3 5.7 %collective-permute-start.30 = (bf16[192,512]{1,0:T(8,128)(2,1)S(1)}, bf16[192,512]{1,0:T(8,128)(2,1)S(1)}, u32[]{:S(2)}, u32[]{:S(2)}) collective-permute-start(bf16[192,512]{1,0:T(8,128)(2,1)S(1)} %pad_maximum_fusion.6), channel_id=1, source_target_pairs={{0,4},{1,5},{2,10},{3,11},{4,0},{5,1},{6,14},{7,15},{8,12},{9,13},... | collective-permute-start | bytes 589832 | tf_op jit(solution)/shard_map/ppermute | solution.py:451
  (31 other events, 223.6 us)

commit v5 on v4

--- a/solution.py
+++ b/solution.py
@@ -17,7 +17,6 @@
 BF16 = jnp.bfloat16
 NEG = -1e30
 CHUNK = 256
-UNROLL = 4
 
 
 def dot_nn(a, b):
@@ -59,23 +58,36 @@
     return jnp.concatenate([rows * m for m in masks], axis=0)
 
 
-def pick_heads(full, masks, rows):
-    out = full[0:rows] * masks[0]
-    for h in range(1, HEADS_PER_GROUP):
-        out = out + full[h * rows : (h + 1) * rows] * masks[h]
-    return out
+def pick_heads(full, rows):
+    low = lax.broadcasted_iota(jnp.int32, (rows, 2 * HEAD_DIM), 1) < HEAD_DIM
+    out = []
+    for pair in range(HEADS_PER_GROUP // 2):
+        cols = slice(2 * pair * HEAD_DIM, 2 * (pair + 1) * HEAD_DIM)
+        at = 2 * pair * rows
+        out.append(jnp.where(low, full[at : at + rows, cols], full[at + rows : at + 2 * rows, cols]))
+    return jnp.concatenate(out, axis=1)
 
 
 def rows_at(index, size):
     return pl.ds(pl.multiple_of(index * size, size), size)
 
 
+def staged(count, first, second, third, lag=2):
+    a, b = {}, {}
+    for t in range(count + lag):
+        if t < count:
+            a[t] = first(t)
+        if 0 <= t - 1 < count:
+            b[t - 1] = second(t - 1, *a.pop(t - 1))
+        if 0 <= t - lag < count:
+            third(t - lag, *b.pop(t - lag))
+
+
 def each(count, body, unroll=1):
     lax.fori_loop(0, count, lambda i, carry: (body(i), carry)[1], 0, unroll=unroll)
 
 
-def attn_fwd_kernel(idc, idr, xp, xo, xn, w0, w1, gain, shift, *rest):
-    qkv_ref, att_ref = rest[-2:]
+def attn_fwd_kernel(idc, idr, xp, xo, xn, w0, w1, gain, shift, qkv_ref, att_ref):
     feats, samp, width = xo.shape
     rows = feats * samp
     x = jnp.concatenate(
@@ -89,28 +101,28 @@
         qkv_ref[hg] = qkv.reshape(3, rows, 3 * GROUP_COLS)
     allowed = idc[...] == idr[1:2, :]
     m16 = lane_head(1, BF16)
-    m32 = lane_head(1, F32)
-
-    def column(f):
-        sl = rows_at(f, samp)
-        for hg in range(2):
-            q = qkv_ref[hg, 1, sl, 0:GROUP_COLS]
-            k = jnp.concatenate(
-                [qkv_ref[hg, w, sl, GROUP_COLS : 2 * GROUP_COLS] for w in range(3)], axis=0
-            )
-            v = jnp.concatenate(
-                [qkv_ref[hg, w, sl, 2 * GROUP_COLS : 3 * GROUP_COLS] for w in range(3)], axis=0
-            )
-            s = dot_nt(k, block_diag(q, m16)) * SCALE
-            s = jnp.where(allowed, s, NEG)
-            top = jnp.max(s, axis=0, keepdims=True)
-            e = jnp.exp(s - top)
-            total = jnp.sum(e, axis=0, keepdims=True)
-            p = (e * (1.0 / total)).astype(BF16)
-            o = pick_heads(dot_tn(p, v), m32, samp)
-            att_ref[f, :, hg * GROUP_COLS : (hg + 1) * GROUP_COLS] = o.astype(BF16)
-
-    each(feats, column, UNROLL)
+    q16 = [m * SCALE for m in m16]
+
+    def first(i):
+        f, hg = i // 2, i % 2
+        sl = slice(f * samp, (f + 1) * samp)
+        k, _ = bwd_pieces(qkv_ref, hg, sl)
+        return (dot_nt(k, block_diag(qkv_ref[hg, 1, sl, 0:GROUP_COLS], q16)),)
+
+    def second(i, s):
+        s = jnp.where(allowed, s, NEG)
+        top = jnp.max(s, axis=0, keepdims=True)
+        e = jnp.exp(s - top)
+        total = jnp.sum(e, axis=0, keepdims=True)
+        return ((e * (1.0 / total)).astype(BF16),)
+
+    def third(i, p):
+        f, hg = i // 2, i % 2
+        _, v = bwd_pieces(qkv_ref, hg, slice(f * samp, (f + 1) * samp))
+        o = pick_heads(dot_tn(p, v), samp)
+        att_ref[f, :, hg * GROUP_COLS : (hg + 1) * GROUP_COLS] = o.astype(BF16)
+
+    staged(2 * feats, first, second, third, 1)
 
 
 def phi_parts(u):
@@ -136,9 +148,13 @@
     count = 2 if ordered else 3
     out_ref, hgrad_ref, dat_ref, g2_ref, s2_ref = refs[:5]
     packed, refs = refs[5 : 5 + count], refs[5 + count :]
-    (wo, upb, downb, hidden, normed, mlp, dn2, act, pre, res, gd, gu, go) = refs
+    (wo, up_a, down_a, up_b, down_b, hidden, normed, mlp, dn2) = refs[:9]
+    act_a, pre_a, act_b, pre_b, res, gd, gu, go = refs[9:]
     tokens, width = x.shape
-    slot = upb.shape[1]
+    unit = up_a.shape[1]
+    slot = up_own.shape[1] // 2
+    per = slot // unit
+    last = (2 * others + 2) * per // 2
     narrow_rows = out_own.shape[0]
     half_rows = narrow_rows // 2
     chunks = tokens // CHUNK
@@ -157,6 +173,8 @@
             wo[rows_at(base, half_rows)] = packs[i][2 * slot : 2 * slot + half_rows] if inpack else packs[i][slot : slot + half_rows]
         g2_ref[...] = jnp.zeros_like(g2_ref)
         s2_ref[...] = jnp.zeros_like(s2_ref)
+        for ref in (act_b, pre_b, up_b, down_b):
+            ref[...] = jnp.zeros_like(ref)
 
         def start(i):
             sl = rows_at(i, CHUNK)
@@ -169,40 +187,78 @@
 
         each(chunks, start)
 
-    for i in range(2 * others + 2):
-
-        @pl.when(step == i)
-        def _(i=i):
-            if i < 2:
-                upb[...] = up_own[:, i * slot : (i + 1) * slot]
-                downb[...] = down_own[i * slot : (i + 1) * slot]
-            elif inpack:
-                upb[...] = packs[i - 2][:slot]
-                downb[...] = packs[i - 2][slot : 2 * slot]
-            else:
-                upb[...] = extra[i - 2][...]
-                downb[...] = packs[i - 2][:slot]
-
-    def tokens_of(i):
-        sl = rows_at(i, CHUNK)
-        u = dot_nn(normed[sl], upb[...])
-        cdf, upd = phi_parts(u)
-        a = (u * cdf).astype(BF16)
-        act[sl] = a
-        p = (dot_nt(cot[sl], downb[...]) * (cdf + upd)).astype(BF16)
-        pre[sl] = p
-        mlp[sl] += dot_nn(a, downb[...])
-        dn2[sl] += dot_nt(p, upb[...])
-
-    each(chunks, tokens_of)
-    swapped = jnp.where(step % 2 == 0, core, 1 - core)
-    base = jnp.where(step < 2, step, step - step % 2 + swapped)
-    at = rows_at(base, slot)
-    gd[at] = dot_tn(act[...], cot[...]).astype(BF16)
-    gu[at] = dot_tn(pre[...], normed[...]).astype(BF16)
-
-    @pl.when(step == 2 * others + 1)
+    def load(parity, up, down):
+        for pair in range(last):
+
+            @pl.when(step == pair)
+            def _():
+                i, sub = divmod(2 * pair + parity, per)
+                low, high = sub * unit, (sub + 1) * unit
+                if i < 2:
+                    low, high = low + i * slot, high + i * slot
+                    up[...] = up_own[:, low:high]
+                    down[...] = down_own[low:high]
+                elif inpack:
+                    up[...] = packs[i - 2][:slot, low:high]
+                    down[...] = packs[i - 2][slot + low : slot + high]
+                else:
+                    up[...] = extra[i - 2][:, low:high]
+                    down[...] = packs[i - 2][low:high]
+
+    def place(item):
+        i, sub = item // per, item % per
+        swapped = jnp.where(i % 2 == 0, core, 1 - core)
+        base = jnp.where(i < 2, i, i - i % 2 + swapped)
+        return rows_at(base * per + sub, unit)
+
+    def spread(item, up, down, act, pre):
+        at = place(item)
+        half = width // 2
+        for i in range(chunks):
+            sl = slice(i * CHUNK, (i + 1) * CHUNK)
+            mlp[sl] += dot_nn(act[sl], down[...])
+            dn2[sl] += dot_nt(pre[sl], up[...])
+            for j in range(i, 4, chunks):
+                cols = slice((j % 2) * half, (j % 2 + 1) * half)
+                if j < 2:
+                    gd[at, cols] = dot_tn(act[...], cot[:, cols]).astype(BF16)
+                else:
+                    gu[at, cols] = dot_tn(pre[...], normed[:, cols]).astype(BF16)
+            yield
+
+    def phase(up, down, act, pre, *before):
+        rest = spread(*before)
+        ready = {}
+        for i in range(chunks + 1):
+            if i < chunks:
+                sl = slice(i * CHUNK, (i + 1) * CHUNK)
+                ready[i] = dot_nn(normed[sl], up[...]), dot_nt(cot[sl], down[...])
+            if i > 0:
+                next(rest)
+                u, back = ready.pop(i - 1)
+                sl = slice((i - 1) * CHUNK, i * CHUNK)
+                cdf, upd = phi_parts(u)
+                act[sl] = (u * cdf).astype(BF16)
+                pre[sl] = (back * (cdf + upd)).astype(BF16)
+
+    load(0, up_a, down_a)
+
+    @pl.when(step < last)
     def _():
+        before = jnp.maximum(2 * step - 1, 0)
+        phase(up_a, down_a, act_a, pre_a, before, up_b, down_b, act_b, pre_b)
+
+    load(1, up_b, down_b)
+
+    @pl.when(step < last)
+    def _():
+        phase(up_b, down_b, act_b, pre_b, 2 * step, up_a, down_a, act_a, pre_a)
+
+    @pl.when(step == last)
+    def _():
+        for _ in spread(2 * last - 1, up_b, down_b, act_b, pre_b):
+            pass
+
         def finish(i):
             sl = rows_at(i, CHUNK)
             h = hidden[sl]
@@ -247,14 +303,19 @@
     return k, v
 
 
-def score_grads(ks, vs, qbd, dbd, mask):
-    s = dot_nt(ks, qbd) * SCALE
+def head_rows(a):
+    return jnp.concatenate(
+        [a[:, h * HEAD_DIM : (h + 1) * HEAD_DIM] for h in range(HEADS_PER_GROUP)], axis=0
+    )
+
+
+def score_grads(s, dp, mask):
     s = jnp.where(mask, s, NEG)
     top = jnp.max(s, axis=0, keepdims=True)
     e = jnp.exp(s - top)
     total = jnp.sum(e, axis=0, keepdims=True)
     p = e * (1.0 / total)
-    pd = p * dot_nt(vs, dbd)
+    pd = p * dp
     delta = jnp.sum(pd, axis=0, keepdims=True)
     return (pd - p * delta).astype(BF16), p
 
@@ -262,48 +323,79 @@
 def attn_bwd_own_kernel(idc, idr, qkv_ref, do_ref, dq_ref, dkv_ref):
     feats, samp, width = do_ref.shape
     m16 = lane_head(1, BF16)
-    m32 = lane_head(1, F32)
+    q16 = [m * SCALE for m in m16]
     mask = idc[...] == idr[1:2, :]
 
-    def column(f):
-        sl = rows_at(f, samp)
-        for hg in range(2):
-            k, v = bwd_pieces(qkv_ref, hg, sl)
-            qbd = block_diag(qkv_ref[hg, 1, sl, 0:GROUP_COLS], m16)
-            dbd = block_diag(do_ref[f, :, hg * GROUP_COLS : (hg + 1) * GROUP_COLS], m16)
-            ds, p = score_grads(k, v, qbd, dbd, mask)
-            dq = pick_heads(dot_tn(ds, k), m32, samp)
-            dq_ref[hg, sl, :] = (dq * SCALE).astype(BF16)
-            dkv_ref[hg, sl, 0:GROUP_COLS] = dot_nn(ds[samp : 2 * samp], qbd)
-            dkv_ref[hg, sl, GROUP_COLS : 2 * GROUP_COLS] = dot_nn(p[samp : 2 * samp].astype(BF16), dbd)
-
-    each(feats, column, UNROLL)
-
-
-def attn_bwd_near_kernel(idc, idr, qkv_ref, dp_ref, dn_ref, sum_ref, dkv_ref):
+    def pieces(i):
+        f, hg = i // 2, i % 2
+        sl = slice(f * samp, (f + 1) * samp)
+        q = qkv_ref[hg, 1, sl, 0:GROUP_COLS]
+        d = do_ref[f, :, hg * GROUP_COLS : (hg + 1) * GROUP_COLS]
+        return hg, sl, q, d
+
+    def first(i):
+        hg, sl, q, d = pieces(i)
+        k, v = bwd_pieces(qkv_ref, hg, sl)
+        return dot_nt(k, block_diag(q, q16)), dot_nt(v, block_diag(d, m16))
+
+    def second(i, s, dp):
+        ds, p = score_grads(s, dp, mask)
+        own = slice(samp, 2 * samp)
+        return ds, head_rows(ds[own]), head_rows(p[own].astype(BF16))
+
+    def third(i, ds, dss, ps):
+        hg, sl, q, d = pieces(i)
+        k, _ = bwd_pieces(qkv_ref, hg, sl)
+        dq_ref[hg, sl, :] = (pick_heads(dot_tn(ds, k), samp) * SCALE).astype(BF16)
+        dkv_ref[hg, sl, 0:GROUP_COLS] = pick_heads(dot_nn(dss, q), samp)
+        dkv_ref[hg, sl, GROUP_COLS : 2 * GROUP_COLS] = pick_heads(dot_nn(ps, d), samp)
+
+    staged(2 * feats, first, second, third)
+
+
+def attn_bwd_near_kernel(idc, idr, qkv_ref, dp_ref, dn_ref, sum_ref, *rest):
+    dkv_ref = rest[-1]
     feats, samp, width = dp_ref.shape
     m16 = lane_head(1, BF16)
+    q16 = [m * SCALE for m in m16]
     near = ((0, 0, dp_ref), (2, 1, dn_ref))
     masks = [idc[a * samp : (a + 2) * samp, :] == idr[g : g + 1, :] for g, a, _ in near]
 
-    def column(f):
-        sl = rows_at(f, samp)
-        for hg in range(2):
+    def pieces(i, side):
+        f, hg = i // 2, i % 2
+        sl = slice(f * samp, (f + 1) * samp)
+        g, a, ref = near[side]
+        q = qkv_ref[hg, g, sl, 0:GROUP_COLS]
+        d = ref[f, :, hg * GROUP_COLS : (hg + 1) * GROUP_COLS]
+        return hg, sl, slice(a * samp, (a + 2) * samp), q, d
+
+    def first(i):
+        out = []
+        for side in range(2):
+            hg, sl, span, q, d = pieces(i, side)
             k, v = bwd_pieces(qkv_ref, hg, sl)
-            dk = sum_ref[hg, sl, 0:GROUP_COLS]
-            dv = sum_ref[hg, sl, GROUP_COLS : 2 * GROUP_COLS]
-            for mask, (g, a, ref) in zip(masks, near):
-                span = slice(a * samp, (a + 2) * samp)
-                qbd = block_diag(qkv_ref[hg, g, sl, 0:GROUP_COLS], m16)
-                dbd = block_diag(ref[f, :, hg * GROUP_COLS : (hg + 1) * GROUP_COLS], m16)
-                ds, p = score_grads(k[span], v[span], qbd, dbd, mask)
-                own = slice((1 - a) * samp, (2 - a) * samp)
-                dk = dk + dot_nn(ds[own], qbd)
-                dv = dv + dot_nn(p[own].astype(BF16), dbd)
-            dkv_ref[hg, sl, 0:GROUP_COLS] = (dk * SCALE).astype(BF16)
-            dkv_ref[hg, sl, GROUP_COLS : 2 * GROUP_COLS] = dv.astype(BF16)
-
-    each(feats, column, UNROLL)
+            out += [dot_nt(k[span], block_diag(q, q16)), dot_nt(v[span], block_diag(d, m16))]
+        return out
+
+    def second(i, s0, dp0, s1, dp1):
+        dss, ps = [], []
+        for side, (s, dp) in enumerate(((s0, dp0), (s1, dp1))):
+            ds, p = score_grads(s, dp, masks[side])
+            own = slice((1 - side) * samp, (2 - side) * samp)
+            dss.append(head_rows(ds[own]))
+            ps.append(head_rows(p[own].astype(BF16)))
+        return jnp.concatenate(dss, axis=1), jnp.concatenate(ps, axis=1)
+
+    def third(i, dss, ps):
+        hg, sl, _, q0, d0 = pieces(i, 0)
+        _, _, _, q1, d1 = pieces(i, 1)
+        low, high = slice(0, GROUP_COLS), slice(GROUP_COLS, 2 * GROUP_COLS)
+        dk = pick_heads(dot_nn(dss, jnp.concatenate([q0, q1], axis=0)), samp)
+        dv = pick_heads(dot_nn(ps, jnp.concatenate([d0, d1], axis=0)), samp)
+        dkv_ref[hg, sl, low] = ((dk + sum_ref[hg, sl, low]) * SCALE).astype(BF16)
+        dkv_ref[hg, sl, high] = (dv + sum_ref[hg, sl, high]).astype(BF16)
+
+    staged(2 * feats, first, second, third)
 
 
 def qkv_grad_kernel(ordered, table, x, dq, dkv, gain, shift, *refs):
@@ -396,12 +488,12 @@
 
 class Plan:
 
-    def __init__(self, wide, narrow):
-        self.wide, self.narrow = wide, narrow
+    def __init__(self, wide, narrow, fours=False):
+        self.wide, self.narrow, self.fours = wide, narrow, fours
         nb = [("narrow", 1 << i) for i in range(narrow.bit_length() - 1)][::-1]
         wb = [("wide", 1 << i) for i in range(1, wide.bit_length() - 1)]
         first = nb + wb
-        second = wb[1:2] + nb + wb[:1] + wb[2:]
+        second = wb[:1] + nb + wb[1:] if fours else wb[1:2] + nb + wb[:1] + wb[2:]
         self.orders = (first, second)
         self.steps = len(first)
         self.blocks = 1 << self.steps
@@ -454,8 +546,9 @@
 class Reduction:
 
     def __init__(self, plan, mine, send):
-        self.plan, self.parts, self.operand, self.at = plan, [mine], send, 0
+        self.plan, self.parts, self.operands, self.at = plan, [mine], [send], 0
         self.rows = mine.shape[0]
+        self.work = self.stages()
 
     def total(self, low, high):
         out = self.parts[0][low:high].astype(F32)
@@ -463,54 +556,66 @@
             out = out + p[low:high].astype(F32)
         return out.astype(BF16)
 
+    def around(self, operands):
+        (_, high), (_, low) = self.plan.orders[0][-2:]
+        bits = [low, high, high + low]
+        return [swap(o, "wide", b) for o, b in zip(operands, bits)]
+
+    def stages(self):
+        plan, rows = self.plan, self.rows
+        four = 2 if plan.fours else 0
+        self.parts.append(swap(self.operands[0], "wide", 1))
+        for at in range(plan.steps - four):
+            self.operands = [self.total(rows >> (at + 1), rows >> at)]
+            yield
+            self.parts.append(plan.mixed(self.operands[0], [o[at] for o in plan.orders]))
+        if four:
+            size = rows >> plan.steps
+            self.operands = [self.total(q * size, (q + 1) * size) for q in (1, 2, 3)]
+            yield
+            self.parts += self.around(self.operands)
+        held = self.total(0, rows >> plan.steps)
+        if four:
+            self.operands = [held]
+            yield
+            held = jnp.concatenate([held] + self.around([self.operands[0]] * 3), axis=0)
+        for at in range(four, len(plan.back[0])):
+            self.operands = [held]
+            yield
+            got = plan.mixed(self.operands[0], [o[at] for o in plan.back])
+            held = jnp.concatenate([self.operands[0], got], axis=0)
+        self.operands = [held]
+        yield
+        self.result = (self.operands[0], swap(self.operands[0], "wide", 1))
+
     def advance(self):
-        plan, at = self.plan, self.at
-        back = len(plan.back[0])
-        if at == 0:
-            got = swap(self.operand, "wide", 1)
-        elif at <= plan.steps:
-            got = plan.mixed(self.operand, [o[at - 1] for o in plan.orders])
-        elif at <= plan.steps + back:
-            got = plan.mixed(self.operand, [o[at - plan.steps - 1] for o in plan.back])
-        else:
-            got = swap(self.operand, "wide", 1)
-        self.at = at + 1
-        if at <= plan.steps:
-            self.parts.append(got)
-            if at == plan.steps:
-                self.operand = self.total(0, self.rows >> at)
-            else:
-                self.operand = self.total(self.rows >> (at + 1), self.rows >> at)
-        elif at <= plan.steps + back:
-            self.operand = jnp.concatenate([self.operand, got], axis=0)
-        else:
-            self.result = (self.operand, got)
-
-    @property
-    def left(self):
-        return self.plan.steps + len(self.plan.back[0]) + 2 - self.at
+        next(self.work, None)
 
 
 def lockstep(*chains):
-    live = [c for c in chains if c.left > 0]
-    if len(live) > 1:
-        for c, o in zip(live, tied(*[c.operand for c in live])):
-            c.operand = o
-    for c in live:
+    if len(chains) > 1:
+        held = tied([c.operands for c in chains])[0]
+        for c, o in zip(chains, held):
+            c.operands = list(o)
+    for c in chains:
         c.advance()
+
+
+def hold(value, chain):
+    value, operands = tied(value, chain.operands)
+    chain.operands = list(operands)
+    return value
 
 
 class SmallSum:
     def __init__(self, value):
-        self.operand = value
+        self.operands = [value]
         self.bits = [(a, 1 << i) for a in ("wide", "narrow") for i in range(lax.axis_size(a).bit_length() - 1)]
 
     def advance(self):
-        self.operand = self.operand + swap(self.operand, *self.bits.pop(0))
-
-    @property
-    def left(self):
-        return len(self.bits)
+        if self.bits:
+            (value,) = self.operands
+            self.operands = [value + swap(value, *self.bits.pop(0))]
 
 
 def local(
@@ -521,17 +626,17 @@
     tokens = feats * samp
     narrow = lax.axis_size("narrow")
     wide = lax.axis_size("wide")
-    plan = Plan(wide, narrow)
+    plan, short = Plan(wide, narrow), Plan(wide, narrow, True)
     core = plan.core
-    part = feats // 2
-    group = max(g for g in (1, 2, 4) if part % g == 0)
-    steps = part // group
+    group = max(g for g in (1, 2, 4) if feats % (2 * g) == 0)
+    steps = feats // group
     rows = group * samp
     head_cols = w_qkv.shape[2]
     own_ff = w_up.shape[1]
     slot = own_ff // 2
     ff = own_ff * narrow
     inpack = slot == 512
+    unit = min(256, slot)
     n_ff, n_out, n_qkv = own_ff // wide, w_out.shape[0] // wide, 3 * head_cols // wide
     ordered = narrow == 2 and n_ff % 16 == 0 and n_out % 16 == 0 and n_qkv % 16 == 0
     blocks = plan.blocks
@@ -541,20 +646,14 @@
         return lax.dynamic_slice_in_dim(a, core * size, size, axis)
 
     qkv_half = core_half(w_qkv.reshape(width, 3 * head_cols), 0)
-    qkv_half, early = tied(qkv_half, inputs[:part])
-    qkv_mine = gather_pieces(qkv_half, "narrow")[1:]
-    prev0, next0 = halo(early, "wide")
     up_half = core_half(w_up, 1)
     small = jnp.concatenate(
         [up_half.reshape(-1, 512), core_half(w_down, 0), core_half(w_out, 0)], axis=0
     )
-    held = tied(small, *qkv_mine)
-    small, qkv_mine = held[0], list(held[1:])
+    x_prev, x_next = halo(inputs, "wide")
+    qkv_mine = gather_pieces(qkv_half, "narrow")[1:]
     pack_mine = gather_pieces(small, "narrow")[1:]
     qkv_got = [swap(p, "wide", 1) for p in qkv_mine]
-    late, prev0, next0 = tied(inputs, prev0, next0)
-    prev1, next1 = halo(late[part:], "wide")
-
     def whole_of(mine, got):
         first = jnp.where(core == 0, mine, got)
         second = jnp.where(core == 0, got, mine)
@@ -577,15 +676,13 @@
     gain1, shift1 = norm1_gain[None, :], norm1_shift[None, :]
     gain2, shift2 = norm2_gain[None, :], norm2_shift[None, :]
     sources, targets = plan.sources(), plan.targets()
+    short_sources, short_targets = short.sources(), short.targets()
 
     def whole(a):
         return pl.BlockSpec(a.shape, lambda i: (0,) * a.ndim, pipeline_mode=pl.Buffered(1))
 
-    def cube(offset):
-        return pl.BlockSpec((group, samp, width), lambda i: (i + offset, 0, 0))
-
+    cube = pl.BlockSpec((group, samp, width), lambda i: (i, 0, 0))
     smem = pl.BlockSpec(memory_space=pltpu.SMEM)
-    anywhere = pl.BlockSpec(memory_space=pl.ANY)
     line = pl.BlockSpec((1, width), lambda i: (0, 0))
     vec = jax.ShapeDtypeStruct((1, width), F32)
 
@@ -595,37 +692,24 @@
     def cost(flops, size):
         return pl.CostEstimate(flops=flops, bytes_accessed=size, transcendentals=0)
 
-    def qkv_block(offset):
-        return pl.BlockSpec((2, 3, rows, 3 * GROUP_COLS), lambda i: (0, 0, i + offset, 0))
-
-    done = None
-    for h, (before, after) in enumerate(((prev0, next0), (prev1, next1))):
-        off = h * steps
-        args = [id_col, id_row, before, inputs, after, w0, w1, gain1, shift1]
-        specs = [whole(id_col), whole(id_row), cube(0), cube(off), cube(0)]
-        specs += [whole(a) for a in (w0, w1, gain1, shift1)]
-        alias = {}
-        if done is not None:
-            alias = {len(args): 0, len(args) + 1: 1}
-            args += done
-            specs += [anywhere, anywhere]
-        done = pl.pallas_call(
-            attn_fwd_kernel,
-            grid=(steps,),
-            in_specs=specs,
-            out_specs=[qkv_block(off), cube(off)],
-            out_shape=[
-                jax.ShapeDtypeStruct((2, 3, tokens, 3 * GROUP_COLS), BF16),
-                jax.ShapeDtypeStruct((feats, samp, width), BF16),
-            ],
-            input_output_aliases=alias,
-            cost_estimate=cost(6 * 10**9 // 2, 12 << 20),
-            name=f"attn_fwd_{h}",
-        )(*args)
-    held = tied(done[1], *pack_mine)
-    done, pack_mine = [done[0], held[0]], list(held[1:])
+    qkv_block = pl.BlockSpec((2, 3, rows, 3 * GROUP_COLS), lambda i: (0, 0, i, 0))
+
+    args = [id_col, id_row, x_prev, inputs, x_next, w0, w1, gain1, shift1]
+    qkv, attended = pl.pallas_call(
+        attn_fwd_kernel,
+        grid=(steps,),
+        in_specs=[whole(id_col), whole(id_row), cube, cube, cube]
+        + [whole(a) for a in (w0, w1, gain1, shift1)],
+        out_specs=[qkv_block, cube],
+        out_shape=[
+            jax.ShapeDtypeStruct((2, 3, tokens, 3 * GROUP_COLS), BF16),
+            jax.ShapeDtypeStruct((feats, samp, width), BF16),
+        ],
+        cost_estimate=cost(6 * 10**9, 24 << 20),
+        name="attn_fwd",
+    )(*args)
+    attended, *pack_mine = tied(attended, *pack_mine)
     pack_got = [swap(p, "wide", 1) for p in pack_mine]
-    qkv, attended = done
 
     x_flat = inputs.reshape(tokens, width)
     cot_flat = cotangent.reshape(tokens, width)
@@ -646,14 +730,16 @@
     outs = [tok(BF16), tok(F32), tok(BF16), vec, vec]
     outs += [jax.ShapeDtypeStruct(s, BF16) for s in sums]
     scratch = [
-        ((width, width), BF16), ((width, slot), BF16), ((slot, width), BF16),
+        ((width, width), BF16), ((width, unit), BF16), ((unit, width), BF16),
+        ((width, unit), BF16), ((unit, width), BF16),
         ((tokens, width), F32), ((tokens, width), BF16), ((tokens, width), F32), ((tokens, width), F32),
-        ((tokens, slot), BF16), ((tokens, slot), BF16), ((tokens, width), BF16),
+        ((tokens, unit), BF16), ((tokens, unit), BF16), ((tokens, unit), BF16), ((tokens, unit), BF16),
+        ((tokens, width), BF16),
         ((ff, width), BF16), ((ff, width), BF16), ((width, width), BF16),
     ]
     block_out, hidden_grad, dattended, gain2_grad, shift2_grad, *packed = pl.pallas_call(
         functools.partial(chain_kernel, narrow - 1, inpack, ordered),
-        grid=(2 * narrow,),
+        grid=(narrow * slot // unit + 1,),
         in_specs=[smem] + [whole(a) for a in args[1:]],
         out_specs=[whole(o) for o in outs],
         out_shape=outs,
@@ -662,29 +748,27 @@
         name="chain",
     )(*args)
 
-    def arranged(natural):
+    def arranged(natural, sources):
         flat = natural.reshape(narrow * wide, natural.shape[2], 512)
         places = sources[1:].reshape(2, blocks)
         return [jnp.take(flat, places[s], axis=0).reshape(-1, 512) for s in range(2)]
 
     if not ordered:
         down, up, out = (p.reshape(narrow, wide, -1, 512) for p in packed)
-        packed = arranged(jnp.concatenate([down, up, out], axis=2))
+        packed = arranged(jnp.concatenate([down, up, out], axis=2), sources)
     big = Reduction(plan, packed[0], packed[1])
 
     datt = dattended.reshape(feats, samp, width)
     d_prev, d_next = halo(datt, "wide")
-    lockstep(big)
-    group2 = group
-    all_steps = feats // group2
+    big.advance()
 
     def pair_block(cols):
         return pl.BlockSpec((2, rows, cols), lambda i: (0, i, 0))
 
     dq, dkv_own = pl.pallas_call(
         attn_bwd_own_kernel,
-        grid=(all_steps,),
-        in_specs=[whole(id_col), whole(id_row), qkv_block(0), cube(0)],
+        grid=(steps,),
+        in_specs=[whole(id_col), whole(id_row), qkv_block, cube],
         out_specs=[pair_block(GROUP_COLS), pair_block(2 * GROUP_COLS)],
         out_shape=[
             jax.ShapeDtypeStruct((2, tokens, GROUP_COLS), BF16),
@@ -693,25 +777,39 @@
         cost_estimate=cost(10 * 10**9, 14 << 20),
         name="attn_bwd_own",
     )(id_col, id_row, qkv, datt)
-    dkv_own, big.operand = tied(dkv_own, big.operand)
-    lockstep(big)
-    dkv = pl.pallas_call(
-        attn_bwd_near_kernel,
-        grid=(all_steps,),
-        in_specs=[whole(id_col), whole(id_row), qkv_block(0), cube(0), cube(0), pair_block(2 * GROUP_COLS)],
-        out_specs=pair_block(2 * GROUP_COLS),
-        out_shape=jax.ShapeDtypeStruct((2, tokens, 2 * GROUP_COLS), BF16),
-        cost_estimate=cost(10 * 10**9, 14 << 20),
-        name="attn_bwd_near",
-    )(id_col, id_row, qkv, d_prev, d_next, dkv_own)
-    dkv, big.operand = tied(dkv, big.operand)
-    lockstep(big)
+    dkv, near = dkv_own, None
+    for h in range(2):
+        off = h * (steps // 2)
+
+        def shifted(spec, off=off):
+            return pl.BlockSpec(spec.block_shape, lambda i: spec.index_map(i + off))
+
+        dkv = hold(dkv, big)
+        big.advance()
+        args = [id_col, id_row, qkv, d_prev, d_next, dkv_own if h else dkv]
+        specs = [whole(id_col), whole(id_row)]
+        specs += [shifted(b) for b in (qkv_block, cube, cube, pair_block(2 * GROUP_COLS))]
+        if h:
+            args.append(dkv)
+            specs.append(pl.BlockSpec(memory_space=pl.ANY))
+        dkv = pl.pallas_call(
+            attn_bwd_near_kernel,
+            grid=(steps // 2,),
+            in_specs=specs,
+            out_specs=shifted(pair_block(2 * GROUP_COLS)),
+            out_shape=jax.ShapeDtypeStruct((2, tokens, 2 * GROUP_COLS), BF16),
+            input_output_aliases={6: 0} if h else {},
+            cost_estimate=cost(5 * 10**9, 7 << 20),
+            name=f"attn_bwd_near_{h}",
+        )(*args)
+    dkv = hold(dkv, big)
+    big.advance()
 
     natural = (6 * GROUP_COLS, width)
     outs = [jax.ShapeDtypeStruct((blocks * n_qkv, 512), BF16)] * 2
     if not ordered:
         outs = [jax.ShapeDtypeStruct(natural, BF16)]
-    args = [sources, x_flat, dq, dkv, gain1, shift1]
+    args = [short_sources, x_flat, dq, dkv, gain1, shift1]
     packed = pl.pallas_call(
         functools.partial(qkv_grad_kernel, ordered),
         grid=(1,),
@@ -724,11 +822,13 @@
     )(*args)
     if not ordered:
         turned = packed[0].reshape(2, 3, narrow // 2, head_cols, width).transpose(0, 2, 1, 3, 4)
-        packed = arranged(turned.reshape(narrow, wide, n_qkv, width))
-    last = Reduction(plan, packed[0], packed[1])
+        packed = arranged(turned.reshape(narrow, wide, n_qkv, width), short_sources)
+    *packed, dkv = hold([*packed, dkv], big)
+    big.advance()
+    last = Reduction(short, packed[0], packed[1])
+    last.advance()
 
     flat = pl.BlockSpec((CHUNK, width), lambda i: (i, 0))
-    dkv, last.operand = tied(dkv, last.operand)
     input_grad, gain1_grad, shift1_grad = pl.pallas_call(
         input_grad_kernel,
         grid=(tokens // CHUNK,),
@@ -742,9 +842,13 @@
     )(x_flat, hidden_grad, dq, dkv, w0, w1, gain1)
     norms = SmallSum(jnp.concatenate([gain1_grad, shift1_grad, gain2_grad, shift2_grad], axis=0))
 
-    lockstep(last, big)
-    lockstep(last, big)
-    while big.left > 0:
+    lockstep(last, big, norms)
+    lockstep(last, norms)
+    lockstep(last, big, norms)
+    lockstep(last, big, norms)
+    lockstep(last, norms)
+    lockstep(last, big, norms)
+    for _ in range(9):
         lockstep(last, big, norms)
     down_rows, out_rows, qkv_rows = own_ff, w_out.shape[0], 3 * head_cols
     if ordered:
@@ -759,11 +863,6 @@
             cost_estimate=cost(0, 8 << 20),
             name="ffn_out",
         )(targets, *big.result)
-    while last.left > 0 or norms.left > 0:
-        if ordered and last.left == 1:
-            last.operand, out_grad = tied(last.operand, out_grad)
-        lockstep(last, norms)
-
     if ordered:
         shape = jax.ShapeDtypeStruct((3, width, head_cols), F32)
         qkv_grad = pl.pallas_call(
@@ -775,21 +874,21 @@
             scratch_shapes=[pltpu.VMEM((qkv_rows, width), F32)],
             cost_estimate=cost(0, 3 << 20),
             name="qkv_out",
-        )(targets, *last.result)
+        )(short_targets, *last.result)
         qkv_grad = qkv_grad.transpose(1, 0, 2)
     else:
 
-        def natural_rows(pair, count):
+        def natural_rows(pair, targets):
             both = jnp.concatenate(pair, axis=0).reshape(wide, -1, 512)
             places = jnp.zeros((wide,), jnp.int32).at[targets].set(jnp.arange(wide, dtype=jnp.int32))
             return jnp.take(both, places, axis=0).astype(F32)
 
-        full = natural_rows(big.result, wide)
+        full = natural_rows(big.result, targets)
         down_grad = full[:, :n_ff].reshape(w_down.shape)
         up_grad = full[:, n_ff : 2 * n_ff].reshape(own_ff, width).T
         out_grad = full[:, 2 * n_ff :].reshape(w_out.shape)
-        qkv_grad = natural_rows(last.result, wide).reshape(qkv_rows, width).T.reshape(width, 3, head_cols)
-    norm_sums = norms.operand
+        qkv_grad = natural_rows(last.result, short_targets).reshape(qkv_rows, width).T.reshape(width, 3, head_cols)
+    norm_sums = norms.operands[0]
     return (
         block_out.reshape(feats, samp, width),
         input_grad.reshape(feats, samp, width),

time: 240 us -> 212 us (0.88)
  Pallas kernels: 114 us -> 92.6 us
  starting transfers between devices: 49.5 us -> 44.5 us
  waiting for transfers between devices: 44.7 us -> 48.8 us
  local copies, waits for them, and re-layouts: 11.2 us -> 8.15 us
    pallas_call x4, Pallas kernels: 57.6 us -> 40.5 us  [the longest x2 15.9 us: local(): pl.pallas_call(attn_bwd_near_kernel, grid=(steps // 2,), in_specs=specs,...]
    ppermute x13 -> x19, waiting for transfers between devices: 21.9 us -> 31.8 us  [swap(): return lax.ppermute(x, axis, [(i, i ^ bit) for i in range(count)])]
    ppermute x13 -> x19, starting transfers between devices: 12.2 us -> 20.6 us  [swap(): return lax.ppermute(x, axis, [(i, i ^ bit) for i in range(count)])]
    ppermute x14 -> x10, starting transfers between devices: 22.5 us -> 14.8 us  [mixed(): return lax.ppermute(x, ('wide', 'narrow'), pairs)]
    ppermute x14 -> x10, waiting for transfers between devices: 22.8 us -> 17 us  [mixed(): return lax.ppermute(x, ('wide', 'narrow'), pairs)]
    ppermute x3 -> x2, starting transfers between devices: 10.9 us -> 6.5 us  [halo(): prev = lax.ppermute(x, axis, [(i, i + 1) for i in range(count - 1)])]
    pallas_call x1, Pallas kernels: 35.2 us -> 31.2 us  [local(): pl.pallas_call(functools.partial(chain_kernel, narrow - 1, inpack, ordere...]
    convert_element_type x10 -> x9, other arithmetic: 13.4 us -> 12 us  [total(): return out.astype(BF16)]
  transfers between devices with their start and end apart: 33 -> 33, of which waited for: 15 -> 15; matrix products, arithmetic and copies ran while one was open for 7% -> 6% of each run, Pallas kernels for 30% -> 27%
where the time goes in v5:
time: 212 us
  Pallas kernels  92.6 us (44%)
  waiting for transfers between devices  48.8 us (23%)
  starting transfers between devices  44.5 us (21%)
  other arithmetic  16.5 us (8%)
  local copies, waits for them, and re-layouts  8.15 us (4%)
    ppermute x19, waiting for transfers between devices, swap(): return lax.ppermute(x, axis, [(i, i ^ bit) for i in range(count)])  31.8 us
    pallas_call x1, Pallas kernels, local(): pl.pallas_call(functools.partial(chain_kernel, narrow - 1, inpack, ordere...  31.2 us
    ppermute x19, starting transfers between devices, swap(): return lax.ppermute(x, axis, [(i, i ^ bit) for i in range(count)])  20.6 us
    ppermute x10, waiting for transfers between devices, mixed(): return lax.ppermute(x, ('wide', 'narrow'), pairs)  17 us
    pallas_call x2, Pallas kernels, local(): pl.pallas_call(attn_bwd_near_kernel, grid=(steps // 2,), in_specs=specs,...  15.9 us
    ppermute x10, starting transfers between devices, mixed(): return lax.ppermute(x, ('wide', 'narrow'), pairs)  14.8 us
    pallas_call x1, Pallas kernels, local(): pl.pallas_call(attn_fwd_kernel, grid=(steps,), in_specs=[whole(id_col), w...  13.9 us
    convert_element_type x9, other arithmetic, total(): return out.astype(BF16)  12 us
  transfers between devices with their start and end apart: 33, of which 15 were waited for; matrix products, arithmetic and copies ran while one was open for 6% of the time, Pallas kernels for 27%

profile of v5, /device:TPU:0, one launch (start us, length us, event | category | flops | bytes accessed | tf_op | source)
XLA Modules:
  0.0 211.6 jit_solution(5352719081511741484)
XLA Ops:
  2.4 3.0 %collective-permute-start.2 = (bf16[256,768]{1,0:T(8,128)(2,1)S(1)}, bf16[256,768]{1,0:T(8,128)(2,1)S(1)}, u32[]{:S(2)}, u32[]{:S(2)}) collective-permute-start(bf16[256,768]{1,0:T(8,128)(2,1)S(1)} %constant_dynamic-slice_fusion.3), channel_id=1, source_target_pairs={{0,1},{1,0},{2,3},{3,2},{4,5},{5,4},{6,7},{7,6},{8,9},{9,8},{10,11... | collective-permute-start | bytes 1179656 | tf_op jit(solution)/shard_map/ppermute | solution.py:466
  5.5 2.5 %collective-permute-start = (bf16[16,64,512]{2,1,0:T(8,128)(2,1)S(1)}, bf16[16,64,512]{2,1,0:T(8,128)(2,1)}, u32[]{:S(2)}, u32[]{:S(2)}) collective-permute-start(bf16[16,64,512]{2,1,0:T(8,128)(2,1)S(1)} %copy-done.5), channel_id=1, source_target_pairs={{0,2},{2,4},{4,6},{6,8},{8,10},{10,12},{12,14},{14,16},{16,18},{18... | collective-permute-start | bytes 3145736 | tf_op jit(solution)/shard_map/ppermute | solution.py:471
  10.6 4.0 %collective-permute-done.2 = bf16[256,768]{1,0:T(8,128)(2,1)S(1)} collective-permute-done((bf16[256,768]{1,0:T(8,128)(2,1)S(1)}, bf16[256,768]{1,0:T(8,128)(2,1)S(1)}, u32[]{:S(2)}, u32[]{:S(2)}) %collective-permute-start.2) | collective-permute-done | bytes 393248 | tf_op jit(solution)/shard_map/ppermute | solution.py:466
  19.3 13.9 %attn_fwd.1 = (bf16[2,3,1024,768]{3,2,1,0:T(8,128)(2,1)}, bf16[16,64,512]{2,1,0:T(8,128)(2,1)}) custom-call(s32[192,1]{1,0:T(8,128)} %copy.49.idc, s32[3,256]{1,0:T(4,128)} %tile.12.idr, bf16[16,64,512]{2,1,0:T(8,128)(2,1)} %collective-permute-done.xp, bf16[16,64,512]{2,1,0:T(8,128)(2,1)} %xo.1, bf16[16,64,512]{2,1,0:T(8,128)(2,1)} %collective-permute-done.1.xn, ...), custom_call_target="tpu_custom_call" | custom-call | flops 6000000000 | bytes 25165824 | tf_op jit(solution)/shard_map/attn_fwd/pallas_call | solution.py:698
  33.2 10.0 %collective-permute-done.4.refs_9_ = bf16[1152,512]{1,0:T(8,128)(2,1)} collective-permute-done((bf16[1152,512]{1,0:T(8,128)(2,1)S(1)}, bf16[1152,512]{1,0:T(8,128)(2,1)}, u32[]{:S(2)}, u32[]{:S(2)}) %collective-permute-start.4) | collective-permute-done | bytes 1179680 | tf_op jit(solution)/shard_map/ppermute | solution.py:466
  43.2 2.8 %collective-permute-start.5 = (bf16[1152,512]{1,0:T(8,128)(2,1)}, bf16[1152,512]{1,0:T(8,128)(2,1)S(1)}, u32[]{:S(2)}, u32[]{:S(2)}) collective-permute-start(bf16[1152,512]{1,0:T(8,128)(2,1)} %collective-permute-done.4.refs_9_), channel_id=1, source_target_pairs={{0,2},{2,0},{4,6},{6,4},{8,10},{10,8},{12,14},{14,12},{16,18},{18,... | collective-permute-start | bytes 3538952 | tf_op jit(solution)/shard_map/ppermute | solution.py:466
  49.7 31.2 %chain.1 = (bf16[1024,512]{1,0:T(8,128)(2,1)}, f32[1024,512]{1,0:T(8,128)}, bf16[1024,512]{1,0:T(8,128)(2,1)}, f32[1,512]{1,0:T(1,128)}, f32[1,512]{1,0:T(1,128)...) custom-call(s32[33]{0:T(128)} %pad_add_fusion.refs_0_, bf16[1024,512]{1,0:T(8,128)(2,1)} %bitcast.20, ...), custom_call_target="tpu_custom_call" | custom-call | flops 15000000512 | bytes 20971520 | tf_op jit(solution)/shard_map/chain/pallas_call | solution.py:740
  82.6 4.0 %collective-permute-start.6 = (bf16[16,64,512]{2,1,0:T(8,128)(2,1)}, bf16[16,64,512]{2,1,0:T(8,128)(2,1)}, u32[]{:S(2)}, u32[]{:S(2)}) collective-permute-start(bf16[16,64,512]{2,1,0:T(8,128)(2,1)} %bitcast.34), channel_id=1, source_target_pairs={{0,2},{2,4},{4,6},{6,8},{8,10},{10,12},{12,14},{14,16},{16,18},{18... | collective-permute-start | bytes 3145736 | tf_op jit(solution)/shard_map/ppermute | solution.py:471
  86.6 10.6 %attn_bwd_own.1 = (bf16[2,1024,256]{2,1,0:T(8,128)(2,1)}, f32[2,1024,512]{2,1,0:T(8,128)}) custom-call(s32[192,1]{1,0:T(8,128)} %copy.49.idc, s32[3,256]{1,0:T(4,128)} %tile.12.idr, bf16[2,3,1024,768]{3,2,1,0:T(8,128)(2,1)} %get-tuple-element.73.qkv_ref, bf16[16,64,512]{2,1,0:T(8,128)(2,1)} %bitcast.35), custom_call_target="tpu_custom_call" | custom-call | flops 10000000000 | bytes 14680064 | tf_op jit(solution)/shard_map/attn_bwd_own/pallas_call | solution.py:768
  99.8 8.0 %attn_bwd_near_0.1.rest_0_ = bf16[2,1024,512]{2,1,0:T(8,128)(2,1)} custom-call(s32[192,1]{1,0:T(8,128)} %copy.49.idc, s32[3,256]{1,0:T(4,128)} %tile.12.idr, bf16[2,3,1024,768]{3,2,1,0:T(8,128)(2,1)} %get-tuple-element.73.qkv_ref, bf16[16,64,512]{2,1,0:T(8,128)(2,1)} %collective-permute-done.6.dp_ref, bf16[16,64,512]{2,1,0:T(8,128)(2,1)} %collective-permute-done.7.dn_ref, ...), custom_call_target="tpu_custom_call" | custom-call | flops 5000000000 | bytes 7340032 | tf_op jit(solution)/shard_map/attn_bwd_near_0/pallas_call | solution.py:795
  107.7 7.5 %collective-permute-done.9 = bf16[1152,512]{1,0:T(8,128)(2,1)} collective-permute-done((bf16[1152,512]{1,0:T(8,128)(2,1)S(1)}, bf16[1152,512]{1,0:T(8,128)(2,1)}, u32[]{:S(2)}, u32[]{:S(2)}) %collective-permute-start.9) | collective-permute-done | bytes 1179680 | tf_op jit(solution)/shard_map/ppermute | solution.py:543
  116.7 5.8 %collective-permute-start.10 = (bf16[576,512]{1,0:T(8,128)(2,1)S(1)}, bf16[576,512]{1,0:T(8,128)(2,1)S(1)}, u32[]{:S(2)}, u32[]{:S(2)}) collective-permute-start(bf16[576,512]{1,0:T(8,128)(2,1)S(1)} %add_convert_fusion.1), channel_id=1, source_target_pairs={{0,4},{1,5},{2,3},{3,2},{4,0},{5,1},{6,7},{7,6},{8,12},{9,13},{10,... | collective-permute-start | bytes 1769480 | tf_op jit(solution)/shard_map/ppermute | solution.py:543
  122.5 8.0 %attn_bwd_near_1.1.dkv = bf16[2,1024,512]{2,1,0:T(8,128)(2,1)} custom-call(s32[192,1]{1,0:T(8,128)} %copy.49.idc, s32[3,256]{1,0:T(4,128)} %tile.12.idr, bf16[2,3,1024,768]{3,2,1,0:T(8,128)(2,1)} %get-tuple-element.73.qkv_ref, bf16[16,64,512]{2,1,0:T(8,128)(2,1)} %collective-permute-done.6.dp_ref, ...), custom_call_target="tpu_custom_call", output_to_operand_aliasing={{}: (6, {})} | custom-call | flops 5000000000 | bytes 7340032 | tf_op jit(solution)/shard_map/attn_bwd_near_1/pallas_call | solution.py:795
  134.8 6.3 %qkv_grad.1 = (bf16[768,512]{1,0:T(8,128)(2,1)}, bf16[768,512]{1,0:T(8,128)(2,1)}) custom-call(s32[33]{0:T(128)} %pad_add_fusion.1.table, bf16[1024,512]{1,0:T(8,128)(2,1)} %bitcast.21, bf16[2,1024,256]{2,1,0:T(8,128)(2,1)} %get-tuple-element.75.dq, bf16[2,1024,512]{2,1,0:T(8,128)(2,1)} %attn_bwd_near_1.1.dkv, f32[1,512]{1,0:T(1,128)} %bitcast.25, ...), custom_call_target="tpu_custom_call" | custom-call | flops 2000000000 | bytes 6291456 | tf_op jit(solution)/shard_map/qkv_grad/pallas_call | solution.py:813
  143.9 7.1 %input_grad.1 = (f32[1024,512]{1,0:T(8,128)}, f32[1,512]{1,0:T(1,128)}, f32[1,512]{1,0:T(1,128)}) custom-call(bf16[1024,512]{1,0:T(8,128)(2,1)} %bitcast.22, f32[1024,512]{1,0:T(8,128)} %get-tuple-element.72.hgrad, bf16[2,1024,256]{2,1,0:T(8,128)(2,1)} %get-tuple-element.75.dq, bf16[2,1024,512]{2,1,0:T(8,128)(2,1)} %attn_bwd_near_1.1.dkv, ...), custom_call_target="tpu_custom_call" | custom-call | flops 2000000000 | bytes 8388608 | tf_op jit(solution)/shard_map/input_grad/pallas_call | solution.py:832
  158.3 5.2 %collective-permute-done.14 = bf16[384,512]{1,0:T(8,128)(2,1)S(1)} collective-permute-done((bf16[384,512]{1,0:T(8,128)(2,1)S(1)}, bf16[384,512]{1,0:T(8,128)(2,1)S(1)}, u32[]{:S(2)}, u32[]{:S(2)}) %collective-permute-start.14) | collective-permute-done | bytes 393248 | tf_op jit(solution)/shard_map/ppermute | solution.py:543
  167.2 3.1 %collective-permute-done.18 = f32[4,512]{1,0:T(4,128)S(1)} collective-permute-done((f32[4,512]{1,0:T(4,128)S(1)}, f32[4,512]{1,0:T(4,128)S(1)}, u32[]{:S(2)}, u32[]{:S(2)}) %collective-permute-start.18) | collective-permute-done | bytes 8224 | tf_op jit(solution)/shard_map/ppermute | solution.py:466
  171.7 2.3 %collective-permute-start.19 = (bf16[48,512]{1,0:T(8,128)(2,1)S(1)}, bf16[48,512]{1,0:T(8,128)(2,1)S(1)}, u32[]{:S(2)}, u32[]{:S(2)}) collective-permute-start(bf16[48,512]{1,0:T(8,128)(2,1)S(1)} %get-tuple-element.101), channel_id=1, source_target_pairs={{0,16},{2,18},{4,20},{6,22},{8,24},{10,26},{12,28},{14,30},{16,0},... | collective-permute-start | bytes 147464 | tf_op jit(solution)/shard_map/ppermute | solution.py:466
  176.9 3.6 %collective-permute-done.23 = f32[4,512]{1,0:T(4,128)S(1)} collective-permute-done((f32[4,512]{1,0:T(4,128)S(1)}, f32[4,512]{1,0:T(4,128)S(1)}, u32[]{:S(2)}, u32[]{:S(2)}) %collective-permute-start.23) | collective-permute-done | bytes 8224 | tf_op jit(solution)/shard_map/ppermute | solution.py:466
  185.3 2.3 %collective-permute-start.24 = (bf16[48,512]{1,0:T(8,128)(2,1)S(1)}, bf16[48,512]{1,0:T(8,128)(2,1)S(1)}, u32[]{:S(2)}, u32[]{:S(2)}) collective-permute-start(bf16[48,512]{1,0:T(8,128)(2,1)S(1)} %add_convert_fusion.7), channel_id=1, source_target_pairs={{0,16},{2,18},{4,20},{6,22},{8,24},{10,26},{12,28},{14,30},{16,0},... | collective-permute-start | bytes 147464 | tf_op jit(solution)/shard_map/ppermute | solution.py:466
  188.3 4.2 %collective-permute-done.27 = f32[4,512]{1,0:T(4,128)S(1)} collective-permute-done((f32[4,512]{1,0:T(4,128)S(1)}, f32[4,512]{1,0:T(4,128)S(1)}, u32[]{:S(2)}, u32[]{:S(2)}) %collective-permute-start.27) | collective-permute-done | bytes 8224 | tf_op jit(solution)/shard_map/ppermute | solution.py:466
  194.0 2.9 %collective-permute-done.30 = f32[4,512]{1,0:T(4,128)S(1)} collective-permute-done((f32[4,512]{1,0:T(4,128)S(1)}, f32[4,512]{1,0:T(4,128)S(1)}, u32[]{:S(2)}, u32[]{:S(2)}) %collective-permute-start.30) | collective-permute-done | bytes 8224 | tf_op jit(solution)/shard_map/ppermute | solution.py:466
  203.1 2.8 %qkv_out.1 = f32[3,512,256]{2,1,0:T(8,128)} custom-call(s32[16]{0:T(128)} %pad_add_fusion.2.table, bf16[384,512]{1,0:T(8,128)(2,1)} %copy-done.3, bf16[384,512]{1,0:T(8,128)(2,1)} %copy-done.8), custom_call_target="tpu_custom_call" | custom-call | bytes 3145728 | tf_op jit(solution)/shard_map/qkv_out/pallas_call | solution.py:868
  207.0 4.6 %ffn_out.1 = (f32[512,1024]{1,0:T(8,128)}, f32[1024,512]{1,0:T(8,128)}, f32[256,512]{1,0:T(8,128)}) custom-call(s32[16]{0:T(128)} %pad_add_fusion.3.table, bf16[1152,512]{1,0:T(8,128)(2,1)} %copy-done.1, bf16[1152,512]{1,0:T(8,128)(2,1)} %copy-done.4), custom_call_target="tpu_custom_call" | custom-call | bytes 8388608 | tf_op jit(solution)/shard_map/ffn_out/pallas_call | solution.py:856
  (135 shorter events, 54.8 us)
Async XLA Ops:
  2.4 12.1 %collective-permute-start.2 = (bf16[256,768]{1,0:T(8,128)(2,1)S(1)}, bf16[256,768]{1,0:T(8,128)(2,1)S(1)}, u32[]{:S(2)}, u32[]{:S(2)}) collective-permute-start(bf16[256,768]{1,0:T(8,128)(2,1)S(1)} %constant_dynamic-slice_fusion.3), channel_id=1, source_target_pairs={{0,1},{1,0},{2,3},{3,2},{4,5},{5,4},{6,7},{7,6},{8,9},{9,8},{10,11... | collective-permute-start | bytes 1179656 | tf_op jit(solution)/shard_map/ppermute | solution.py:466
  5.5 13.8 %collective-permute-start = (bf16[16,64,512]{2,1,0:T(8,128)(2,1)S(1)}, bf16[16,64,512]{2,1,0:T(8,128)(2,1)}, u32[]{:S(2)}, u32[]{:S(2)}) collective-permute-start(bf16[16,64,512]{2,1,0:T(8,128)(2,1)S(1)} %copy-done.5), channel_id=1, source_target_pairs={{0,2},{2,4},{4,6},{6,8},{8,10},{10,12},{12,14},{14,16},{16,18},{18... | collective-permute-start | bytes 3145736 | tf_op jit(solution)/shard_map/ppermute | solution.py:471
  7.9 11.3 %collective-permute-start.1 = (bf16[16,64,512]{2,1,0:T(8,128)(2,1)S(1)}, bf16[16,64,512]{2,1,0:T(8,128)(2,1)}, u32[]{:S(2)}, u32[]{:S(2)}) collective-permute-start(bf16[16,64,512]{2,1,0:T(8,128)(2,1)S(1)} %copy-done.5), channel_id=1, source_target_pairs={{2,0},{4,2},{6,4},{8,6},{10,8},{12,10},{14,12},{16,14},{18,16},{20... | collective-permute-start | bytes 3145736 | tf_op jit(solution)/shard_map/ppermute | solution.py:472
  14.7 28.6 %collective-permute-start.4 = (bf16[1152,512]{1,0:T(8,128)(2,1)S(1)}, bf16[1152,512]{1,0:T(8,128)(2,1)}, u32[]{:S(2)}, u32[]{:S(2)}) collective-permute-start(bf16[1152,512]{1,0:T(8,128)(2,1)S(1)} %pad_maximum_fusion), channel_id=1, source_target_pairs={{0,1},{1,0},{2,3},{3,2},{4,5},{5,4},{6,7},{7,6},{8,9},{9,8},{10,11... | collective-permute-start | bytes 3538952 | tf_op jit(solution)/shard_map/ppermute | solution.py:466
  80.9 16.4 %collective-permute-start.8 = (bf16[2304,512]{1,0:T(8,128)(2,1)}, bf16[2304,512]{1,0:T(8,128)(2,1)}, u32[]{:S(2)}, u32[]{:S(2)}) collective-permute-start(bf16[2304,512]{1,0:T(8,128)(2,1)} %get-tuple-element.78), channel_id=1, source_target_pairs={{0,2},{2,0},{4,6},{6,4},{8,10},{10,8},{12,14},{14,12},{16,18},{18,... | collective-permute-start | bytes 7077896 | tf_op jit(solution)/shard_map/ppermute | solution.py:466
  81.3 18.4 %collective-permute-start.7 = (bf16[16,64,512]{2,1,0:T(8,128)(2,1)}, bf16[16,64,512]{2,1,0:T(8,128)(2,1)}, u32[]{:S(2)}, u32[]{:S(2)}) collective-permute-start(bf16[16,64,512]{2,1,0:T(8,128)(2,1)} %bitcast.33), channel_id=1, source_target_pairs={{2,0},{4,2},{6,4},{8,6},{10,8},{12,10},{14,12},{16,14},{18,16},{20... | collective-permute-start | bytes 3145736 | tf_op jit(solution)/shard_map/ppermute | solution.py:472
  82.6 17.2 %collective-permute-start.6 = (bf16[16,64,512]{2,1,0:T(8,128)(2,1)}, bf16[16,64,512]{2,1,0:T(8,128)(2,1)}, u32[]{:S(2)}, u32[]{:S(2)}) collective-permute-start(bf16[16,64,512]{2,1,0:T(8,128)(2,1)} %bitcast.34), channel_id=1, source_target_pairs={{0,2},{2,4},{4,6},{6,8},{8,10},{10,12},{12,14},{14,16},{16,18},{18... | collective-permute-start | bytes 3145736 | tf_op jit(solution)/shard_map/ppermute | solution.py:471
  98.9 16.4 %collective-permute-start.9 = (bf16[1152,512]{1,0:T(8,128)(2,1)S(1)}, bf16[1152,512]{1,0:T(8,128)(2,1)}, u32[]{:S(2)}, u32[]{:S(2)}) collective-permute-start(bf16[1152,512]{1,0:T(8,128)(2,1)S(1)} %add_convert_fusion), channel_id=1, source_target_pairs={{0,1},{1,0},{2,10},{3,11},{4,5},{5,4},{6,14},{7,15},{8,9},{9,8},{1... | collective-permute-start | bytes 3538952 | tf_op jit(solution)/shard_map/ppermute | solution.py:543
  116.7 13.7 %collective-permute-start.10 = (bf16[576,512]{1,0:T(8,128)(2,1)S(1)}, bf16[576,512]{1,0:T(8,128)(2,1)S(1)}, u32[]{:S(2)}, u32[]{:S(2)}) collective-permute-start(bf16[576,512]{1,0:T(8,128)(2,1)S(1)} %add_convert_fusion.1), channel_id=1, source_target_pairs={{0,4},{1,5},{2,3},{3,2},{4,0},{5,1},{6,7},{7,6},{8,12},{9,13},{10,... | collective-permute-start | bytes 1769480 | tf_op jit(solution)/shard_map/ppermute | solution.py:543
  132.6 8.5 %collective-permute-start.11 = (bf16[288,512]{1,0:T(8,128)(2,1)}, bf16[288,512]{1,0:T(8,128)(2,1)S(1)}, u32[]{:S(2)}, u32[]{:S(2)}) collective-permute-start(bf16[288,512]{1,0:T(8,128)(2,1)} %add_convert_fusion.3), channel_id=1, source_target_pairs={{0,8},{1,9},{2,6},{3,7},{4,12},{5,13},{6,2},{7,3},{8,0},{9,1},{10,... | collective-permute-start | bytes 884744 | tf_op jit(solution)/shard_map/ppermute | solution.py:543
  142.8 11.8 %collective-permute-start.12 = (bf16[768,512]{1,0:T(8,128)(2,1)}, bf16[768,512]{1,0:T(8,128)(2,1)}, u32[]{:S(2)}, u32[]{:S(2)}) collective-permute-start(bf16[768,512]{1,0:T(8,128)(2,1)} %get-tuple-element.90), channel_id=1, source_target_pairs={{0,2},{2,0},{4,6},{6,4},{8,10},{10,8},{12,14},{14,12},{16,18},{18,... | collective-permute-start | bytes 2359304 | tf_op jit(solution)/shard_map/ppermute | solution.py:466
  142.8 10.5 %collective-permute-start.13 = (bf16[144,512]{1,0:T(8,128)(2,1)}, bf16[144,512]{1,0:T(8,128)(2,1)}, u32[]{:S(2)}, u32[]{:S(2)}) collective-permute-start(bf16[144,512]{1,0:T(8,128)(2,1)} %add_convert_fusion.6), channel_id=1, source_target_pairs={{0,16},{1,17},{2,18},{3,19},{4,20},{5,21},{6,22},{7,23},{8,24},{9,... | collective-permute-start | bytes 442376 | tf_op jit(solution)/shard_map/ppermute | solution.py:543
  155.7 7.8 %collective-permute-start.14 = (bf16[384,512]{1,0:T(8,128)(2,1)S(1)}, bf16[384,512]{1,0:T(8,128)(2,1)S(1)}, u32[]{:S(2)}, u32[]{:S(2)}) collective-permute-start(bf16[384,512]{1,0:T(8,128)(2,1)S(1)} %add_convert_fusion.2), channel_id=1, source_target_pairs={{0,1},{1,0},{2,6},{3,7},{4,5},{5,4},{6,2},{7,3},{8,9},{9,8},{10,14... | collective-permute-start | bytes 1179656 | tf_op jit(solution)/shard_map/ppermute | solution.py:543
  157.5 9.7 %collective-permute-start.17 = (bf16[144,512]{1,0:T(8,128)(2,1)S(1)}, bf16[144,512]{1,0:T(8,128)(2,1)S(1)}, u32[]{:S(2)}, u32[]{:S(2)}) collective-permute-start(bf16[144,512]{1,0:T(8,128)(2,1)S(1)} %add_convert_fusion.5), channel_id=1, source_target_pairs={{0,16},{1,17},{2,18},{3,19},{4,20},{5,21},{6,22},{7,23},{8,24},{9,... | collective-permute-start | bytes 442376 | tf_op jit(solution)/shard_map/ppermute | solution.py:543
  171.3 10.6 %collective-permute-start.22 = (bf16[288,512]{1,0:T(8,128)(2,1)S(1)}, bf16[288,512]{1,0:T(8,128)(2,1)S(1)}, u32[]{:S(2)}, u32[]{:S(2)}) collective-permute-start(bf16[288,512]{1,0:T(8,128)(2,1)S(1)} %pad_maximum_fusion.5), channel_id=1, source_target_pairs={{0,8},{1,9},{2,6},{3,7},{4,12},{5,13},{6,2},{7,3},{8,0},{9,1},{10,... | collective-permute-start | bytes 884744 | tf_op jit(solution)/shard_map/ppermute | solution.py:543
  171.7 8.7 %collective-permute-start.19 = (bf16[48,512]{1,0:T(8,128)(2,1)S(1)}, bf16[48,512]{1,0:T(8,128)(2,1)S(1)}, u32[]{:S(2)}, u32[]{:S(2)}) collective-permute-start(bf16[48,512]{1,0:T(8,128)(2,1)S(1)} %get-tuple-element.101), channel_id=1, source_target_pairs={{0,16},{2,18},{4,20},{6,22},{8,24},{10,26},{12,28},{14,30},{16,0},... | collective-permute-start | bytes 147464 | tf_op jit(solution)/shard_map/ppermute | solution.py:466
  174.0 6.5 %collective-permute-start.20 = (bf16[48,512]{1,0:T(8,128)(2,1)S(1)}, bf16[48,512]{1,0:T(8,128)(2,1)S(1)}, u32[]{:S(2)}, u32[]{:S(2)}) collective-permute-start(bf16[48,512]{1,0:T(8,128)(2,1)S(1)} %get-tuple-element.102), channel_id=1, source_target_pairs={{0,8},{2,10},{4,12},{6,14},{8,0},{10,2},{12,4},{14,6},{16,24},{18,... | collective-permute-start | bytes 147464 | tf_op jit(solution)/shard_map/ppermute | solution.py:466
  174.1 7.0 %collective-permute-start.21 = (bf16[48,512]{1,0:T(8,128)(2,1)S(1)}, bf16[48,512]{1,0:T(8,128)(2,1)S(1)}, u32[]{:S(2)}, u32[]{:S(2)}) collective-permute-start(bf16[48,512]{1,0:T(8,128)(2,1)S(1)} %get-tuple-element.103), channel_id=1, source_target_pairs={{0,24},{2,26},{4,28},{6,30},{8,16},{10,18},{12,20},{14,22},{16,8},... | collective-permute-start | bytes 147464 | tf_op jit(solution)/shard_map/ppermute | solution.py:466
  182.0 16.8 %collective-permute-start.29 = (bf16[576,512]{1,0:T(8,128)(2,1)S(1)}, bf16[576,512]{1,0:T(8,128)(2,1)S(1)}, u32[]{:S(2)}, u32[]{:S(2)}) collective-permute-start(bf16[576,512]{1,0:T(8,128)(2,1)S(1)} %pad_maximum_fusion.3), channel_id=1, source_target_pairs={{0,4},{1,5},{2,10},{3,11},{4,0},{5,1},{6,14},{7,15},{8,12},{9,13},... | collective-permute-start | bytes 1769480 | tf_op jit(solution)/shard_map/ppermute | solution.py:543
  183.3 9.2 %collective-permute-start.26 = (bf16[48,512]{1,0:T(8,128)(2,1)S(1)}, bf16[48,512]{1,0:T(8,128)(2,1)S(1)}, u32[]{:S(2)}, u32[]{:S(2)}) collective-permute-start(bf16[48,512]{1,0:T(8,128)(2,1)S(1)} %add_convert_fusion.7), channel_id=1, source_target_pairs={{0,24},{2,26},{4,28},{6,30},{8,16},{10,18},{12,20},{14,22},{16,8},... | collective-permute-start | bytes 147464 | tf_op jit(solution)/shard_map/ppermute | solution.py:466
  185.3 7.1 %collective-permute-start.25 = (bf16[48,512]{1,0:T(8,128)(2,1)S(1)}, bf16[48,512]{1,0:T(8,128)(2,1)S(1)}, u32[]{:S(2)}, u32[]{:S(2)}) collective-permute-start(bf16[48,512]{1,0:T(8,128)(2,1)S(1)} %add_convert_fusion.7), channel_id=1, source_target_pairs={{0,8},{2,10},{4,12},{6,14},{8,0},{10,2},{12,4},{14,6},{16,24},{18,... | collective-permute-start | bytes 147464 | tf_op jit(solution)/shard_map/ppermute | solution.py:466
  185.3 7.1 %collective-permute-start.24 = (bf16[48,512]{1,0:T(8,128)(2,1)S(1)}, bf16[48,512]{1,0:T(8,128)(2,1)S(1)}, u32[]{:S(2)}, u32[]{:S(2)}) collective-permute-start(bf16[48,512]{1,0:T(8,128)(2,1)S(1)} %add_convert_fusion.7), channel_id=1, source_target_pairs={{0,16},{2,18},{4,20},{6,22},{8,24},{10,26},{12,28},{14,30},{16,0},... | collective-permute-start | bytes 147464 | tf_op jit(solution)/shard_map/ppermute | solution.py:466
  192.5 6.3 %collective-permute-start.28 = (bf16[192,512]{1,0:T(8,128)(2,1)S(1)}, bf16[192,512]{1,0:T(8,128)(2,1)S(1)}, u32[]{:S(2)}, u32[]{:S(2)}) collective-permute-start(bf16[192,512]{1,0:T(8,128)(2,1)S(1)} %pad_maximum_fusion.6), channel_id=1, source_target_pairs={{0,4},{1,5},{2,6},{3,7},{4,0},{5,1},{6,2},{7,3},{8,12},{9,13},{10,... | collective-permute-start | bytes 589832 | tf_op jit(solution)/shard_map/ppermute | solution.py:543
  198.9 7.1 %collective-permute-start.32 = (bf16[1152,512]{1,0:T(8,128)(2,1)S(1)}, bf16[1152,512]{1,0:T(8,128)(2,1)S(1)}, u32[]{:S(2)}, u32[]{:S(2)}) collective-permute-start(bf16[1152,512]{1,0:T(8,128)(2,1)S(1)} %pad_maximum_fusion.1.mine), channel_id=1, source_target_pairs={{0,2},{2,0},{4,6},{6,4},{8,10},{10,8},{12,14},{14,12},{16,18},{18,... | collective-permute-start | bytes 3538952 | tf_op jit(solution)/shard_map/ppermute | solution.py:466
  (30 other events, 260.7 us)

commit v6 on v5

--- a/solution.py
+++ b/solution.py
@@ -17,6 +17,7 @@
 BF16 = jnp.bfloat16
 NEG = -1e30
 CHUNK = 256
+RHYTHM = (1, 0, 1, 1, 0)
 
 
 def dot_nn(a, b):
@@ -87,18 +88,27 @@
     lax.fori_loop(0, count, lambda i, carry: (body(i), carry)[1], 0, unroll=unroll)
 
 
-def attn_fwd_kernel(idc, idr, xp, xo, xn, w0, w1, gain, shift, qkv_ref, att_ref):
-    feats, samp, width = xo.shape
+def own_kernel(xo, w0, w1, gain, shift, own_ref, normed_ref):
+    xhat, _ = norm_parts(xo[...].astype(F32))
+    normed = (xhat * gain[...] + shift[...]).astype(BF16)
+    normed_ref[...] = normed
+    for hg, w in enumerate((w0, w1)):
+        own_ref[hg] = dot_nn(normed, w[...]).astype(BF16)
+
+
+def attn_fwd_kernel(idc, idr, xp, own, xn, w0, w1, gain, shift, qkv_ref, att_ref):
+    feats, samp, width = xp.shape
     rows = feats * samp
     x = jnp.concatenate(
-        [xp[...].reshape(rows, width), xo[...].reshape(rows, width), xn[...].reshape(rows, width)],
-        axis=0,
+        [xp[...].reshape(rows, width), xn[...].reshape(rows, width)], axis=0
     ).astype(F32)
     xhat, _ = norm_parts(x)
     normed = (xhat * gain[...] + shift[...]).astype(BF16)
     for hg, w in enumerate((w0, w1)):
         qkv = dot_nn(normed, w[...]).astype(BF16)
-        qkv_ref[hg] = qkv.reshape(3, rows, 3 * GROUP_COLS)
+        qkv_ref[hg, 0] = qkv[:rows]
+        qkv_ref[hg, 1] = own[hg]
+        qkv_ref[hg, 2] = qkv[rows:]
     allowed = idc[...] == idr[1:2, :]
     m16 = lane_head(1, BF16)
     q16 = [m * SCALE for m in m16]
@@ -398,21 +408,20 @@
     staged(2 * feats, first, second, third)
 
 
-def qkv_grad_kernel(ordered, table, x, dq, dkv, gain, shift, *refs):
-    normed, gq = refs[-2:]
-    outs = refs[:-2]
-    tokens, width = x.shape
-
-    def start(i):
-        sl = rows_at(i, CHUNK)
-        xhat, _ = norm_parts(x[sl].astype(F32))
-        normed[sl] = (xhat * gain[...] + shift[...]).astype(BF16)
-
-    each(tokens // CHUNK, start)
-    for hg in range(2):
-        low = 3 * hg * GROUP_COLS
-        gq[low : low + GROUP_COLS] = dot_tn(dq[hg], normed[...]).astype(BF16)
-        gq[low + GROUP_COLS : low + 3 * GROUP_COLS] = dot_tn(dkv[hg], normed[...]).astype(BF16)
+def qkv_grad_kernel(ordered, table, normed, dq, dkv, *refs):
+    outs, gq = refs[:-1], refs[-1]
+    hg = pl.program_id(0)
+    gq[rows_at(3 * hg, GROUP_COLS)] = dot_tn(dq[0], normed[...]).astype(BF16)
+    for j in range(2):
+        cols = slice(j * GROUP_COLS, (j + 1) * GROUP_COLS)
+        gq[rows_at(3 * hg + 1 + j, GROUP_COLS)] = dot_tn(dkv[0, :, cols], normed[...]).astype(BF16)
+
+    @pl.when(hg == 1)
+    def _():
+        arrange_qkv(ordered, table, outs, gq)
+
+
+def arrange_qkv(ordered, table, outs, gq):
     if ordered:
         blocks = (table.shape[0] - 1) // 2
         size = gq.shape[0] // (2 * blocks)
@@ -694,11 +703,22 @@
 
     qkv_block = pl.BlockSpec((2, 3, rows, 3 * GROUP_COLS), lambda i: (0, 0, i, 0))
 
-    args = [id_col, id_row, x_prev, inputs, x_next, w0, w1, gain1, shift1]
+    own_block = pl.BlockSpec((2, rows, 3 * GROUP_COLS), lambda i: (0, i, 0))
+    args = [w0, w1, gain1, shift1]
+    own, normed_one = pl.pallas_call(
+        own_kernel,
+        grid=(steps,),
+        in_specs=[pl.BlockSpec((rows, width), lambda i: (i, 0))] + [whole(a) for a in args],
+        out_specs=[own_block, pl.BlockSpec((rows, width), lambda i: (i, 0))],
+        out_shape=[jax.ShapeDtypeStruct((2, tokens, 3 * GROUP_COLS), BF16), tok(BF16)],
+        cost_estimate=cost(2 * 10**9, 6 << 20),
+        name="own_qkv",
+    )(inputs.reshape(tokens, width), *args)
+    args = [id_col, id_row, x_prev, own, x_next, w0, w1, gain1, shift1]
     qkv, attended = pl.pallas_call(
         attn_fwd_kernel,
         grid=(steps,),
-        in_specs=[whole(id_col), whole(id_row), cube, cube, cube]
+        in_specs=[whole(id_col), whole(id_row), cube, own_block, cube]
         + [whole(a) for a in (w0, w1, gain1, shift1)],
         out_specs=[qkv_block, cube],
         out_shape=[
@@ -777,9 +797,10 @@
         cost_estimate=cost(10 * 10**9, 14 << 20),
         name="attn_bwd_own",
     )(id_col, id_row, qkv, datt)
-    dkv, near = dkv_own, None
-    for h in range(2):
-        off = h * (steps // 2)
+    dkv = dkv_own
+    shares = [steps // 4, steps // 2, steps // 4] if steps % 4 == 0 else [1] * steps
+    for h, share in enumerate(shares):
+        off = sum(shares[:h])
 
         def shifted(spec, off=off):
             return pl.BlockSpec(spec.block_shape, lambda i: spec.index_map(i + off))
@@ -794,12 +815,12 @@
             specs.append(pl.BlockSpec(memory_space=pl.ANY))
         dkv = pl.pallas_call(
             attn_bwd_near_kernel,
-            grid=(steps // 2,),
+            grid=(share,),
             in_specs=specs,
             out_specs=shifted(pair_block(2 * GROUP_COLS)),
             out_shape=jax.ShapeDtypeStruct((2, tokens, 2 * GROUP_COLS), BF16),
             input_output_aliases={6: 0} if h else {},
-            cost_estimate=cost(5 * 10**9, 7 << 20),
+            cost_estimate=cost(2 * share * 10**9, share * 3 << 20),
             name=f"attn_bwd_near_{h}",
         )(*args)
     dkv = hold(dkv, big)
@@ -809,14 +830,15 @@
     outs = [jax.ShapeDtypeStruct((blocks * n_qkv, 512), BF16)] * 2
     if not ordered:
         outs = [jax.ShapeDtypeStruct(natural, BF16)]
-    args = [short_sources, x_flat, dq, dkv, gain1, shift1]
+    args = [short_sources, normed_one, dq, dkv]
     packed = pl.pallas_call(
         functools.partial(qkv_grad_kernel, ordered),
-        grid=(1,),
-        in_specs=[smem] + [whole(a) for a in args[1:]],
+        grid=(2,),
+        in_specs=[smem, whole(normed_one)]
+        + [pl.BlockSpec((1, tokens, n * GROUP_COLS), lambda i: (i, 0, 0)) for n in (1, 2)],
         out_specs=[whole(o) for o in outs],
         out_shape=outs,
-        scratch_shapes=[pltpu.VMEM((tokens, width), BF16), pltpu.VMEM(natural, BF16)],
+        scratch_shapes=[pltpu.VMEM(natural, BF16)],
         cost_estimate=cost(2 * 10**9, 6 << 20),
         name="qkv_grad",
     )(*args)
@@ -842,15 +864,14 @@
     )(x_flat, hidden_grad, dq, dkv, w0, w1, gain1)
     norms = SmallSum(jnp.concatenate([gain1_grad, shift1_grad, gain2_grad, shift2_grad], axis=0))
 
-    lockstep(last, big, norms)
+    for beside in RHYTHM:
+        lockstep(*([last, big, norms] if beside else [last, norms]))
+    while not hasattr(big, "result"):
+        lockstep(last, big, norms)
+    if not hasattr(last, "result"):
+        big.result = hold(list(big.result), last)
     lockstep(last, norms)
-    lockstep(last, big, norms)
-    lockstep(last, big, norms)
-    lockstep(last, norms)
-    lockstep(last, big, norms)
-    for _ in range(9):
-        lockstep(last, big, norms)
-    down_rows, out_rows, qkv_rows = own_ff, w_out.shape[0], 3 * head_cols
+    qkv_rows = 3 * head_cols
     if ordered:
         shapes = [jax.ShapeDtypeStruct(s, F32) for s in (w_up.shape, w_down.shape, w_out.shape)]
         up_grad, down_grad, out_grad = pl.pallas_call(
@@ -863,6 +884,9 @@
             cost_estimate=cost(0, 8 << 20),
             name="ffn_out",
         )(targets, *big.result)
+    for _ in range(8):
+        lockstep(last, norms)
+
     if ordered:
         shape = jax.ShapeDtypeStruct((3, width, head_cols), F32)
         qkv_grad = pl.pallas_call(

time: 212 us -> 209 us (0.986)
  waiting for transfers between devices: 48.8 us -> 42.9 us
  Pallas kernels: 92.6 us -> 98.3 us
  other arithmetic: 16.5 us -> 13 us
    ppermute x19, waiting for transfers between devices: 31.8 us -> 22.5 us  [swap(): return lax.ppermute(x, axis, [(i, i ^ bit) for i in range(count)])]
    pallas_call x3 -> x5, Pallas kernels: 22.2 us -> 30 us  [the longest x3 18.8 us: local(): pl.pallas_call(attn_bwd_near_kernel, grid=(share,), in_specs=specs, out_s...]
    convert_element_type x9, other arithmetic: 12 us -> 7.51 us  [total(): return out.astype(BF16)]
    ppermute x10, waiting for transfers between devices: 17 us -> 20.5 us  [mixed(): return lax.ppermute(x, ('wide', 'narrow'), pairs)]
    unnamed x43 -> x41, local copies, waits for them, and re-layouts: 4.27 us -> 5.28 us
  transfers between devices with their start and end apart: 33 -> 33, of which waited for: 15 -> 13; matrix products, arithmetic and copies ran while one was open for 6% -> 5% of each run, Pallas kernels for 27% -> 31%
where the time goes in v6:
time: 209 us
  Pallas kernels  98.3 us (47%)
  starting transfers between devices  44.1 us (21%)
  waiting for transfers between devices  42.9 us (21%)
  other arithmetic  13 us (6%)
  local copies, waits for them, and re-layouts  9.15 us (4%)
    pallas_call x1, Pallas kernels, local(): pl.pallas_call(functools.partial(chain_kernel, narrow - 1, inpack, ordere...  31.2 us
    ppermute x19, waiting for transfers between devices, swap(): return lax.ppermute(x, axis, [(i, i ^ bit) for i in range(count)])  22.5 us
    ppermute x10, waiting for transfers between devices, mixed(): return lax.ppermute(x, ('wide', 'narrow'), pairs)  20.5 us
    ppermute x19, starting transfers between devices, swap(): return lax.ppermute(x, axis, [(i, i ^ bit) for i in range(count)])  19.5 us
    pallas_call x3, Pallas kernels, local(): pl.pallas_call(attn_bwd_near_kernel, grid=(share,), in_specs=specs, out_s...  18.8 us
    ppermute x10, starting transfers between devices, mixed(): return lax.ppermute(x, ('wide', 'narrow'), pairs)  14.8 us
    pallas_call x1, Pallas kernels, local(): pl.pallas_call(attn_fwd_kernel, grid=(steps,), in_specs=[whole(id_col), w...  12.1 us
    pallas_call x1, Pallas kernels, local(): pl.pallas_call(attn_bwd_own_kernel, grid=(steps,), in_specs=[whole(id_col...  10.5 us
  transfers between devices with their start and end apart: 33, of which 13 were waited for; matrix products, arithmetic and copies ran while one was open for 5% of the time, Pallas kernels for 31%

profile of v6, /device:TPU:0, one launch (start us, length us, event | category | flops | bytes accessed | tf_op | source)
XLA Modules:
  0.0 208.7 jit_solution(319619853887091033)
XLA Ops:
  2.4 3.0 %collective-permute-start.1 = (bf16[256,768]{1,0:T(8,128)(2,1)S(1)}, bf16[256,768]{1,0:T(8,128)(2,1)S(1)}, u32[]{:S(2)}, u32[]{:S(2)}) collective-permute-start(bf16[256,768]{1,0:T(8,128)(2,1)S(1)} %constant_dynamic-slice_fusion.3), channel_id=1, source_target_pairs={{0,1},{1,0},{2,3},{3,2},{4,5},{5,4},{6,7},{7,6},{8,9},{9,8},{10,11... | collective-permute-start | bytes 1179656 | tf_op jit(solution)/shard_map/ppermute | solution.py:475
  6.7 4.0 %collective-permute-start = (bf16[16,64,512]{2,1,0:T(8,128)(2,1)}, bf16[16,64,512]{2,1,0:T(8,128)(2,1)}, u32[]{:S(2)}, u32[]{:S(2)}) collective-permute-start(bf16[16,64,512]{2,1,0:T(8,128)(2,1)} %param.35), channel_id=1, source_target_pairs={{0,2},{2,4},{4,6},{6,8},{8,10},{10,12},{12,14},{14,16},{16,18},{18... | collective-permute-start | bytes 3145736 | tf_op jit(solution)/shard_map/ppermute | solution.py:480
  20.2 6.1 %own_qkv.1 = (bf16[2,1024,768]{2,1,0:T(8,128)(2,1)}, bf16[1024,512]{1,0:T(8,128)(2,1)}) custom-call(bf16[1024,512]{1,0:T(8,128)(2,1)} %bitcast.1.xo.refs_1_.x, bf16[512,768]{1,0:T(8,128)(2,1)} %copy-done.2, bf16[512,768]{1,0:T(8,128)(2,1)} %pad_maximum_fusion.2.w1, f32[1,512]{1,0:T(1,128)} %bitcast.21, f32[1,512]{1,0:T(1,128)} %bitcast.33), custom_call_target="tpu_custom_call" | custom-call | flops 2000000000 | bytes 6291456 | tf_op jit(solution)/shard_map/own_qkv/pallas_call | solution.py:708
  26.3 12.1 %attn_fwd.1 = (bf16[2,3,1024,768]{3,2,1,0:T(8,128)(2,1)}, bf16[16,64,512]{2,1,0:T(8,128)(2,1)}) custom-call(s32[192,1]{1,0:T(8,128)} %copy.51.idc, s32[3,256]{1,0:T(4,128)} %tile.12.idr, bf16[16,64,512]{2,1,0:T(8,128)(2,1)} %collective-permute-done.xp, bf16[2,1024,768]{2,1,0:T(8,128)(2,1)} %get-tuple-element.73.own, ...), custom_call_target="tpu_custom_call" | custom-call | flops 6000000000 | bytes 25165824 | tf_op jit(solution)/shard_map/attn_fwd/pallas_call | solution.py:718
  38.4 4.8 %collective-permute-done.4.refs_9_ = bf16[1152,512]{1,0:T(8,128)(2,1)} collective-permute-done((bf16[1152,512]{1,0:T(8,128)(2,1)S(1)}, bf16[1152,512]{1,0:T(8,128)(2,1)}, u32[]{:S(2)}, u32[]{:S(2)}) %collective-permute-start.4) | collective-permute-done | bytes 1179680 | tf_op jit(solution)/shard_map/ppermute | solution.py:475
  48.8 31.2 %chain.1 = (bf16[1024,512]{1,0:T(8,128)(2,1)}, f32[1024,512]{1,0:T(8,128)}, bf16[1024,512]{1,0:T(8,128)(2,1)}, f32[1,512]{1,0:T(1,128)}, f32[1,512]{1,0:T(1,128)...) custom-call(s32[33]{0:T(128)} %pad_add_fusion.refs_0_, bf16[1024,512]{1,0:T(8,128)(2,1)} %bitcast.1.xo.refs_1_.x, ...), custom_call_target="tpu_custom_call" | custom-call | flops 15000000512 | bytes 20971520 | tf_op jit(solution)/shard_map/chain/pallas_call | solution.py:760
  81.9 3.1 %collective-permute-start.6 = (bf16[16,64,512]{2,1,0:T(8,128)(2,1)}, bf16[16,64,512]{2,1,0:T(8,128)(2,1)S(1)}, u32[]{:S(2)}, u32[]{:S(2)}) collective-permute-start(bf16[16,64,512]{2,1,0:T(8,128)(2,1)} %bitcast.31), channel_id=1, source_target_pairs={{0,2},{2,4},{4,6},{6,8},{8,10},{10,12},{12,14},{14,16},{16,18},{18... | collective-permute-start | bytes 3145736 | tf_op jit(solution)/shard_map/ppermute | solution.py:480
  85.0 10.5 %attn_bwd_own.1 = (bf16[2,1024,256]{2,1,0:T(8,128)(2,1)}, f32[2,1024,512]{2,1,0:T(8,128)}) custom-call(s32[192,1]{1,0:T(8,128)} %copy.51.idc, s32[3,256]{1,0:T(4,128)} %tile.12.idr, bf16[2,3,1024,768]{3,2,1,0:T(8,128)(2,1)} %get-tuple-element.79.qkv_ref, bf16[16,64,512]{2,1,0:T(8,128)(2,1)} %bitcast.32), custom_call_target="tpu_custom_call" | custom-call | flops 10000000000 | bytes 14680064 | tf_op jit(solution)/shard_map/attn_bwd_own/pallas_call | solution.py:788
  100.1 5.5 %attn_bwd_near_0.1.rest_0_ = bf16[2,1024,512]{2,1,0:T(8,128)(2,1)} custom-call(s32[192,1]{1,0:T(8,128)} %copy.51.idc, s32[3,256]{1,0:T(4,128)} %tile.12.idr, bf16[2,3,1024,768]{3,2,1,0:T(8,128)(2,1)} %get-tuple-element.79.qkv_ref, bf16[16,64,512]{2,1,0:T(8,128)(2,1)} %copy-done.1, bf16[16,64,512]{2,1,0:T(8,128)(2,1)} %copy-done, ...), custom_call_target="tpu_custom_call" | custom-call | flops 2000000000 | bytes 3145728 | tf_op jit(solution)/shard_map/attn_bwd_near_0/pallas_call | solution.py:816
  105.5 8.3 %collective-permute-done.9 = bf16[1152,512]{1,0:T(8,128)(2,1)} collective-permute-done((bf16[1152,512]{1,0:T(8,128)(2,1)S(1)}, bf16[1152,512]{1,0:T(8,128)(2,1)}, u32[]{:S(2)}, u32[]{:S(2)}) %collective-permute-start.9) | collective-permute-done | bytes 1179680 | tf_op jit(solution)/shard_map/ppermute | solution.py:552
  115.5 4.6 %collective-permute-start.10 = (bf16[576,512]{1,0:T(8,128)(2,1)S(1)}, bf16[576,512]{1,0:T(8,128)(2,1)S(1)}, u32[]{:S(2)}, u32[]{:S(2)}) collective-permute-start(bf16[576,512]{1,0:T(8,128)(2,1)S(1)} %add_convert_fusion.1), channel_id=1, source_target_pairs={{0,4},{1,5},{2,3},{3,2},{4,0},{5,1},{6,7},{7,6},{8,12},{9,13},{10,... | collective-permute-start | bytes 1769480 | tf_op jit(solution)/shard_map/ppermute | solution.py:552
  120.1 7.9 %attn_bwd_near_1.1.rest_0_ = bf16[2,1024,512]{2,1,0:T(8,128)(2,1)} custom-call(s32[192,1]{1,0:T(8,128)} %copy.51.idc, s32[3,256]{1,0:T(4,128)} %tile.12.idr, bf16[2,3,1024,768]{3,2,1,0:T(8,128)(2,1)} %get-tuple-element.79.qkv_ref, bf16[16,64,512]{2,1,0:T(8,128)(2,1)} %copy-done.1, bf16[16,64,512]{2,1,0:T(8,128)(2,1)} %copy-done, ...), custom_call_target="tpu_custom_call", output_to_operand_aliasing={{}: (6, {})} | custom-call | flops 4000000000 | bytes 6291456 | tf_op jit(solution)/shard_map/attn_bwd_near_1/pallas_call | solution.py:816
  131.6 5.4 %attn_bwd_near_2.1.dkv = bf16[2,1024,512]{2,1,0:T(8,128)(2,1)} custom-call(s32[192,1]{1,0:T(8,128)} %copy.51.idc, s32[3,256]{1,0:T(4,128)} %tile.12.idr, bf16[2,3,1024,768]{3,2,1,0:T(8,128)(2,1)} %get-tuple-element.79.qkv_ref, bf16[16,64,512]{2,1,0:T(8,128)(2,1)} %copy-done.1, bf16[16,64,512]{2,1,0:T(8,128)(2,1)} %copy-done, ...), custom_call_target="tpu_custom_call", output_to_operand_aliasing={{}: (6, {})} | custom-call | flops 2000000000 | bytes 3145728 | tf_op jit(solution)/shard_map/attn_bwd_near_2/pallas_call | solution.py:816
  140.0 5.0 %qkv_grad.1 = (bf16[768,512]{1,0:T(8,128)(2,1)}, bf16[768,512]{1,0:T(8,128)(2,1)}) custom-call(s32[33]{0:T(128)} %pad_add_fusion.1.table, bf16[1024,512]{1,0:T(8,128)(2,1)} %get-tuple-element.82.normed, bf16[2,1024,256]{2,1,0:T(8,128)(2,1)} %get-tuple-element.81.dq, bf16[2,1024,512]{2,1,0:T(8,128)(2,1)} %attn_bwd_near_2.1.dkv), custom_call_target="tpu_custom_call" | custom-call | flops 2000000000 | bytes 6291456 | tf_op jit(solution)/shard_map/qkv_grad/pallas_call | solution.py:834
  147.9 7.1 %input_grad.1 = (f32[1024,512]{1,0:T(8,128)}, f32[1,512]{1,0:T(1,128)}, f32[1,512]{1,0:T(1,128)}) custom-call(bf16[1024,512]{1,0:T(8,128)(2,1)} %bitcast.1.xo.refs_1_.x, f32[1024,512]{1,0:T(8,128)} %get-tuple-element.78.hgrad, bf16[2,1024,256]{2,1,0:T(8,128)(2,1)} %get-tuple-element.81.dq, bf16[2,1024,512]{2,1,0:T(8,128)(2,1)} %attn_bwd_near_2.1.dkv, ...), custom_call_target="tpu_custom_call" | custom-call | flops 2000000000 | bytes 8388608 | tf_op jit(solution)/shard_map/input_grad/pallas_call | solution.py:854
  160.7 5.4 %collective-permute-done.15 = bf16[384,512]{1,0:T(8,128)(2,1)S(1)} collective-permute-done((bf16[384,512]{1,0:T(8,128)(2,1)S(1)}, bf16[384,512]{1,0:T(8,128)(2,1)S(1)}, u32[]{:S(2)}, u32[]{:S(2)}) %collective-permute-start.15) | collective-permute-done | bytes 393248 | tf_op jit(solution)/shard_map/ppermute | solution.py:552
  168.3 3.7 %collective-permute-done.19 = f32[4,512]{1,0:T(4,128)S(1)} collective-permute-done((f32[4,512]{1,0:T(4,128)S(1)}, f32[4,512]{1,0:T(4,128)S(1)}, u32[]{:S(2)}, u32[]{:S(2)}) %collective-permute-start.19) | collective-permute-done | bytes 8224 | tf_op jit(solution)/shard_map/ppermute | solution.py:475
  175.2 2.6 %collective-permute-start.22 = (bf16[48,512]{1,0:T(8,128)(2,1)S(1)}, bf16[48,512]{1,0:T(8,128)(2,1)S(1)}, u32[]{:S(2)}, u32[]{:S(2)}) collective-permute-start(bf16[48,512]{1,0:T(8,128)(2,1)S(1)} %get-tuple-element.112), channel_id=1, source_target_pairs={{0,24},{2,26},{4,28},{6,30},{8,16},{10,18},{12,20},{14,22},{16,8},... | collective-permute-start | bytes 147464 | tf_op jit(solution)/shard_map/ppermute | solution.py:475
  178.1 3.6 %collective-permute-done.24 = f32[4,512]{1,0:T(4,128)S(1)} collective-permute-done((f32[4,512]{1,0:T(4,128)S(1)}, f32[4,512]{1,0:T(4,128)S(1)}, u32[]{:S(2)}, u32[]{:S(2)}) %collective-permute-start.24) | collective-permute-done | bytes 8224 | tf_op jit(solution)/shard_map/ppermute | solution.py:475
  182.6 2.7 %collective-permute-start.28 = (bf16[48,512]{1,0:T(8,128)(2,1)S(1)}, bf16[48,512]{1,0:T(8,128)(2,1)S(1)}, u32[]{:S(2)}, u32[]{:S(2)}) collective-permute-start(bf16[48,512]{1,0:T(8,128)(2,1)S(1)} %add_convert_fusion.7), channel_id=1, source_target_pairs={{0,24},{2,26},{4,28},{6,30},{8,16},{10,18},{12,20},{14,22},{16,8},... | collective-permute-start | bytes 147464 | tf_op jit(solution)/shard_map/ppermute | solution.py:475
  188.2 3.7 %collective-permute-done.29 = f32[4,512]{1,0:T(4,128)S(1)} collective-permute-done((f32[4,512]{1,0:T(4,128)S(1)}, f32[4,512]{1,0:T(4,128)S(1)}, u32[]{:S(2)}, u32[]{:S(2)}) %collective-permute-start.29) | collective-permute-done | bytes 8224 | tf_op jit(solution)/shard_map/ppermute | solution.py:475
  195.7 2.7 %collective-permute-done.30 = bf16[192,512]{1,0:T(8,128)(2,1)S(1)} collective-permute-done((bf16[192,512]{1,0:T(8,128)(2,1)S(1)}, bf16[192,512]{1,0:T(8,128)(2,1)S(1)}, u32[]{:S(2)}, u32[]{:S(2)}) %collective-permute-start.30) | collective-permute-done | bytes 196640 | tf_op jit(solution)/shard_map/ppermute | solution.py:552
  199.8 4.6 %ffn_out.1 = (f32[512,1024]{1,0:T(8,128)}, f32[1024,512]{1,0:T(8,128)}, f32[256,512]{1,0:T(8,128)}) custom-call(s32[16]{0:T(128)} %pad_add_fusion.3.table, bf16[1152,512]{1,0:T(8,128)(2,1)} %copy-done.3, bf16[1152,512]{1,0:T(8,128)(2,1)} %copy-done.5), custom_call_target="tpu_custom_call" | custom-call | bytes 8388608 | tf_op jit(solution)/shard_map/ffn_out/pallas_call | solution.py:877
  205.8 2.8 %qkv_out.1 = f32[3,512,256]{2,1,0:T(8,128)} custom-call(s32[16]{0:T(128)} %pad_add_fusion.2.table, bf16[384,512]{1,0:T(8,128)(2,1)} %copy-done.4, bf16[384,512]{1,0:T(8,128)(2,1)} %copy-done.7), custom_call_target="tpu_custom_call" | custom-call | bytes 3145728 | tf_op jit(solution)/shard_map/qkv_out/pallas_call | solution.py:892
  (135 shorter events, 57.1 us)
Async XLA Ops:
  2.4 12.1 %collective-permute-start.1 = (bf16[256,768]{1,0:T(8,128)(2,1)S(1)}, bf16[256,768]{1,0:T(8,128)(2,1)S(1)}, u32[]{:S(2)}, u32[]{:S(2)}) collective-permute-start(bf16[256,768]{1,0:T(8,128)(2,1)S(1)} %constant_dynamic-slice_fusion.3), channel_id=1, source_target_pairs={{0,1},{1,0},{2,3},{3,2},{4,5},{5,4},{6,7},{7,6},{8,9},{9,8},{10,11... | collective-permute-start | bytes 1179656 | tf_op jit(solution)/shard_map/ppermute | solution.py:475
  5.5 20.8 %collective-permute-start.3 = (bf16[16,64,512]{2,1,0:T(8,128)(2,1)}, bf16[16,64,512]{2,1,0:T(8,128)(2,1)}, u32[]{:S(2)}, u32[]{:S(2)}) collective-permute-start(bf16[16,64,512]{2,1,0:T(8,128)(2,1)} %param.35), channel_id=1, source_target_pairs={{2,0},{4,2},{6,4},{8,6},{10,8},{12,10},{14,12},{16,14},{18,16},{20... | collective-permute-start | bytes 3145736 | tf_op jit(solution)/shard_map/ppermute | solution.py:481
  6.7 19.5 %collective-permute-start = (bf16[16,64,512]{2,1,0:T(8,128)(2,1)}, bf16[16,64,512]{2,1,0:T(8,128)(2,1)}, u32[]{:S(2)}, u32[]{:S(2)}) collective-permute-start(bf16[16,64,512]{2,1,0:T(8,128)(2,1)} %param.35), channel_id=1, source_target_pairs={{0,2},{2,4},{4,6},{6,8},{8,10},{10,12},{12,14},{14,16},{16,18},{18... | collective-permute-start | bytes 3145736 | tf_op jit(solution)/shard_map/ppermute | solution.py:480
  14.7 28.6 %collective-permute-start.4 = (bf16[1152,512]{1,0:T(8,128)(2,1)S(1)}, bf16[1152,512]{1,0:T(8,128)(2,1)}, u32[]{:S(2)}, u32[]{:S(2)}) collective-permute-start(bf16[1152,512]{1,0:T(8,128)(2,1)S(1)} %pad_maximum_fusion), channel_id=1, source_target_pairs={{0,1},{1,0},{2,3},{3,2},{4,5},{5,4},{6,7},{7,6},{8,9},{9,8},{10,11... | collective-permute-start | bytes 3538952 | tf_op jit(solution)/shard_map/ppermute | solution.py:475
  80.0 15.5 %collective-permute-start.8 = (bf16[2304,512]{1,0:T(8,128)(2,1)}, bf16[2304,512]{1,0:T(8,128)(2,1)}, u32[]{:S(2)}, u32[]{:S(2)}) collective-permute-start(bf16[2304,512]{1,0:T(8,128)(2,1)} %get-tuple-element.85), channel_id=1, source_target_pairs={{0,2},{2,0},{4,6},{6,4},{8,10},{10,8},{12,14},{14,12},{16,18},{18,... | collective-permute-start | bytes 7077896 | tf_op jit(solution)/shard_map/ppermute | solution.py:475
  80.4 17.6 %collective-permute-start.7 = (bf16[16,64,512]{2,1,0:T(8,128)(2,1)}, bf16[16,64,512]{2,1,0:T(8,128)(2,1)S(1)}, u32[]{:S(2)}, u32[]{:S(2)}) collective-permute-start(bf16[16,64,512]{2,1,0:T(8,128)(2,1)} %bitcast.30), channel_id=1, source_target_pairs={{2,0},{4,2},{6,4},{8,6},{10,8},{12,10},{14,12},{16,14},{18,16},{20... | collective-permute-start | bytes 3145736 | tf_op jit(solution)/shard_map/ppermute | solution.py:481
  81.9 16.2 %collective-permute-start.6 = (bf16[16,64,512]{2,1,0:T(8,128)(2,1)}, bf16[16,64,512]{2,1,0:T(8,128)(2,1)S(1)}, u32[]{:S(2)}, u32[]{:S(2)}) collective-permute-start(bf16[16,64,512]{2,1,0:T(8,128)(2,1)} %bitcast.31), channel_id=1, source_target_pairs={{0,2},{2,4},{4,6},{6,8},{8,10},{10,12},{12,14},{14,16},{16,18},{18... | collective-permute-start | bytes 3145736 | tf_op jit(solution)/shard_map/ppermute | solution.py:480
  97.4 16.4 %collective-permute-start.9 = (bf16[1152,512]{1,0:T(8,128)(2,1)S(1)}, bf16[1152,512]{1,0:T(8,128)(2,1)}, u32[]{:S(2)}, u32[]{:S(2)}) collective-permute-start(bf16[1152,512]{1,0:T(8,128)(2,1)S(1)} %add_convert_fusion), channel_id=1, source_target_pairs={{0,1},{1,0},{2,10},{3,11},{4,5},{5,4},{6,14},{7,15},{8,9},{9,8},{1... | collective-permute-start | bytes 3538952 | tf_op jit(solution)/shard_map/ppermute | solution.py:552
  115.5 12.6 %collective-permute-start.10 = (bf16[576,512]{1,0:T(8,128)(2,1)S(1)}, bf16[576,512]{1,0:T(8,128)(2,1)S(1)}, u32[]{:S(2)}, u32[]{:S(2)}) collective-permute-start(bf16[576,512]{1,0:T(8,128)(2,1)S(1)} %add_convert_fusion.1), channel_id=1, source_target_pairs={{0,4},{1,5},{2,3},{3,2},{4,0},{5,1},{6,7},{7,6},{8,12},{9,13},{10,... | collective-permute-start | bytes 1769480 | tf_op jit(solution)/shard_map/ppermute | solution.py:552
  129.3 7.7 %collective-permute-start.11 = (bf16[288,512]{1,0:T(8,128)(2,1)S(1)}, bf16[288,512]{1,0:T(8,128)(2,1)S(1)}, u32[]{:S(2)}, u32[]{:S(2)}) collective-permute-start(bf16[288,512]{1,0:T(8,128)(2,1)S(1)} %add_convert_fusion.3), channel_id=1, source_target_pairs={{0,8},{1,9},{2,6},{3,7},{4,12},{5,13},{6,2},{7,3},{8,0},{9,1},{10,... | collective-permute-start | bytes 884744 | tf_op jit(solution)/shard_map/ppermute | solution.py:552
  138.2 8.3 %collective-permute-start.12 = (bf16[144,512]{1,0:T(8,128)(2,1)S(1)}, bf16[144,512]{1,0:T(8,128)(2,1)S(1)}, u32[]{:S(2)}, u32[]{:S(2)}) collective-permute-start(bf16[144,512]{1,0:T(8,128)(2,1)S(1)} %add_convert_fusion.6), channel_id=1, source_target_pairs={{0,16},{1,17},{2,18},{3,19},{4,20},{5,21},{6,22},{7,23},{8,24},{9,... | collective-permute-start | bytes 442376 | tf_op jit(solution)/shard_map/ppermute | solution.py:552
  147.7 10.4 %collective-permute-start.13 = (bf16[768,512]{1,0:T(8,128)(2,1)}, bf16[768,512]{1,0:T(8,128)(2,1)S(1)}, u32[]{:S(2)}, u32[]{:S(2)}) collective-permute-start(bf16[768,512]{1,0:T(8,128)(2,1)} %get-tuple-element.99), channel_id=1, source_target_pairs={{0,2},{2,0},{4,6},{6,4},{8,10},{10,8},{12,14},{14,12},{16,18},{18,... | collective-permute-start | bytes 2359304 | tf_op jit(solution)/shard_map/ppermute | solution.py:475
  147.8 10.3 %collective-permute-start.14 = (bf16[144,512]{1,0:T(8,128)(2,1)S(1)}, bf16[144,512]{1,0:T(8,128)(2,1)S(1)}, u32[]{:S(2)}, u32[]{:S(2)}) collective-permute-start(bf16[144,512]{1,0:T(8,128)(2,1)S(1)} %add_convert_fusion.5), channel_id=1, source_target_pairs={{0,16},{1,17},{2,18},{3,19},{4,20},{5,21},{6,22},{7,23},{8,24},{9,... | collective-permute-start | bytes 442376 | tf_op jit(solution)/shard_map/ppermute | solution.py:552
  158.2 7.8 %collective-permute-start.15 = (bf16[384,512]{1,0:T(8,128)(2,1)S(1)}, bf16[384,512]{1,0:T(8,128)(2,1)S(1)}, u32[]{:S(2)}, u32[]{:S(2)}) collective-permute-start(bf16[384,512]{1,0:T(8,128)(2,1)S(1)} %add_convert_fusion.2), channel_id=1, source_target_pairs={{0,1},{1,0},{2,6},{3,7},{4,5},{5,4},{6,2},{7,3},{8,9},{9,8},{10,14... | collective-permute-start | bytes 1179656 | tf_op jit(solution)/shard_map/ppermute | solution.py:552
  159.0 9.3 %collective-permute-start.18 = (bf16[288,512]{1,0:T(8,128)(2,1)S(1)}, bf16[288,512]{1,0:T(8,128)(2,1)S(1)}, u32[]{:S(2)}, u32[]{:S(2)}) collective-permute-start(bf16[288,512]{1,0:T(8,128)(2,1)S(1)} %pad_maximum_fusion.5), channel_id=1, source_target_pairs={{0,8},{1,9},{2,6},{3,7},{4,12},{5,13},{6,2},{7,3},{8,0},{9,1},{10,... | collective-permute-start | bytes 884744 | tf_op jit(solution)/shard_map/ppermute | solution.py:552
  172.1 9.9 %collective-permute-start.23 = (bf16[576,512]{1,0:T(8,128)(2,1)S(1)}, bf16[576,512]{1,0:T(8,128)(2,1)S(1)}, u32[]{:S(2)}, u32[]{:S(2)}) collective-permute-start(bf16[576,512]{1,0:T(8,128)(2,1)S(1)} %pad_maximum_fusion.3), channel_id=1, source_target_pairs={{0,4},{1,5},{2,10},{3,11},{4,0},{5,1},{6,14},{7,15},{8,12},{9,13},... | collective-permute-start | bytes 1769480 | tf_op jit(solution)/shard_map/ppermute | solution.py:552
  173.4 8.3 %collective-permute-start.20 = (bf16[48,512]{1,0:T(8,128)(2,1)S(1)}, bf16[48,512]{1,0:T(8,128)(2,1)S(1)}, u32[]{:S(2)}, u32[]{:S(2)}) collective-permute-start(bf16[48,512]{1,0:T(8,128)(2,1)S(1)} %get-tuple-element.110), channel_id=1, source_target_pairs={{0,16},{2,18},{4,20},{6,22},{8,24},{10,26},{12,28},{14,30},{16,0},... | collective-permute-start | bytes 147464 | tf_op jit(solution)/shard_map/ppermute | solution.py:475
  173.9 7.8 %collective-permute-start.21 = (bf16[48,512]{1,0:T(8,128)(2,1)S(1)}, bf16[48,512]{1,0:T(8,128)(2,1)S(1)}, u32[]{:S(2)}, u32[]{:S(2)}) collective-permute-start(bf16[48,512]{1,0:T(8,128)(2,1)S(1)} %get-tuple-element.111), channel_id=1, source_target_pairs={{0,8},{2,10},{4,12},{6,14},{8,0},{10,2},{12,4},{14,6},{16,24},{18,... | collective-permute-start | bytes 147464 | tf_op jit(solution)/shard_map/ppermute | solution.py:475
  175.2 6.5 %collective-permute-start.22 = (bf16[48,512]{1,0:T(8,128)(2,1)S(1)}, bf16[48,512]{1,0:T(8,128)(2,1)S(1)}, u32[]{:S(2)}, u32[]{:S(2)}) collective-permute-start(bf16[48,512]{1,0:T(8,128)(2,1)S(1)} %get-tuple-element.112), channel_id=1, source_target_pairs={{0,24},{2,26},{4,28},{6,30},{8,16},{10,18},{12,20},{14,22},{16,8},... | collective-permute-start | bytes 147464 | tf_op jit(solution)/shard_map/ppermute | solution.py:475
  182.1 16.3 %collective-permute-start.25 = (bf16[1152,512]{1,0:T(8,128)(2,1)S(1)}, bf16[1152,512]{1,0:T(8,128)(2,1)S(1)}, u32[]{:S(2)}, u32[]{:S(2)}) collective-permute-start(bf16[1152,512]{1,0:T(8,128)(2,1)S(1)} %pad_maximum_fusion.1.mine), channel_id=1, source_target_pairs={{0,2},{2,0},{4,6},{6,4},{8,10},{10,8},{12,14},{14,12},{16,18},{18,... | collective-permute-start | bytes 3538952 | tf_op jit(solution)/shard_map/ppermute | solution.py:475
  182.6 9.3 %collective-permute-start.28 = (bf16[48,512]{1,0:T(8,128)(2,1)S(1)}, bf16[48,512]{1,0:T(8,128)(2,1)S(1)}, u32[]{:S(2)}, u32[]{:S(2)}) collective-permute-start(bf16[48,512]{1,0:T(8,128)(2,1)S(1)} %add_convert_fusion.7), channel_id=1, source_target_pairs={{0,24},{2,26},{4,28},{6,30},{8,16},{10,18},{12,20},{14,22},{16,8},... | collective-permute-start | bytes 147464 | tf_op jit(solution)/shard_map/ppermute | solution.py:475
  185.3 6.6 %collective-permute-start.27 = (bf16[48,512]{1,0:T(8,128)(2,1)S(1)}, bf16[48,512]{1,0:T(8,128)(2,1)S(1)}, u32[]{:S(2)}, u32[]{:S(2)}) collective-permute-start(bf16[48,512]{1,0:T(8,128)(2,1)S(1)} %add_convert_fusion.7), channel_id=1, source_target_pairs={{0,8},{2,10},{4,12},{6,14},{8,0},{10,2},{12,4},{14,6},{16,24},{18,... | collective-permute-start | bytes 147464 | tf_op jit(solution)/shard_map/ppermute | solution.py:475
  185.3 6.6 %collective-permute-start.26 = (bf16[48,512]{1,0:T(8,128)(2,1)S(1)}, bf16[48,512]{1,0:T(8,128)(2,1)S(1)}, u32[]{:S(2)}, u32[]{:S(2)}) collective-permute-start(bf16[48,512]{1,0:T(8,128)(2,1)S(1)} %add_convert_fusion.7), channel_id=1, source_target_pairs={{0,16},{2,18},{4,20},{6,22},{8,24},{10,26},{12,28},{14,30},{16,0},... | collective-permute-start | bytes 147464 | tf_op jit(solution)/shard_map/ppermute | solution.py:475
  198.4 6.6 %collective-permute-start.32 = (bf16[384,512]{1,0:T(8,128)(2,1)S(1)}, bf16[384,512]{1,0:T(8,128)(2,1)S(1)}, u32[]{:S(2)}, u32[]{:S(2)}) collective-permute-start(bf16[384,512]{1,0:T(8,128)(2,1)S(1)} %pad_maximum_fusion.4.mine), channel_id=1, source_target_pairs={{0,2},{2,0},{4,6},{6,4},{8,10},{10,8},{12,14},{14,12},{16,18},{18,... | collective-permute-start | bytes 1179656 | tf_op jit(solution)/shard_map/ppermute | solution.py:475
  (29 other events, 267.5 us)

commit v7 on v6

--- a/solution.py
+++ b/solution.py
@@ -17,7 +17,7 @@
 BF16 = jnp.bfloat16
 NEG = -1e30
 CHUNK = 256
-RHYTHM = (1, 0, 1, 1, 0)
+RHYTHM = (1, 0, 1, 1)
 
 
 def dot_nn(a, b):
@@ -884,6 +884,8 @@
             cost_estimate=cost(0, 8 << 20),
             name="ffn_out",
         )(targets, *big.result)
+    if ordered:
+        out_grad = hold(out_grad, last)
     for _ in range(8):
         lockstep(last, norms)
 

time: 209 us -> 205 us (0.981)
  waiting for transfers between devices: 42.9 us -> 38.5 us
    ppermute x10, waiting for transfers between devices: 20.5 us -> 17.8 us  [mixed(): return lax.ppermute(x, ('wide', 'narrow'), pairs)]
  transfers between devices with their start and end apart: 33 -> 33, of which waited for: 13 -> 12; matrix products, arithmetic and copies ran while one was open for 5% -> 5% of each run, Pallas kernels for 31% -> 31%
where the time goes in v7:
time: 205 us; the launch traced here: 204 us
  Pallas kernels  98.3 us (48%)
  starting transfers between devices  44.2 us (22%)
  waiting for transfers between devices  38.5 us (19%)
  other arithmetic  12.9 us (6%)
  local copies, waits for them, and re-layouts  9.15 us (4%)
    pallas_call x1, Pallas kernels, local(): pl.pallas_call(functools.partial(chain_kernel, narrow - 1, inpack, ordere...  31.2 us
    ppermute x19, waiting for transfers between devices, swap(): return lax.ppermute(x, axis, [(i, i ^ bit) for i in range(count)])  20.8 us
    ppermute x19, starting transfers between devices, swap(): return lax.ppermute(x, axis, [(i, i ^ bit) for i in range(count)])  19.4 us
    pallas_call x3, Pallas kernels, local(): pl.pallas_call(attn_bwd_near_kernel, grid=(share,), in_specs=specs, out_s...  18.8 us
    ppermute x10, waiting for transfers between devices, mixed(): return lax.ppermute(x, ('wide', 'narrow'), pairs)  17.8 us
    ppermute x10, starting transfers between devices, mixed(): return lax.ppermute(x, ('wide', 'narrow'), pairs)  14.9 us
    pallas_call x1, Pallas kernels, local(): pl.pallas_call(attn_fwd_kernel, grid=(steps,), in_specs=[whole(id_col), w...  12.1 us
    pallas_call x1, Pallas kernels, local(): pl.pallas_call(attn_bwd_own_kernel, grid=(steps,), in_specs=[whole(id_col...  10.5 us
  transfers between devices with their start and end apart: 33, of which 12 were waited for; matrix products, arithmetic and copies ran while one was open for 5% of the time, Pallas kernels for 31%

profile of v7, /device:TPU:0, one launch (start us, length us, event | category | flops | bytes accessed | tf_op | source)
XLA Modules:
  0.0 204.3 jit_solution(6433704187276131783)
XLA Ops:
  2.4 3.0 %collective-permute-start.1 = (bf16[256,768]{1,0:T(8,128)(2,1)S(1)}, bf16[256,768]{1,0:T(8,128)(2,1)S(1)}, u32[]{:S(2)}, u32[]{:S(2)}) collective-permute-start(bf16[256,768]{1,0:T(8,128)(2,1)S(1)} %constant_dynamic-slice_fusion.3), channel_id=1, source_target_pairs={{0,1},{1,0},{2,3},{3,2},{4,5},{5,4},{6,7},{7,6},{8,9},{9,8},{10,11... | collective-permute-start | bytes 1179656 | tf_op jit(solution)/shard_map/ppermute | solution.py:475
  6.7 4.0 %collective-permute-start = (bf16[16,64,512]{2,1,0:T(8,128)(2,1)}, bf16[16,64,512]{2,1,0:T(8,128)(2,1)}, u32[]{:S(2)}, u32[]{:S(2)}) collective-permute-start(bf16[16,64,512]{2,1,0:T(8,128)(2,1)} %param.35), channel_id=1, source_target_pairs={{0,2},{2,4},{4,6},{6,8},{8,10},{10,12},{12,14},{14,16},{16,18},{18... | collective-permute-start | bytes 3145736 | tf_op jit(solution)/shard_map/ppermute | solution.py:480
  12.0 2.5 %collective-permute-done.1 = bf16[256,768]{1,0:T(8,128)(2,1)S(1)} collective-permute-done((bf16[256,768]{1,0:T(8,128)(2,1)S(1)}, bf16[256,768]{1,0:T(8,128)(2,1)S(1)}, u32[]{:S(2)}, u32[]{:S(2)}) %collective-permute-start.1) | collective-permute-done | bytes 393248 | tf_op jit(solution)/shard_map/ppermute | solution.py:475
  20.2 6.1 %own_qkv.1 = (bf16[2,1024,768]{2,1,0:T(8,128)(2,1)}, bf16[1024,512]{1,0:T(8,128)(2,1)}) custom-call(bf16[1024,512]{1,0:T(8,128)(2,1)} %bitcast.1.xo.refs_1_.x, bf16[512,768]{1,0:T(8,128)(2,1)} %copy-done.2, bf16[512,768]{1,0:T(8,128)(2,1)} %pad_maximum_fusion.2.w1, f32[1,512]{1,0:T(1,128)} %bitcast.21, f32[1,512]{1,0:T(1,128)} %bitcast.33), custom_call_target="tpu_custom_call" | custom-call | flops 2000000000 | bytes 6291456 | tf_op jit(solution)/shard_map/own_qkv/pallas_call | solution.py:708
  26.3 12.1 %attn_fwd.1 = (bf16[2,3,1024,768]{3,2,1,0:T(8,128)(2,1)}, bf16[16,64,512]{2,1,0:T(8,128)(2,1)}) custom-call(s32[192,1]{1,0:T(8,128)} %copy.51.idc, s32[3,256]{1,0:T(4,128)} %tile.12.idr, bf16[16,64,512]{2,1,0:T(8,128)(2,1)} %collective-permute-done.xp, bf16[2,1024,768]{2,1,0:T(8,128)(2,1)} %get-tuple-element.74.own, ...), custom_call_target="tpu_custom_call" | custom-call | flops 6000000000 | bytes 25165824 | tf_op jit(solution)/shard_map/attn_fwd/pallas_call | solution.py:718
  38.4 4.8 %collective-permute-done.4.refs_9_ = bf16[1152,512]{1,0:T(8,128)(2,1)} collective-permute-done((bf16[1152,512]{1,0:T(8,128)(2,1)S(1)}, bf16[1152,512]{1,0:T(8,128)(2,1)}, u32[]{:S(2)}, u32[]{:S(2)}) %collective-permute-start.4) | collective-permute-done | bytes 1179680 | tf_op jit(solution)/shard_map/ppermute | solution.py:475
  48.8 31.2 %chain.1 = (bf16[1024,512]{1,0:T(8,128)(2,1)}, f32[1024,512]{1,0:T(8,128)}, bf16[1024,512]{1,0:T(8,128)(2,1)}, f32[1,512]{1,0:T(1,128)}, f32[1,512]{1,0:T(1,128)...) custom-call(s32[33]{0:T(128)} %pad_add_fusion.refs_0_, bf16[1024,512]{1,0:T(8,128)(2,1)} %bitcast.1.xo.refs_1_.x, ...), custom_call_target="tpu_custom_call" | custom-call | flops 15000000512 | bytes 20971520 | tf_op jit(solution)/shard_map/chain/pallas_call | solution.py:760
  81.9 3.1 %collective-permute-start.6 = (bf16[16,64,512]{2,1,0:T(8,128)(2,1)}, bf16[16,64,512]{2,1,0:T(8,128)(2,1)S(1)}, u32[]{:S(2)}, u32[]{:S(2)}) collective-permute-start(bf16[16,64,512]{2,1,0:T(8,128)(2,1)} %bitcast.31), channel_id=1, source_target_pairs={{0,2},{2,4},{4,6},{6,8},{8,10},{10,12},{12,14},{14,16},{16,18},{18... | collective-permute-start | bytes 3145736 | tf_op jit(solution)/shard_map/ppermute | solution.py:480
  85.0 10.5 %attn_bwd_own.1 = (bf16[2,1024,256]{2,1,0:T(8,128)(2,1)}, f32[2,1024,512]{2,1,0:T(8,128)}) custom-call(s32[192,1]{1,0:T(8,128)} %copy.51.idc, s32[3,256]{1,0:T(4,128)} %tile.12.idr, bf16[2,3,1024,768]{3,2,1,0:T(8,128)(2,1)} %get-tuple-element.80.qkv_ref, bf16[16,64,512]{2,1,0:T(8,128)(2,1)} %bitcast.32), custom_call_target="tpu_custom_call" | custom-call | flops 10000000000 | bytes 14680064 | tf_op jit(solution)/shard_map/attn_bwd_own/pallas_call | solution.py:788
  100.1 5.5 %attn_bwd_near_0.1.rest_0_ = bf16[2,1024,512]{2,1,0:T(8,128)(2,1)} custom-call(s32[192,1]{1,0:T(8,128)} %copy.51.idc, s32[3,256]{1,0:T(4,128)} %tile.12.idr, bf16[2,3,1024,768]{3,2,1,0:T(8,128)(2,1)} %get-tuple-element.80.qkv_ref, bf16[16,64,512]{2,1,0:T(8,128)(2,1)} %copy-done.1, bf16[16,64,512]{2,1,0:T(8,128)(2,1)} %copy-done, ...), custom_call_target="tpu_custom_call" | custom-call | flops 2000000000 | bytes 3145728 | tf_op jit(solution)/shard_map/attn_bwd_near_0/pallas_call | solution.py:816
  105.5 8.3 %collective-permute-done.9 = bf16[1152,512]{1,0:T(8,128)(2,1)} collective-permute-done((bf16[1152,512]{1,0:T(8,128)(2,1)S(1)}, bf16[1152,512]{1,0:T(8,128)(2,1)}, u32[]{:S(2)}, u32[]{:S(2)}) %collective-permute-start.9) | collective-permute-done | bytes 1179680 | tf_op jit(solution)/shard_map/ppermute | solution.py:552
  115.5 4.6 %collective-permute-start.10 = (bf16[576,512]{1,0:T(8,128)(2,1)S(1)}, bf16[576,512]{1,0:T(8,128)(2,1)S(1)}, u32[]{:S(2)}, u32[]{:S(2)}) collective-permute-start(bf16[576,512]{1,0:T(8,128)(2,1)S(1)} %add_convert_fusion.1), channel_id=1, source_target_pairs={{0,4},{1,5},{2,3},{3,2},{4,0},{5,1},{6,7},{7,6},{8,12},{9,13},{10,... | collective-permute-start | bytes 1769480 | tf_op jit(solution)/shard_map/ppermute | solution.py:552
  120.1 7.9 %attn_bwd_near_1.1.rest_0_ = bf16[2,1024,512]{2,1,0:T(8,128)(2,1)} custom-call(s32[192,1]{1,0:T(8,128)} %copy.51.idc, s32[3,256]{1,0:T(4,128)} %tile.12.idr, bf16[2,3,1024,768]{3,2,1,0:T(8,128)(2,1)} %get-tuple-element.80.qkv_ref, bf16[16,64,512]{2,1,0:T(8,128)(2,1)} %copy-done.1, bf16[16,64,512]{2,1,0:T(8,128)(2,1)} %copy-done, ...), custom_call_target="tpu_custom_call", output_to_operand_aliasing={{}: (6, {})} | custom-call | flops 4000000000 | bytes 6291456 | tf_op jit(solution)/shard_map/attn_bwd_near_1/pallas_call | solution.py:816
  131.6 5.4 %attn_bwd_near_2.1.dkv = bf16[2,1024,512]{2,1,0:T(8,128)(2,1)} custom-call(s32[192,1]{1,0:T(8,128)} %copy.51.idc, s32[3,256]{1,0:T(4,128)} %tile.12.idr, bf16[2,3,1024,768]{3,2,1,0:T(8,128)(2,1)} %get-tuple-element.80.qkv_ref, bf16[16,64,512]{2,1,0:T(8,128)(2,1)} %copy-done.1, bf16[16,64,512]{2,1,0:T(8,128)(2,1)} %copy-done, ...), custom_call_target="tpu_custom_call", output_to_operand_aliasing={{}: (6, {})} | custom-call | flops 2000000000 | bytes 3145728 | tf_op jit(solution)/shard_map/attn_bwd_near_2/pallas_call | solution.py:816
  140.0 5.0 %qkv_grad.1 = (bf16[768,512]{1,0:T(8,128)(2,1)}, bf16[768,512]{1,0:T(8,128)(2,1)}) custom-call(s32[33]{0:T(128)} %pad_add_fusion.1.table, bf16[1024,512]{1,0:T(8,128)(2,1)} %get-tuple-element.83.normed, bf16[2,1024,256]{2,1,0:T(8,128)(2,1)} %get-tuple-element.82.dq, bf16[2,1024,512]{2,1,0:T(8,128)(2,1)} %attn_bwd_near_2.1.dkv), custom_call_target="tpu_custom_call" | custom-call | flops 2000000000 | bytes 6291456 | tf_op jit(solution)/shard_map/qkv_grad/pallas_call | solution.py:834
  147.9 7.1 %input_grad.1 = (f32[1024,512]{1,0:T(8,128)}, f32[1,512]{1,0:T(1,128)}, f32[1,512]{1,0:T(1,128)}) custom-call(bf16[1024,512]{1,0:T(8,128)(2,1)} %bitcast.1.xo.refs_1_.x, f32[1024,512]{1,0:T(8,128)} %get-tuple-element.79.hgrad, bf16[2,1024,256]{2,1,0:T(8,128)(2,1)} %get-tuple-element.82.dq, bf16[2,1024,512]{2,1,0:T(8,128)(2,1)} %attn_bwd_near_2.1.dkv, ...), custom_call_target="tpu_custom_call" | custom-call | flops 2000000000 | bytes 8388608 | tf_op jit(solution)/shard_map/input_grad/pallas_call | solution.py:854
  160.7 5.4 %collective-permute-done.15 = bf16[384,512]{1,0:T(8,128)(2,1)S(1)} collective-permute-done((bf16[384,512]{1,0:T(8,128)(2,1)S(1)}, bf16[384,512]{1,0:T(8,128)(2,1)S(1)}, u32[]{:S(2)}, u32[]{:S(2)}) %collective-permute-start.15) | collective-permute-done | bytes 393248 | tf_op jit(solution)/shard_map/ppermute | solution.py:552
  168.3 3.7 %collective-permute-done.19 = f32[4,512]{1,0:T(4,128)S(1)} collective-permute-done((f32[4,512]{1,0:T(4,128)S(1)}, f32[4,512]{1,0:T(4,128)S(1)}, u32[]{:S(2)}, u32[]{:S(2)}) %collective-permute-start.19) | collective-permute-done | bytes 8224 | tf_op jit(solution)/shard_map/ppermute | solution.py:475
  175.2 2.6 %collective-permute-start.22 = (bf16[48,512]{1,0:T(8,128)(2,1)S(1)}, bf16[48,512]{1,0:T(8,128)(2,1)S(1)}, u32[]{:S(2)}, u32[]{:S(2)}) collective-permute-start(bf16[48,512]{1,0:T(8,128)(2,1)S(1)} %get-tuple-element.113), channel_id=1, source_target_pairs={{0,24},{2,26},{4,28},{6,30},{8,16},{10,18},{12,20},{14,22},{16,8},... | collective-permute-start | bytes 147464 | tf_op jit(solution)/shard_map/ppermute | solution.py:475
  178.1 3.6 %collective-permute-done.24 = f32[4,512]{1,0:T(4,128)S(1)} collective-permute-done((f32[4,512]{1,0:T(4,128)S(1)}, f32[4,512]{1,0:T(4,128)S(1)}, u32[]{:S(2)}, u32[]{:S(2)}) %collective-permute-start.24) | collective-permute-done | bytes 8224 | tf_op jit(solution)/shard_map/ppermute | solution.py:475
  182.6 2.7 %collective-permute-start.28 = (bf16[48,512]{1,0:T(8,128)(2,1)S(1)}, bf16[48,512]{1,0:T(8,128)(2,1)S(1)}, u32[]{:S(2)}, u32[]{:S(2)}) collective-permute-start(bf16[48,512]{1,0:T(8,128)(2,1)S(1)} %add_convert_fusion.7), channel_id=1, source_target_pairs={{0,24},{2,26},{4,28},{6,30},{8,16},{10,18},{12,20},{14,22},{16,8},... | collective-permute-start | bytes 147464 | tf_op jit(solution)/shard_map/ppermute | solution.py:475
  188.2 3.7 %collective-permute-done.29 = f32[4,512]{1,0:T(4,128)S(1)} collective-permute-done((f32[4,512]{1,0:T(4,128)S(1)}, f32[4,512]{1,0:T(4,128)S(1)}, u32[]{:S(2)}, u32[]{:S(2)}) %collective-permute-start.29) | collective-permute-done | bytes 8224 | tf_op jit(solution)/shard_map/ppermute | solution.py:475
  194.2 4.6 %ffn_out.1 = (f32[512,1024]{1,0:T(8,128)}, f32[1024,512]{1,0:T(8,128)}, f32[256,512]{1,0:T(8,128)}) custom-call(s32[16]{0:T(128)} %pad_add_fusion.2.table, bf16[1152,512]{1,0:T(8,128)(2,1)} %copy-done.3, bf16[1152,512]{1,0:T(8,128)(2,1)} %copy-done.5), custom_call_target="tpu_custom_call" | custom-call | bytes 8388608 | tf_op jit(solution)/shard_map/ffn_out/pallas_call | solution.py:877
  201.4 2.8 %qkv_out.1 = f32[3,512,256]{2,1,0:T(8,128)} custom-call(s32[16]{0:T(128)} %pad_add_fusion.3.table, bf16[384,512]{1,0:T(8,128)(2,1)} %copy-done.4, bf16[384,512]{1,0:T(8,128)(2,1)} %copy-done.7), custom_call_target="tpu_custom_call" | custom-call | bytes 3145728 | tf_op jit(solution)/shard_map/qkv_out/pallas_call | solution.py:894
  (135 shorter events, 52.9 us)
Async XLA Ops:
  2.4 12.1 %collective-permute-start.1 = (bf16[256,768]{1,0:T(8,128)(2,1)S(1)}, bf16[256,768]{1,0:T(8,128)(2,1)S(1)}, u32[]{:S(2)}, u32[]{:S(2)}) collective-permute-start(bf16[256,768]{1,0:T(8,128)(2,1)S(1)} %constant_dynamic-slice_fusion.3), channel_id=1, source_target_pairs={{0,1},{1,0},{2,3},{3,2},{4,5},{5,4},{6,7},{7,6},{8,9},{9,8},{10,11... | collective-permute-start | bytes 1179656 | tf_op jit(solution)/shard_map/ppermute | solution.py:475
  5.5 20.8 %collective-permute-start.3 = (bf16[16,64,512]{2,1,0:T(8,128)(2,1)}, bf16[16,64,512]{2,1,0:T(8,128)(2,1)}, u32[]{:S(2)}, u32[]{:S(2)}) collective-permute-start(bf16[16,64,512]{2,1,0:T(8,128)(2,1)} %param.35), channel_id=1, source_target_pairs={{2,0},{4,2},{6,4},{8,6},{10,8},{12,10},{14,12},{16,14},{18,16},{20... | collective-permute-start | bytes 3145736 | tf_op jit(solution)/shard_map/ppermute | solution.py:481
  6.7 19.5 %collective-permute-start = (bf16[16,64,512]{2,1,0:T(8,128)(2,1)}, bf16[16,64,512]{2,1,0:T(8,128)(2,1)}, u32[]{:S(2)}, u32[]{:S(2)}) collective-permute-start(bf16[16,64,512]{2,1,0:T(8,128)(2,1)} %param.35), channel_id=1, source_target_pairs={{0,2},{2,4},{4,6},{6,8},{8,10},{10,12},{12,14},{14,16},{16,18},{18... | collective-permute-start | bytes 3145736 | tf_op jit(solution)/shard_map/ppermute | solution.py:480
  14.7 28.6 %collective-permute-start.4 = (bf16[1152,512]{1,0:T(8,128)(2,1)S(1)}, bf16[1152,512]{1,0:T(8,128)(2,1)}, u32[]{:S(2)}, u32[]{:S(2)}) collective-permute-start(bf16[1152,512]{1,0:T(8,128)(2,1)S(1)} %pad_maximum_fusion), channel_id=1, source_target_pairs={{0,1},{1,0},{2,3},{3,2},{4,5},{5,4},{6,7},{7,6},{8,9},{9,8},{10,11... | collective-permute-start | bytes 3538952 | tf_op jit(solution)/shard_map/ppermute | solution.py:475
  80.0 15.5 %collective-permute-start.8 = (bf16[2304,512]{1,0:T(8,128)(2,1)}, bf16[2304,512]{1,0:T(8,128)(2,1)}, u32[]{:S(2)}, u32[]{:S(2)}) collective-permute-start(bf16[2304,512]{1,0:T(8,128)(2,1)} %get-tuple-element.86), channel_id=1, source_target_pairs={{0,2},{2,0},{4,6},{6,4},{8,10},{10,8},{12,14},{14,12},{16,18},{18,... | collective-permute-start | bytes 7077896 | tf_op jit(solution)/shard_map/ppermute | solution.py:475
  80.4 17.6 %collective-permute-start.7 = (bf16[16,64,512]{2,1,0:T(8,128)(2,1)}, bf16[16,64,512]{2,1,0:T(8,128)(2,1)S(1)}, u32[]{:S(2)}, u32[]{:S(2)}) collective-permute-start(bf16[16,64,512]{2,1,0:T(8,128)(2,1)} %bitcast.30), channel_id=1, source_target_pairs={{2,0},{4,2},{6,4},{8,6},{10,8},{12,10},{14,12},{16,14},{18,16},{20... | collective-permute-start | bytes 3145736 | tf_op jit(solution)/shard_map/ppermute | solution.py:481
  81.9 16.2 %collective-permute-start.6 = (bf16[16,64,512]{2,1,0:T(8,128)(2,1)}, bf16[16,64,512]{2,1,0:T(8,128)(2,1)S(1)}, u32[]{:S(2)}, u32[]{:S(2)}) collective-permute-start(bf16[16,64,512]{2,1,0:T(8,128)(2,1)} %bitcast.31), channel_id=1, source_target_pairs={{0,2},{2,4},{4,6},{6,8},{8,10},{10,12},{12,14},{14,16},{16,18},{18... | collective-permute-start | bytes 3145736 | tf_op jit(solution)/shard_map/ppermute | solution.py:480
  97.4 16.4 %collective-permute-start.9 = (bf16[1152,512]{1,0:T(8,128)(2,1)S(1)}, bf16[1152,512]{1,0:T(8,128)(2,1)}, u32[]{:S(2)}, u32[]{:S(2)}) collective-permute-start(bf16[1152,512]{1,0:T(8,128)(2,1)S(1)} %add_convert_fusion), channel_id=1, source_target_pairs={{0,1},{1,0},{2,10},{3,11},{4,5},{5,4},{6,14},{7,15},{8,9},{9,8},{1... | collective-permute-start | bytes 3538952 | tf_op jit(solution)/shard_map/ppermute | solution.py:552
  115.5 12.6 %collective-permute-start.10 = (bf16[576,512]{1,0:T(8,128)(2,1)S(1)}, bf16[576,512]{1,0:T(8,128)(2,1)S(1)}, u32[]{:S(2)}, u32[]{:S(2)}) collective-permute-start(bf16[576,512]{1,0:T(8,128)(2,1)S(1)} %add_convert_fusion.1), channel_id=1, source_target_pairs={{0,4},{1,5},{2,3},{3,2},{4,0},{5,1},{6,7},{7,6},{8,12},{9,13},{10,... | collective-permute-start | bytes 1769480 | tf_op jit(solution)/shard_map/ppermute | solution.py:552
  129.3 7.7 %collective-permute-start.11 = (bf16[288,512]{1,0:T(8,128)(2,1)S(1)}, bf16[288,512]{1,0:T(8,128)(2,1)S(1)}, u32[]{:S(2)}, u32[]{:S(2)}) collective-permute-start(bf16[288,512]{1,0:T(8,128)(2,1)S(1)} %add_convert_fusion.3), channel_id=1, source_target_pairs={{0,8},{1,9},{2,6},{3,7},{4,12},{5,13},{6,2},{7,3},{8,0},{9,1},{10,... | collective-permute-start | bytes 884744 | tf_op jit(solution)/shard_map/ppermute | solution.py:552
  138.2 8.3 %collective-permute-start.12 = (bf16[144,512]{1,0:T(8,128)(2,1)S(1)}, bf16[144,512]{1,0:T(8,128)(2,1)S(1)}, u32[]{:S(2)}, u32[]{:S(2)}) collective-permute-start(bf16[144,512]{1,0:T(8,128)(2,1)S(1)} %add_convert_fusion.6), channel_id=1, source_target_pairs={{0,16},{1,17},{2,18},{3,19},{4,20},{5,21},{6,22},{7,23},{8,24},{9,... | collective-permute-start | bytes 442376 | tf_op jit(solution)/shard_map/ppermute | solution.py:552
  147.7 10.4 %collective-permute-start.13 = (bf16[768,512]{1,0:T(8,128)(2,1)}, bf16[768,512]{1,0:T(8,128)(2,1)S(1)}, u32[]{:S(2)}, u32[]{:S(2)}) collective-permute-start(bf16[768,512]{1,0:T(8,128)(2,1)} %get-tuple-element.100), channel_id=1, source_target_pairs={{0,2},{2,0},{4,6},{6,4},{8,10},{10,8},{12,14},{14,12},{16,18},{18,... | collective-permute-start | bytes 2359304 | tf_op jit(solution)/shard_map/ppermute | solution.py:475
  147.8 10.3 %collective-permute-start.14 = (bf16[144,512]{1,0:T(8,128)(2,1)S(1)}, bf16[144,512]{1,0:T(8,128)(2,1)S(1)}, u32[]{:S(2)}, u32[]{:S(2)}) collective-permute-start(bf16[144,512]{1,0:T(8,128)(2,1)S(1)} %add_convert_fusion.5), channel_id=1, source_target_pairs={{0,16},{1,17},{2,18},{3,19},{4,20},{5,21},{6,22},{7,23},{8,24},{9,... | collective-permute-start | bytes 442376 | tf_op jit(solution)/shard_map/ppermute | solution.py:552
  158.2 7.8 %collective-permute-start.15 = (bf16[384,512]{1,0:T(8,128)(2,1)S(1)}, bf16[384,512]{1,0:T(8,128)(2,1)S(1)}, u32[]{:S(2)}, u32[]{:S(2)}) collective-permute-start(bf16[384,512]{1,0:T(8,128)(2,1)S(1)} %add_convert_fusion.2), channel_id=1, source_target_pairs={{0,1},{1,0},{2,6},{3,7},{4,5},{5,4},{6,2},{7,3},{8,9},{9,8},{10,14... | collective-permute-start | bytes 1179656 | tf_op jit(solution)/shard_map/ppermute | solution.py:552
  159.0 9.3 %collective-permute-start.18 = (bf16[288,512]{1,0:T(8,128)(2,1)S(1)}, bf16[288,512]{1,0:T(8,128)(2,1)S(1)}, u32[]{:S(2)}, u32[]{:S(2)}) collective-permute-start(bf16[288,512]{1,0:T(8,128)(2,1)S(1)} %pad_maximum_fusion.5), channel_id=1, source_target_pairs={{0,8},{1,9},{2,6},{3,7},{4,12},{5,13},{6,2},{7,3},{8,0},{9,1},{10,... | collective-permute-start | bytes 884744 | tf_op jit(solution)/shard_map/ppermute | solution.py:552
  172.1 9.9 %collective-permute-start.23 = (bf16[576,512]{1,0:T(8,128)(2,1)S(1)}, bf16[576,512]{1,0:T(8,128)(2,1)S(1)}, u32[]{:S(2)}, u32[]{:S(2)}) collective-permute-start(bf16[576,512]{1,0:T(8,128)(2,1)S(1)} %pad_maximum_fusion.3), channel_id=1, source_target_pairs={{0,4},{1,5},{2,10},{3,11},{4,0},{5,1},{6,14},{7,15},{8,12},{9,13},... | collective-permute-start | bytes 1769480 | tf_op jit(solution)/shard_map/ppermute | solution.py:552
  173.4 8.3 %collective-permute-start.20 = (bf16[48,512]{1,0:T(8,128)(2,1)S(1)}, bf16[48,512]{1,0:T(8,128)(2,1)S(1)}, u32[]{:S(2)}, u32[]{:S(2)}) collective-permute-start(bf16[48,512]{1,0:T(8,128)(2,1)S(1)} %get-tuple-element.111), channel_id=1, source_target_pairs={{0,16},{2,18},{4,20},{6,22},{8,24},{10,26},{12,28},{14,30},{16,0},... | collective-permute-start | bytes 147464 | tf_op jit(solution)/shard_map/ppermute | solution.py:475
  173.9 7.8 %collective-permute-start.21 = (bf16[48,512]{1,0:T(8,128)(2,1)S(1)}, bf16[48,512]{1,0:T(8,128)(2,1)S(1)}, u32[]{:S(2)}, u32[]{:S(2)}) collective-permute-start(bf16[48,512]{1,0:T(8,128)(2,1)S(1)} %get-tuple-element.112), channel_id=1, source_target_pairs={{0,8},{2,10},{4,12},{6,14},{8,0},{10,2},{12,4},{14,6},{16,24},{18,... | collective-permute-start | bytes 147464 | tf_op jit(solution)/shard_map/ppermute | solution.py:475
  175.2 6.5 %collective-permute-start.22 = (bf16[48,512]{1,0:T(8,128)(2,1)S(1)}, bf16[48,512]{1,0:T(8,128)(2,1)S(1)}, u32[]{:S(2)}, u32[]{:S(2)}) collective-permute-start(bf16[48,512]{1,0:T(8,128)(2,1)S(1)} %get-tuple-element.113), channel_id=1, source_target_pairs={{0,24},{2,26},{4,28},{6,30},{8,16},{10,18},{12,20},{14,22},{16,8},... | collective-permute-start | bytes 147464 | tf_op jit(solution)/shard_map/ppermute | solution.py:475
  182.1 9.9 %collective-permute-start.25 = (bf16[1152,512]{1,0:T(8,128)(2,1)S(1)}, bf16[1152,512]{1,0:T(8,128)(2,1)S(1)}, u32[]{:S(2)}, u32[]{:S(2)}) collective-permute-start(bf16[1152,512]{1,0:T(8,128)(2,1)S(1)} %pad_maximum_fusion.1.mine), channel_id=1, source_target_pairs={{0,2},{2,0},{4,6},{6,4},{8,10},{10,8},{12,14},{14,12},{16,18},{18,... | collective-permute-start | bytes 3538952 | tf_op jit(solution)/shard_map/ppermute | solution.py:475
  182.6 9.3 %collective-permute-start.28 = (bf16[48,512]{1,0:T(8,128)(2,1)S(1)}, bf16[48,512]{1,0:T(8,128)(2,1)S(1)}, u32[]{:S(2)}, u32[]{:S(2)}) collective-permute-start(bf16[48,512]{1,0:T(8,128)(2,1)S(1)} %add_convert_fusion.7), channel_id=1, source_target_pairs={{0,24},{2,26},{4,28},{6,30},{8,16},{10,18},{12,20},{14,22},{16,8},... | collective-permute-start | bytes 147464 | tf_op jit(solution)/shard_map/ppermute | solution.py:475
  185.3 6.6 %collective-permute-start.27 = (bf16[48,512]{1,0:T(8,128)(2,1)S(1)}, bf16[48,512]{1,0:T(8,128)(2,1)S(1)}, u32[]{:S(2)}, u32[]{:S(2)}) collective-permute-start(bf16[48,512]{1,0:T(8,128)(2,1)S(1)} %add_convert_fusion.7), channel_id=1, source_target_pairs={{0,8},{2,10},{4,12},{6,14},{8,0},{10,2},{12,4},{14,6},{16,24},{18,... | collective-permute-start | bytes 147464 | tf_op jit(solution)/shard_map/ppermute | solution.py:475
  185.3 6.6 %collective-permute-start.26 = (bf16[48,512]{1,0:T(8,128)(2,1)S(1)}, bf16[48,512]{1,0:T(8,128)(2,1)S(1)}, u32[]{:S(2)}, u32[]{:S(2)}) collective-permute-start(bf16[48,512]{1,0:T(8,128)(2,1)S(1)} %add_convert_fusion.7), channel_id=1, source_target_pairs={{0,16},{2,18},{4,20},{6,22},{8,24},{10,26},{12,28},{14,30},{16,0},... | collective-permute-start | bytes 147464 | tf_op jit(solution)/shard_map/ppermute | solution.py:475
  192.0 6.9 %collective-permute-start.30 = (bf16[192,512]{1,0:T(8,128)(2,1)S(1)}, bf16[192,512]{1,0:T(8,128)(2,1)S(1)}, u32[]{:S(2)}, u32[]{:S(2)}) collective-permute-start(bf16[192,512]{1,0:T(8,128)(2,1)S(1)} %pad_maximum_fusion.6), channel_id=1, source_target_pairs={{0,4},{1,5},{2,6},{3,7},{4,0},{5,1},{6,2},{7,3},{8,12},{9,13},{10,... | collective-permute-start | bytes 589832 | tf_op jit(solution)/shard_map/ppermute | solution.py:552
  (29 other events, 255.0 us)
